TPU v7x, 256 devices: a whole 4x4x8 slice. The times are simulated.
256 devices in a mesh: energy: 32 (over x, y, core), space: 8 (over z).
Axes of the slice: x: 4, y: 4, z: 8, core: 2. Of those that a mesh axis runs over, the one named last changes fastest.
Arguments:
- g_upper: bfloat16 [2, 128, 8, 384, 384], P(None, 'energy', 'space'), may hold values from -6 to 6
- p_diag: bfloat16 [2, 128, 8, 384, 384], P(None, 'energy', 'space'), may hold values from -0.8984375 to 0.8984375
- p_upper: bfloat16 [2, 128, 8, 384, 384], P(None, 'energy', 'space'), may hold values from -0.8984375 to 0.8984375
- v_diag: bfloat16 [8, 384, 384], P('space'), may hold values from -0.3125 to 0.3125
- v_upper: bfloat16 [8, 384, 384], P('space'), may hold values from -0.3125 to 0.3125
- v_pattern: int32 [8], P('space'), may hold values from 0 to 1, as said below
- element_present: int32 [8, 48], P('space'), may hold values from 0 to 1, as said below
Outputs:
- sigma_upper: bfloat16 [2, 128, 8, 384, 384], P(None, 'energy', 'space')
Inputs may be any that keep to these rules, and one draw needn't show every extreme that they name: `element_present`: no block row has more than 30 present groups, and some block row has exactly 30. `v_pattern`: the first and the last block row always have their upper block; the others may lack it.
All inputs are finite; a program needn't handle non-finite values.
Results may differ from a plain program's by a relative error of at most 0.013.
Values may be sent and summed in bfloat16 or wider, within the bound.
No kernel may reach another device: no remote copies, remote signals or barrier semaphores. Data moves between devices by JAX's collectives and lax.ppermute only.
A program may use at most 128 MiB of HBM per device.

v0:
```python
import functools
import math

import jax
import jax.numpy as jnp
import numpy as np
from jax import lax
from jax.experimental import pallas as pl
from jax.experimental.pallas import tpu as pltpu
from jax.sharding import PartitionSpec as P

LIVE = 30
RG = 8
LANES = 128
CHUNKS = 1

F32 = jnp.float32
BF16 = jnp.bfloat16


def smem():
    return pl.BlockSpec(memory_space=pltpu.SMEM)


def vmem():
    return pl.BlockSpec(memory_space=pltpu.VMEM)


def shifted(value, steps):
    count = lax.axis_size("space")
    pairs = [(source, (source + steps) % count) for source in range(count)]
    return lax.ppermute(value, "space", pairs)


def dot(left, right):
    return lax.dot_general(left, right, (((1,), (0,)), ((), ())), preferred_element_type=F32)


def dot_nt(left, right):
    return lax.dot_general(left, right, (((1,), (1,)), ((), ())), preferred_element_type=F32)


def tables(energies, peers):
    local = energies // peers
    src, half, step = np.meshgrid(np.arange(peers), np.arange(2), np.arange(local), indexing="ij")
    time = (src * local + step).reshape(-1)
    half = half.reshape(-1)
    freq = np.arange(energies)
    angles = 2.0 * math.pi / energies * ((freq[:, None] * time[None, :]) % energies)
    cosine, sine = np.cos(angles), np.sin(angles)
    real_part = np.where(half == 0, cosine, sine)
    imag_part = np.where(half == 0, -sine, cosine)
    forward = np.concatenate([real_part, imag_part], 0)
    real_out = np.concatenate([-sine, -cosine], 0).T
    imag_out = np.concatenate([cosine, -sine], 0).T
    inverse = np.where((half == 0)[:, None], real_out, imag_out)
    return jnp.asarray(forward, BF16), jnp.asarray(inverse, BF16)


def spread(dest_ref, plane, planes, value):
    rows = value.shape[0]
    for j in range(value.shape[1] // LANES):
        dest_ref[j, pl.ds(plane, rows, stride=planes), :] = value[:, j * LANES : (j + 1) * LANES]


def joined(source_ref):
    return jnp.concatenate([source_ref[j] for j in range(source_ref.shape[0])], axis=1)


def live_list(present_ref, idx_ref):
    groups = present_ref.shape[0]

    def clear(slot, carry):
        idx_ref[slot] = 0
        return carry

    lax.fori_loop(0, groups, clear, 0)

    def visit(group, count):
        idx_ref[count] = group
        return count + jnp.where(present_ref[group] > 0, 1, 0)

    return lax.fori_loop(0, groups, visit, 0)


def pick_rows(idx_ref, source_ref, dest_ref):
    def one(slot, carry):
        row = pl.multiple_of(idx_ref[slot] * RG, RG)
        dest_ref[pl.ds(pl.multiple_of(slot * RG, RG), RG), :] = source_ref[pl.ds(row, RG), :]
        return carry

    lax.fori_loop(0, LIVE, one, 0, unroll=5)


def pack_kernel(chunks, present_ref, g_ref, out_ref, idx_ref, turn_ref):
    planes = g_ref.shape[0]
    rows = RG // chunks
    per_chunk = LIVE // chunks
    live_list(present_ref, idx_ref)

    def one(slot, carry):
        row = pl.multiple_of(idx_ref[slot] * RG, RG)
        chunk = slot // per_chunk
        peer = (slot % per_chunk) * chunks
        for plane in range(planes):
            spread(turn_ref, plane, planes, g_ref[plane, pl.ds(row, RG), :].astype(F32))
        value = joined(turn_ref).astype(BF16)
        for part in range(chunks):
            at = part * rows * planes
            out_ref[peer + part, pl.ds(chunk * rows, rows)] = value[at : at + rows * planes].reshape(
                rows, planes, value.shape[1]
            )
        return carry

    lax.fori_loop(0, LIVE, one, 0, unroll=2)
    for peer in range(LIVE, out_ref.shape[0]):
        out_ref[peer] = jnp.zeros(out_ref.shape[1:], BF16)


def forward_kernel(present_ref, pattern_ref, vu_ref, pu_ref, out_ref, idx_ref, turned, picked, total):
    planes = pu_ref.shape[0]
    rows = LIVE * RG
    live_list(present_ref, idx_ref)
    scale = pattern_ref[0].astype(F32)
    turned[...] = vu_ref[...].astype(F32).T * scale
    pick_rows(idx_ref, turned, picked)
    left = picked[...].astype(BF16)

    def one(plane, carry):
        spread(total, plane, planes, dot(left, pu_ref[plane]))
        return carry

    lax.fori_loop(0, planes, one, 0)
    out_ref[...] = joined(total).astype(BF16)


def backward_kernel(
    present_ref, pattern_ref, vu_prev_ref, vd_ref, vu_ref, pd_ref, pu_ref, out_ref, idx_ref, wide, picked, total
):
    planes = pu_ref.shape[0]
    rows = LIVE * RG
    live_list(present_ref, idx_ref)
    wide[...] = vu_prev_ref[...].astype(F32)
    pick_rows(idx_ref, wide, picked)
    left = picked[...].astype(BF16)
    scale = pattern_ref[0].astype(F32)
    masked = (vu_ref[...].astype(F32) * scale).astype(BF16)

    def one(plane, carry):
        inner = dot(pd_ref[plane], vd_ref[...]) + dot_nt(pu_ref[plane], masked)
        spread(total, plane, planes, dot(left, inner.astype(BF16)))
        return carry

    lax.fori_loop(0, planes, one, 0)
    out_ref[...] = joined(total).astype(BF16)


def local_kernel(
    present_ref,
    pattern_ref,
    vu_ref,
    vd_ref,
    vd_next_ref,
    pd_ref,
    pu_ref,
    out_ref,
    idx_ref,
    wide,
    picked_u,
    picked_d,
    same,
    one_up,
    bare,
):
    planes = pu_ref.shape[0]
    rows = LIVE * RG
    live_list(present_ref, idx_ref)
    scale = pattern_ref[0].astype(F32)
    wide[...] = vu_ref[...].astype(F32) * scale
    masked = wide[...].astype(BF16)
    pick_rows(idx_ref, wide, picked_u)
    wide[...] = vd_ref[...].astype(F32)
    pick_rows(idx_ref, wide, picked_d)
    left_u = picked_u[...].astype(BF16)
    left_d = picked_d[...].astype(BF16)

    def one(plane, carry):
        spread(same, plane, planes, dot(left_d, pd_ref[plane]) + dot_nt(left_u, pu_ref[plane]))
        spread(one_up, plane, planes, dot(left_d, pu_ref[plane]))
        where = jnp.where(plane < planes // 2, 1.0, 0.0).astype(F32)
        spread(bare, plane, planes, picked_u[...] * where)
        return carry

    lax.fori_loop(0, planes, one, 0)
    out_ref[...] = (
        joined(bare)
        + dot(joined(same).astype(BF16), masked)
        + dot(joined(one_up).astype(BF16), vd_next_ref[...])
    )


def join_kernel(pattern_ref, local_ref, before_ref, after_ref, vu_ref, out_ref):
    scale = pattern_ref[0].astype(F32)
    masked = (vu_ref[...].astype(F32) * scale).astype(BF16)
    size = local_ref.shape[0]
    out_ref[0:size, :] = (
        local_ref[...] + dot(before_ref[...], masked) + after_ref[...].astype(F32) * scale
    ).astype(BF16)
    out_ref[size:, :] = jnp.zeros((out_ref.shape[0] - size, out_ref.shape[1]), BF16)


def spectrum_kernel(scale, forward_ref, got_ref, out_ref):
    peers, rows, planes, cols = got_ref.shape
    for r in range(rows):
        values = got_ref[:, r].reshape(peers * planes, cols)
        out_ref[r] = dot(forward_ref[...], values) * scale


def convolve_kernel(forward_ref, inverse_ref, green_ref, got_ref, out_ref):
    peers, rows, planes, cols = got_ref.shape
    half = forward_ref.shape[0] // 2
    for r in range(rows):
        values = got_ref[:, r].reshape(peers * planes, cols)
        freq = dot(forward_ref[...], values)
        green = green_ref[r]
        green_re, green_im = green[:half], green[half:]
        screen_re, screen_im = freq[:half], freq[half:]
        mixed = jnp.concatenate(
            [green_re * screen_re - green_im * screen_im, green_re * screen_im + green_im * screen_re], 0
        )
        result = dot(inverse_ref[...], mixed.astype(BF16)).astype(BF16)
        out_ref[:, r] = result.reshape(peers, planes, cols)


def unpack_kernel(chunks, present_ref, *refs):
    got_refs, (out_ref, idx_ref, turn_ref) = refs[:chunks], refs[chunks:]
    planes = out_ref.shape[0]
    per_chunk = LIVE // chunks
    count = live_list(present_ref, idx_ref)
    out_ref[...] = jnp.zeros(out_ref.shape, BF16)
    for chunk, got_ref in enumerate(got_refs):

        def one(slot, carry, got_ref=got_ref, chunk=chunk):
            at = pl.multiple_of(slot * RG * planes, RG * planes)
            row = pl.multiple_of(idx_ref[chunk * per_chunk + slot] * RG, RG)
            for j in range(turn_ref.shape[0]):
                cols = slice(j * LANES, (j + 1) * LANES)
                turn_ref[j] = got_ref[pl.ds(at, RG * planes), cols].astype(F32)
                for plane in range(planes):
                    value = turn_ref[j, pl.ds(plane, RG, stride=planes), :]
                    out_ref[plane, pl.ds(row, RG), cols] = value.astype(BF16)
            return carry

        here = jnp.clip(count - chunk * per_chunk, 0, per_chunk)
        lax.fori_loop(0, here, one, 0)


def per_device(g_upper, p_diag, p_upper, v_diag, v_upper, v_pattern, element_present):
    peers = lax.axis_size("energy")
    halves, local, _, size, _ = g_upper.shape
    planes = halves * local
    energies = local * peers
    chunks = CHUNKS
    rows = RG // chunks
    live = LIVE * RG
    flat = live * planes
    piece = flat // chunks

    green = g_upper.reshape(planes, size, size)
    p_d = p_diag.reshape(planes, size, size)
    p_u = p_upper.reshape(planes, size, size)
    v_d = v_diag.reshape(size, size)
    v_u = v_upper.reshape(size, size)
    present = element_present.reshape(-1)
    groups = present.shape[0]

    present_prev = shifted(present, 1)
    present_next = shifted(present, -1)
    v_u_prev = shifted(v_u, 1)
    v_d_next = shifted(v_d, -1)
    forward, inverse = tables(energies, peers)

    idx = pltpu.SMEM((groups,), jnp.int32)
    square = pltpu.VMEM((size, size), F32)
    strip = pltpu.VMEM((live, size), F32)
    total = pltpu.VMEM((size // LANES, flat, LANES), F32)
    turn = pltpu.VMEM((size // LANES, RG * planes, LANES), F32)

    def cost(units, data):
        return pl.CostEstimate(
            flops=int(units * 2 * planes * live * size * size), bytes_accessed=int(data), transcendentals=0
        )

    big = planes * size * size * 2

    send_green = pl.pallas_call(
        functools.partial(pack_kernel, chunks),
        out_shape=jax.ShapeDtypeStruct((peers, RG, planes, size), BF16),
        in_specs=[smem(), vmem()],
        out_specs=vmem(),
        scratch_shapes=[idx, turn],
        cost_estimate=cost(0.2, 2 * big),
        name="pack",
    )(present, green)
    got_green = lax.all_to_all(send_green, "energy", split_axis=0, concat_axis=0, tiled=True)

    to_next = pl.pallas_call(
        forward_kernel,
        out_shape=jax.ShapeDtypeStruct((flat, size), BF16),
        in_specs=[smem(), smem(), vmem(), vmem()],
        out_specs=vmem(),
        scratch_shapes=[idx, square, strip, total],
        cost_estimate=cost(1, 2 * big),
        name="to_next",
    )(present_next, v_pattern, v_u, p_u)
    to_prev = pl.pallas_call(
        backward_kernel,
        out_shape=jax.ShapeDtypeStruct((flat, size), BF16),
        in_specs=[smem(), smem()] + [vmem()] * 5,
        out_specs=vmem(),
        scratch_shapes=[idx, square, strip, total],
        cost_estimate=cost(4, 3 * big),
        name="to_prev",
    )(present_prev, v_pattern, v_u_prev, v_d, v_u, p_d, p_u)

    to_prev, v_d_next = lax.optimization_barrier((to_prev, v_d_next))
    before, after = [], []
    for chunk in range(chunks):
        part = slice(chunk * piece, (chunk + 1) * piece)
        before.append(shifted(to_next[part], 1))
        after.append(shifted(to_prev[part], -1))

    own = pl.pallas_call(
        local_kernel,
        out_shape=jax.ShapeDtypeStruct((flat, size), F32),
        in_specs=[smem(), smem()] + [vmem()] * 5,
        out_specs=vmem(),
        scratch_shapes=[idx, square, strip, strip, total, total, total],
        cost_estimate=cost(5, 4 * big),
        name="own",
    )(present, v_pattern, v_u, v_d, v_d_next, p_d, p_u)

    green_freq = pl.pallas_call(
        functools.partial(spectrum_kernel, 1.0 / (energies * math.sqrt(energies))),
        out_shape=jax.ShapeDtypeStruct((RG, 2 * energies, size), F32),
        in_specs=[vmem(), vmem()],
        out_specs=vmem(),
        cost_estimate=cost(0.5, 3 * big),
        name="green_freq",
    )(forward, got_green)

    returned = []
    for chunk in range(chunks):
        part = slice(chunk * piece, (chunk + 1) * piece)
        send = pl.pallas_call(
            join_kernel,
            out_shape=jax.ShapeDtypeStruct((peers * rows * planes, size), BF16),
            grid=(1,),
            in_specs=[
                smem(),
                pl.BlockSpec((piece, size), lambda i, c=chunk: (c, 0)),
                vmem(),
                vmem(),
                vmem(),
            ],
            out_specs=vmem(),
            cost_estimate=cost(1 / chunks, 3 * big / chunks),
            name="join",
        )(v_pattern, own, before[chunk], after[chunk], v_u)
        got = lax.all_to_all(
            send.reshape(peers, rows, planes, size), "energy", split_axis=0, concat_axis=0, tiled=True
        )
        result = pl.pallas_call(
            convolve_kernel,
            out_shape=jax.ShapeDtypeStruct((peers, rows, planes, size), BF16),
            grid=(1,),
            in_specs=[
                vmem(),
                vmem(),
                pl.BlockSpec((rows, 2 * energies, size), lambda i, c=chunk: (c, 0, 0)),
                vmem(),
            ],
            out_specs=vmem(),
            cost_estimate=cost(1 / chunks, 3 * big / chunks),
            name="convolve",
        )(forward, inverse, green_freq, got)
        back = lax.all_to_all(result, "energy", split_axis=0, concat_axis=0, tiled=True)
        returned.append(back.reshape(peers * rows * planes, size))

    sigma = pl.pallas_call(
        functools.partial(unpack_kernel, chunks),
        out_shape=jax.ShapeDtypeStruct((planes, size, size), BF16),
        in_specs=[smem()] + [vmem()] * chunks,
        out_specs=vmem(),
        scratch_shapes=[idx, turn],
        cost_estimate=cost(0.2, 2 * big),
        name="unpack",
    )(present, *returned)
    return sigma.reshape(halves, local, 1, size, size)


def solution(mesh):
    in_specs = (
        P(None, "energy", "space", None, None),
        P(None, "energy", "space", None, None),
        P(None, "energy", "space", None, None),
        P("space", None, None),
        P("space", None, None),
        P("space"),
        P("space", None),
    )
    out_specs = P(None, "energy", "space", None, None)
    return jax.shard_map(
        per_device, mesh=mesh, in_specs=in_specs, out_specs=out_specs, check_vma=False
    )
```

profile of v0, /device:TPU:33, one launch (start us, length us, event | category | flops | bytes accessed | tf_op | source)
XLA Modules:
  0.0 143.4 jit_solution(13672766894132280927)
XLA Ops:
  0.0 1.6 %collective-permute-start.1 = (bf16[384,384]{1,0:T(8,128)(2,1)}, bf16[384,384]{1,0:T(8,128)(2,1)S(1)}, u32[]{:S(2)}, u32[]{:S(2)}) collective-permute-start(bf16[384,384]{1,0:T(8,128)(2,1)} %bitcast.17), channel_id=1, source_target_pairs={{0,1},{1,2},{2,3},{3,4},{4,5},{5,6},{6,7},{7,0},{8,9},{9,10},{10,1... | collective-permute-start | bytes 884744 | tf_op jit(solution)/shard_map/ppermute | solution.py:32
  1.6 0.0 collective-permute-start.2
  1.6 3.8 %collective-permute-start.3 = (s32[48]{0:T(128)}, s32[48]{0:T(128)S(1)}, u32[]{:S(2)}, u32[]{:S(2)}) collective-permute-start(s32[48]{0:T(128)} %bitcast.22), channel_id=1, source_target_pairs={{0,7},{1,0},{2,1},{3,2},{4,3},{5,4},{6,5},{7,6},{8,15},{9,8},{10,9... | collective-permute-start | bytes 584 | tf_op jit(solution)/shard_map/ppermute | solution.py:32
  5.4 0.0 collective-permute-start
  6.1 3.8 %collective-permute-done.3.present_ref = s32[48]{0:T(128)S(1)} collective-permute-done((s32[48]{0:T(128)}, s32[48]{0:T(128)S(1)}, u32[]{:S(2)}, u32[]{:S(2)}) %collective-permute-start.3) | collective-permute-done | bytes 224 | tf_op jit(solution)/shard_map/ppermute | solution.py:32
  9.8 0.0 copy-start.3
  9.8 0.5 copy-done.3
  10.3 6.5 %to_next.1 = bf16[1920,384]{1,0:T(8,128)(2,1)} custom-call(s32[48]{0:T(128)} %copy-done.3, s32[1]{0:T(128)S(6)} %copy.11.pattern_ref, bf16[384,384]{1,0:T(8,128)(2,1)} %bitcast.18, bf16[8,384,384]{2,1,0:T(8,128)(2,1)} %bitcast.14), custom_call_target="tpu_custom_call" | custom-call | flops 566231040 | bytes 4718592 | tf_op jit(solution)/shard_map/to_next/pallas_call | solution.py:307
  16.8 3.0 %collective-permute-start.4 = (bf16[1920,384]{1,0:T(8,128)(2,1)}, bf16[1920,384]{1,0:T(8,128)(2,1)S(1)}, u32[]{:S(2)}, u32[]{:S(2)}) collective-permute-start(bf16[1920,384]{1,0:T(8,128)(2,1)} %to_next.1), channel_id=1, source_target_pairs={{0,1},{1,2},{2,3},{3,4},{4,5},{5,6},{6,7},{7,0},{8,9},{9,10},{10,1... | collective-permute-start | bytes 4423688 | tf_op jit(solution)/shard_map/ppermute | solution.py:32
  19.7 0.0 collective-permute-done.present_ref
  19.8 0.0 copy-start.6
  19.8 0.0 collective-permute-done.1.vu_prev_ref
  19.8 0.0 copy-start.5
  19.8 0.5 copy-done.6
  20.3 0.2 copy-done.5
  20.5 11.9 %to_prev.1 = bf16[1920,384]{1,0:T(8,128)(2,1)} custom-call(s32[48]{0:T(128)} %copy-done.6, s32[1]{0:T(128)S(6)} %copy.11.pattern_ref, bf16[384,384]{1,0:T(8,128)(2,1)} %copy-done.5, bf16[384,384]{1,0:T(8,128)(2,1)} %bitcast.30, bf16[384,384]{1,0:T(8,128)(2,1)} %bitcast.19, bf16[8,384,384]{2,1,0:T(8,128)(2,1)} %bitcast.27, bf16[8,384,384]{2,1,0:T(8,128)(2,1)} %bitcast.15), custom_call_target="tpu_custom_call" | custom-call | flops 2264924160 | bytes 7077888 | tf_op jit(solution)/shard_map/to_prev/pallas_call | solution.py:316
  32.4 0.0 collective-permute-done.2.vd_next_ref
  32.4 0.0 copy-start.4
  32.4 0.0 collective-permute-start.5
  32.4 4.3 %pack.1 = bf16[32,8,8,384]{3,2,1,0:T(8,128)(2,1)} custom-call(s32[48]{0:T(128)} %bitcast.24, bf16[8,384,384]{2,1,0:T(8,128)(2,1)} %bitcast.13), custom_call_target="tpu_custom_call" | custom-call | flops 113246208 | bytes 4718592 | tf_op jit(solution)/shard_map/pack/pallas_call | solution.py:296
  36.7 0.0 copy-done.4
  36.7 9.0 %all-to-all-start = ((bf16[32,8,8,384]{3,2,1,0:T(8,128)(2,1)}), bf16[32,8,8,384]{3,2,1,0:T(8,128)(2,1)S(1)}, u32[]{:S(2)}, u32[]{:S(2)}) async-start(bf16[32,8,8,384]{3,2,1,0:T(8,128)(2,1)} %pack.1), calls=%async_computation | async-start | bytes 3145728 | tf_op jit(solution)/shard_map/all_to_all | solution.py:305
  45.7 12.9 %own.1.local_ref = f32[1920,384]{1,0:T(8,128)} custom-call(s32[48]{0:T(128)} %bitcast.25, s32[1]{0:T(128)S(6)} %copy.11.pattern_ref, bf16[384,384]{1,0:T(8,128)(2,1)} %bitcast.20, bf16[384,384]{1,0:T(8,128)(2,1)} %bitcast.31, bf16[384,384]{1,0:T(8,128)(2,1)} %copy-done.4, bf16[8,384,384]{2,1,0:T(8,128)(2,1)} %bitcast.28, bf16[8,384,384]{2,1,0:T(8,128)(2,1)} %bitcast.16), custom_call_target="tpu_custom_call" | custom-call | flops 2831155200 | bytes 9437184 | tf_op jit(solution)/shard_map/own/pallas_call | solution.py:333
  58.6 0.0 collective-permute-done.4.before_ref
  58.6 0.0 copy-start.2
  58.6 6.9 %collective-permute-done.5.after_ref = bf16[1920,384]{1,0:T(8,128)(2,1)} collective-permute-done((bf16[1920,384]{1,0:T(8,128)(2,1)}, bf16[1920,384]{1,0:T(8,128)(2,1)}, u32[]{:S(2)}, u32[]{:S(2)}) %collective-permute-start.5) | collective-permute-done | bytes 1474592 | tf_op jit(solution)/shard_map/ppermute | solution.py:32
  65.6 0.0 copy-done.2
  65.6 5.0 %join.1 = bf16[2048,384]{1,0:T(8,128)(2,1)} custom-call(s32[1]{0:T(128)S(6)} %copy.11.pattern_ref, f32[1920,384]{1,0:T(8,128)} %own.1.local_ref, bf16[1920,384]{1,0:T(8,128)(2,1)} %copy-done.2, bf16[1920,384]{1,0:T(8,128)(2,1)} %collective-permute-done.5.after_ref, bf16[384,384]{1,0:T(8,128)(2,1)} %bitcast.21), custom_call_target="tpu_custom_call" | custom-call | flops 566231040 | bytes 7077888 | tf_op jit(solution)/shard_map/join/pallas_call | solution.py:355
  70.6 0.0 all-to-all-done.got_ref
  70.6 0.0 copy-start
  70.6 1.1 copy-done
  71.8 9.8 %all-to-all-start.1 = ((bf16[32,8,8,384]{3,2,1,0:T(8,128)(2,1)}), bf16[32,8,8,384]{3,2,1,0:T(8,128)(2,1)S(1)}, u32[]{:S(2)}, u32[]{:S(2)}) async-start(bf16[32,8,8,384]{3,2,1,0:T(8,128)(2,1)} %bitcast.12), calls=%async_computation.1 | async-start | bytes 3145728 | tf_op jit(solution)/shard_map/all_to_all | solution.py:370
  81.6 3.8 %green_freq.1.green_ref = f32[8,256,384]{2,1,0:T(8,128)} custom-call(bf16[256,256]{1,0:T(8,128)(2,1)} %constant.4.clone.forward_ref, bf16[32,8,8,384]{3,2,1,0:T(8,128)(2,1)} %copy-done), custom_call_target="tpu_custom_call" | custom-call | flops 283115520 | bytes 7077888 | tf_op jit(solution)/shard_map/green_freq/pallas_call | solution.py:343
  85.4 18.8 %all-to-all-done.1.got_ref = bf16[32,8,8,384]{3,2,1,0:T(8,128)(2,1)S(1)} async-done(((bf16[32,8,8,384]{3,2,1,0:T(8,128)(2,1)}), bf16[32,8,8,384]{3,2,1,0:T(8,128)(2,1)S(1)}, u32[]{:S(2)}, u32[]{:S(2)}) %all-to-all-start.1) | async-done | bytes 1572896 | tf_op jit(solution)/shard_map/all_to_all | solution.py:370
  104.3 0.0 copy-start.1
  104.3 1.1 copy-done.1
  105.4 6.1 %convolve.1 = bf16[32,8,8,384]{3,2,1,0:T(8,128)(2,1)} custom-call(bf16[256,256]{1,0:T(8,128)(2,1)} %constant.4.clone.forward_ref, bf16[256,256]{1,0:T(8,128)(2,1)} %constant.5.clone.inverse_ref, f32[8,256,384]{2,1,0:T(8,128)} %green_freq.1.green_ref, bf16[32,8,8,384]{3,2,1,0:T(8,128)(2,1)} %copy-done.1), custom_call_target="tpu_custom_call" | custom-call | flops 566231040 | bytes 7077888 | tf_op jit(solution)/shard_map/convolve/pallas_call | solution.py:373
  111.5 27.8 %all_to_all.15 = bf16[32,8,8,384]{3,2,1,0:T(8,128)(2,1)} all-to-all(bf16[32,8,8,384]{3,2,1,0:T(8,128)(2,1)} %convolve.1), channel_id=1, replica_groups=mesh['energy'=32,'space'=8] {'energy'}, dimensions={0} | all-to-all | bytes 3145728 | tf_op jit(solution)/shard_map/all_to_all | solution.py:387
  139.3 4.1 %unpack.1 = bf16[8,384,384]{2,1,0:T(8,128)(2,1)} custom-call(s32[48]{0:T(128)} %bitcast.26, bf16[2048,384]{1,0:T(8,128)(2,1)} %bitcast.11), custom_call_target="tpu_custom_call" | custom-call | flops 113246208 | bytes 4718592 | tf_op jit(solution)/shard_map/unpack/pallas_call | solution.py:390
Async XLA Ops:
  0.0 19.8 %collective-permute-start.1 = (bf16[384,384]{1,0:T(8,128)(2,1)}, bf16[384,384]{1,0:T(8,128)(2,1)S(1)}, u32[]{:S(2)}, u32[]{:S(2)}) collective-permute-start(bf16[384,384]{1,0:T(8,128)(2,1)} %bitcast.17), channel_id=1, source_target_pairs={{0,1},{1,2},{2,3},{3,4},{4,5},{5,6},{6,7},{7,0},{8,9},{9,10},{10,1... | collective-permute-start | bytes 884744 | tf_op jit(solution)/shard_map/ppermute | solution.py:32
  1.6 30.7 %collective-permute-start.2 = (bf16[384,384]{1,0:T(8,128)(2,1)}, bf16[384,384]{1,0:T(8,128)(2,1)S(1)}, u32[]{:S(2)}, u32[]{:S(2)}) collective-permute-start(bf16[384,384]{1,0:T(8,128)(2,1)} %bitcast.29), channel_id=1, source_target_pairs={{0,7},{1,0},{2,1},{3,2},{4,3},{5,4},{6,5},{7,6},{8,15},{9,8},{10,9... | collective-permute-start | bytes 884744 | tf_op jit(solution)/shard_map/ppermute | solution.py:32
  1.6 8.2 %collective-permute-start.3 = (s32[48]{0:T(128)}, s32[48]{0:T(128)S(1)}, u32[]{:S(2)}, u32[]{:S(2)}) collective-permute-start(s32[48]{0:T(128)} %bitcast.22), channel_id=1, source_target_pairs={{0,7},{1,0},{2,1},{3,2},{4,3},{5,4},{6,5},{7,6},{8,15},{9,8},{10,9... | collective-permute-start | bytes 584 | tf_op jit(solution)/shard_map/ppermute | solution.py:32
  5.4 14.3 %collective-permute-start = (s32[48]{0:T(128)}, s32[48]{0:T(128)S(1)}, u32[]{:S(2)}, u32[]{:S(2)}) collective-permute-start(s32[48]{0:T(128)} %bitcast.23), channel_id=1, source_target_pairs={{0,1},{1,2},{2,3},{3,4},{4,5},{5,6},{6,7},{7,0},{8,9},{9,10},{10,1... | collective-permute-start | bytes 584 | tf_op jit(solution)/shard_map/ppermute | solution.py:32
  9.8 0.5 copy-start.3
  16.8 41.9 %collective-permute-start.4 = (bf16[1920,384]{1,0:T(8,128)(2,1)}, bf16[1920,384]{1,0:T(8,128)(2,1)S(1)}, u32[]{:S(2)}, u32[]{:S(2)}) collective-permute-start(bf16[1920,384]{1,0:T(8,128)(2,1)} %to_next.1), channel_id=1, source_target_pairs={{0,1},{1,2},{2,3},{3,4},{4,5},{5,6},{6,7},{7,0},{8,9},{9,10},{10,1... | collective-permute-start | bytes 4423688 | tf_op jit(solution)/shard_map/ppermute | solution.py:32
  19.8 0.5 copy-start.6
  19.8 0.7 copy-start.5
  32.4 4.4 %copy-start.4 = (bf16[384,384]{1,0:T(8,128)(2,1)}, bf16[384,384]{1,0:T(8,128)(2,1)S(1)}, u32[]{:S(2)}) copy-start(bf16[384,384]{1,0:T(8,128)(2,1)S(1)} %collective-permute-done.2.vd_next_ref) | copy-start | bytes 884740
  32.4 33.2 %collective-permute-start.5 = (bf16[1920,384]{1,0:T(8,128)(2,1)}, bf16[1920,384]{1,0:T(8,128)(2,1)}, u32[]{:S(2)}, u32[]{:S(2)}) collective-permute-start(bf16[1920,384]{1,0:T(8,128)(2,1)} %to_prev.1), channel_id=1, source_target_pairs={{0,7},{1,0},{2,1},{3,2},{4,3},{5,4},{6,5},{7,6},{8,15},{9,8},{10,9... | collective-permute-start | bytes 4423688 | tf_op jit(solution)/shard_map/ppermute | solution.py:32
  36.7 33.9 %all-to-all-start = ((bf16[32,8,8,384]{3,2,1,0:T(8,128)(2,1)}), bf16[32,8,8,384]{3,2,1,0:T(8,128)(2,1)S(1)}, u32[]{:S(2)}, u32[]{:S(2)}) async-start(bf16[32,8,8,384]{3,2,1,0:T(8,128)(2,1)} %pack.1), calls=%async_computation | async-start | bytes 3145728 | tf_op jit(solution)/shard_map/all_to_all | solution.py:305
  58.6 6.9 %copy-start.2 = (bf16[1920,384]{1,0:T(8,128)(2,1)}, bf16[1920,384]{1,0:T(8,128)(2,1)S(1)}, u32[]{:S(2)}) copy-start(bf16[1920,384]{1,0:T(8,128)(2,1)S(1)} %collective-permute-done.4.before_ref) | copy-start | bytes 4423684
  70.6 1.1 copy-start
  71.8 32.5 %all-to-all-start.1 = ((bf16[32,8,8,384]{3,2,1,0:T(8,128)(2,1)}), bf16[32,8,8,384]{3,2,1,0:T(8,128)(2,1)S(1)}, u32[]{:S(2)}, u32[]{:S(2)}) async-start(bf16[32,8,8,384]{3,2,1,0:T(8,128)(2,1)} %bitcast.12), calls=%async_computation.1 | async-start | bytes 3145728 | tf_op jit(solution)/shard_map/all_to_all | solution.py:370
  104.3 1.1 copy-start.1
where the time goes:
time: 144 us; the launch traced here: 143 us
  Pallas kernels  54.6 us (38%)
  waiting for transfers between devices  29.5 us (20%)
  blocking collectives  27.8 us (19%)
  starting transfers between devices  27.2 us (19%)
  local copies, waits for them, and re-layouts  3.51 us (2%)
    all_to_all x1, blocking collectives, per_device(): lax.all_to_all(result, 'energy', split_axis=0, concat_axis=0, tiled=True)  27.8 us
    all_to_all x1, waiting for transfers between devices, per_device(): lax.all_to_all(send.reshape(peers, rows, planes, size), 'energy', split_a...  18.8 us
    pallas_call x1, Pallas kernels, per_device(): pl.pallas_call(local_kernel, out_shape=jax.ShapeDtypeStruct((flat, size),...  12.9 us
    pallas_call x1, Pallas kernels, per_device(): pl.pallas_call(backward_kernel, out_shape=jax.ShapeDtypeStruct((flat, siz...  11.9 us
    ppermute x6, waiting for transfers between devices, shifted(): return lax.ppermute(value, 'space', pairs)  10.7 us
    all_to_all x1, starting transfers between devices, per_device(): lax.all_to_all(send.reshape(peers, rows, planes, size), 'energy', split_a...  9.83 us
    all_to_all x1, starting transfers between devices, per_device(): lax.all_to_all(send_green, 'energy', split_axis=0, concat_axis=0, tiled=T...  8.98 us
    ppermute x6, starting transfers between devices, shifted(): return lax.ppermute(value, 'space', pairs)  8.37 us
  transfers between devices with their start and end apart: 8, of which 3 were waited for; matrix products, arithmetic and copies ran while one was open for 0% of the time, Pallas kernels for 31%

commit v1 on v0

v1 whole, which is shorter than its diff:
```python
import functools
import math

import jax
import jax.numpy as jnp
import numpy as np
from jax import lax
from jax.experimental import pallas as pl
from jax.experimental.pallas import tpu as pltpu
from jax.sharding import PartitionSpec as P


LIVE = 30
RG = 8
LANES = 128
ROWS = (8,)

F32 = jnp.float32
BF16 = jnp.bfloat16


def smem():
    return pl.BlockSpec(memory_space=pltpu.SMEM)


def vmem():
    return pl.BlockSpec(memory_space=pltpu.VMEM)


def hbm():
    return pl.BlockSpec(memory_space=pltpu.HBM)


def shifted(value, steps):
    count = lax.axis_size("space")
    pairs = [(source, (source + steps) % count) for source in range(count)]
    return lax.ppermute(value, "space", pairs)


def routed(value):
    return lax.all_to_all(value, "energy", split_axis=0, concat_axis=0, tiled=True)


def dot(left, right):
    return lax.dot_general(left, right, (((1,), (0,)), ((), ())), preferred_element_type=F32)


def dot_nt(left, right):
    return lax.dot_general(left, right, (((1,), (1,)), ((), ())), preferred_element_type=F32)


def tables(energies, peers):
    local = energies // peers
    src, half, step = np.meshgrid(np.arange(peers), np.arange(2), np.arange(local), indexing="ij")
    time = (src * local + step).reshape(-1)
    half = half.reshape(-1)
    freq = np.arange(energies)
    angles = 2.0 * math.pi / energies * ((freq[:, None] * time[None, :]) % energies)
    cosine, sine = np.cos(angles), np.sin(angles)
    real_part = np.where(half == 0, cosine, sine)
    imag_part = np.where(half == 0, -sine, cosine)
    forward = np.concatenate([real_part, imag_part], 0)
    real_out = np.concatenate([-sine, -cosine], 0).T
    imag_out = np.concatenate([cosine, -sine], 0).T
    inverse = np.where((half == 0)[:, None], real_out, imag_out)
    return jnp.asarray(forward, BF16), jnp.asarray(inverse, BF16)


def spread(dest_ref, plane, planes, value):
    rows = value.shape[0]
    for j in range(value.shape[1] // LANES):
        dest_ref[j, pl.ds(plane, rows, stride=planes), :] = value[:, j * LANES : (j + 1) * LANES]


def joined(source_ref):
    return jnp.concatenate([source_ref[j] for j in range(source_ref.shape[0])], axis=1)


def live_list(present_ref, idx_ref):
    for slot in range(LIVE):
        idx_ref[slot] = 0
    count = jnp.int32(0)
    for group in range(present_ref.shape[0]):
        idx_ref[count] = group
        count = count + jnp.where(present_ref[group] > 0, 1, 0)
    return count


def pick_rows(idx_ref, source_ref, dest_ref):
    for slot in range(LIVE):
        row = pl.multiple_of(idx_ref[slot] * RG, RG)
        dest_ref[slot * RG : (slot + 1) * RG, :] = source_ref[pl.ds(row, RG), :]


def place(row):
    start = 0
    for chunk, rows in enumerate(ROWS):
        if row < start + LIVE * rows:
            peer, inner = divmod(row - start, rows)
            return chunk, peer, inner
        start += LIVE * rows


def pieces(planes):
    starts = np.concatenate([[0], np.cumsum(ROWS)]) * LIVE * planes
    return [(int(x), int(y)) for x, y in zip(starts[:-1], starts[1:])]


def pack_kernel(present_ref, g_ref, out_ref, idx_ref, turn_ref, held_ref, sem):
    planes = g_ref.shape[0]
    live_list(present_ref, idx_ref)
    firsts = np.concatenate([[0], np.cumsum(ROWS)])
    copies = []
    for slot in range(LIVE):
        row = pl.multiple_of(idx_ref[slot] * RG, RG)
        copies.append(
            pltpu.make_async_copy(g_ref.at[:, pl.ds(row, RG), :], held_ref.at[slot], sem.at[slot])
        )
        copies[-1].start()
    for slot in range(LIVE):
        turn = turn_ref.at[slot % turn_ref.shape[0]]
        copies[slot].wait()
        for plane in range(planes):
            spread(turn, plane, planes, held_ref[slot, plane].astype(F32))
        value = joined(turn).astype(BF16)
        for r in range(RG):
            chunk, peer, inner = place(slot * RG + r)
            out_ref[peer, int(firsts[chunk]) + inner] = value[r * planes : (r + 1) * planes]
    for peer in range(LIVE, out_ref.shape[0]):
        out_ref[peer] = jnp.zeros(out_ref.shape[1:], BF16)


def inner_kernel(pattern_ref, vd_ref, vu_ref, pd_hbm, pu_hbm, out_ref, pu_ref, pd_ref, sem):
    planes = pu_ref.shape[0]
    copies = []
    for plane in range(planes):
        copies.append(
            (
                pltpu.make_async_copy(pd_hbm.at[plane], pd_ref.at[plane], sem.at[0, plane]),
                pltpu.make_async_copy(pu_hbm.at[plane], pu_ref.at[plane], sem.at[1, plane]),
            )
        )
        for copy in copies[-1]:
            copy.start()
    scale = pattern_ref[0].astype(F32)
    turned = ((vu_ref[...].astype(F32) * scale).T).astype(BF16)
    right = jnp.concatenate([vd_ref[...], turned], axis=0)
    for plane in range(planes):
        for copy in copies[plane]:
            copy.wait()
        left = jnp.concatenate([pd_ref[plane], pu_ref[plane]], axis=1)
        out_ref[plane] = dot(left, right).astype(BF16)


def outward_kernel(next_ref, prev_ref, pattern_ref, vu_ref, vu_prev_ref, pu_ref, inner_ref, *refs):
    chunks = len(ROWS)
    to_next, to_prev = refs[:chunks], refs[chunks : 2 * chunks]
    idx_next, idx_prev, wide, picked, total_next, total_prev = refs[2 * chunks :]
    planes = pu_ref.shape[0]
    live_list(prev_ref, idx_prev)
    live_list(next_ref, idx_next)
    wide[...] = vu_prev_ref[...].astype(F32)
    pick_rows(idx_prev, wide, picked)
    left_prev = picked[...].astype(BF16)
    scale = pattern_ref[0].astype(F32)
    wide[...] = (vu_ref[...].astype(F32) * scale).T
    pick_rows(idx_next, wide, picked)
    left_next = picked[...].astype(BF16)
    for plane in range(planes):
        spread(total_prev, plane, planes, dot(left_prev, inner_ref[plane]))
        spread(total_next, plane, planes, dot(left_next, pu_ref[plane]))
    for chunk, (start, end) in enumerate(pieces(planes)):
        to_next[chunk][...] = joined(total_next.at[:, start:end]).astype(BF16)
        to_prev[chunk][...] = joined(total_prev.at[:, start:end]).astype(BF16)


def local_kernel(present_ref, pattern_ref, vu_ref, vd_ref, vd_next_ref, pd_hbm, pu_hbm, *refs):
    chunks = len(ROWS)
    outs = refs[:chunks]
    idx_ref, wide, picked_u, picked_d, same, one_up, bare, pd_ref, pu_ref, sem = refs[chunks:]
    planes = pu_ref.shape[0]
    copies = []
    for plane in range(planes):
        copies.append(
            (
                pltpu.make_async_copy(pd_hbm.at[plane], pd_ref.at[plane], sem.at[0, plane]),
                pltpu.make_async_copy(pu_hbm.at[plane], pu_ref.at[plane], sem.at[1, plane]),
            )
        )
        for copy in copies[-1]:
            copy.start()
    live_list(present_ref, idx_ref)
    scale = pattern_ref[0].astype(F32)
    wide[...] = vu_ref[...].astype(F32) * scale
    masked = wide[...].astype(BF16)
    pick_rows(idx_ref, wide, picked_u)
    wide[...] = vd_ref[...].astype(F32)
    pick_rows(idx_ref, wide, picked_d)
    left_u = picked_u[...].astype(BF16)
    left_d = picked_d[...].astype(BF16)
    nothing = jnp.zeros(picked_u.shape, F32)
    for plane in range(planes):
        for copy in copies[plane]:
            copy.wait()
        spread(same, plane, planes, dot(left_d, pd_ref[plane]) + dot_nt(left_u, pu_ref[plane]))
        spread(one_up, plane, planes, dot(left_d, pu_ref[plane]))
        spread(bare, plane, planes, picked_u[...] if plane < planes // 2 else nothing)
    for out_ref, (start, end) in zip(outs, pieces(planes)):
        out_ref[...] = (
            joined(bare.at[:, start:end])
            + dot(joined(same.at[:, start:end]).astype(BF16), masked)
            + dot(joined(one_up.at[:, start:end]).astype(BF16), vd_next_ref[...])
        )


def join_kernel(pattern_ref, local_ref, before_ref, after_ref, vu_ref, out_ref):
    scale = pattern_ref[0].astype(F32)
    masked = (vu_ref[...].astype(F32) * scale).astype(BF16)
    size = local_ref.shape[0]
    out_ref[0:size, :] = (
        local_ref[...] + dot(before_ref[...], masked) + after_ref[...].astype(F32) * scale
    ).astype(BF16)
    out_ref[size:, :] = jnp.zeros((out_ref.shape[0] - size, out_ref.shape[1]), BF16)


def spectrum_kernel(scale, forward_ref, got_ref, *outs):
    peers, _, planes, cols = got_ref.shape
    at = 0
    for out_ref in outs:
        for r in range(out_ref.shape[0]):
            values = got_ref[:, at].reshape(peers * planes, cols)
            out_ref[r] = dot(forward_ref[...], values) * scale
            at += 1


def convolve_kernel(forward_ref, inverse_ref, green_ref, got_ref, out_ref):
    peers, rows, planes, cols = got_ref.shape
    half = forward_ref.shape[0] // 2
    for r in range(rows):
        values = got_ref[:, r].reshape(peers * planes, cols)
        freq = dot(forward_ref[...], values)
        green_re, green_im = green_ref[r, :half], green_ref[r, half:]
        screen_re, screen_im = freq[:half], freq[half:]
        mixed = jnp.concatenate(
            [green_re * screen_re - green_im * screen_im, green_re * screen_im + green_im * screen_re], 0
        )
        result = dot(inverse_ref[...], mixed.astype(BF16)).astype(BF16)
        out_ref[:, r] = result.reshape(peers, planes, cols)


def unpack_kernel(present_ref, *refs):
    chunks = len(ROWS)
    got_refs, (out_ref, idx_ref, turn_ref) = refs[:chunks], refs[chunks:]
    planes = out_ref.shape[0]
    count = live_list(present_ref, idx_ref)
    out_ref[...] = jnp.zeros(out_ref.shape, BF16)
    for slot in range(LIVE):

        @pl.when(slot < count)
        def _(slot=slot):
            turn = turn_ref.at[slot % turn_ref.shape[0]]
            row = pl.multiple_of(idx_ref[slot] * RG, RG)
            for r in range(RG):
                chunk, peer, inner = place(slot * RG + r)
                at = (peer * ROWS[chunk] + inner) * planes
                value = got_refs[chunk][at : at + planes, :].astype(F32)
                for j in range(turn.shape[0]):
                    turn[j, r * planes : (r + 1) * planes] = value[:, j * LANES : (j + 1) * LANES]
            for plane in range(planes):
                value = [turn[j, pl.ds(plane, RG, stride=planes), :] for j in range(turn.shape[0])]
                out_ref[plane, pl.ds(row, RG), :] = jnp.concatenate(value, 1).astype(BF16)


def per_device(g_upper, p_diag, p_upper, v_diag, v_upper, v_pattern, element_present):
    peers = lax.axis_size("energy")
    halves, local, _, size, _ = g_upper.shape
    planes = halves * local
    energies = local * peers
    live = LIVE * RG
    flat = live * planes
    sizes = [end - start for start, end in pieces(planes)]

    green = g_upper.reshape(planes, size, size)
    p_d = p_diag.reshape(planes, size, size)
    p_u = p_upper.reshape(planes, size, size)
    v_d = v_diag.reshape(size, size)
    v_u = v_upper.reshape(size, size)
    present = element_present.reshape(-1)
    groups = present.shape[0]

    present_prev = shifted(present, 1)
    present_next = shifted(present, -1)
    v_u_prev = shifted(v_u, 1)
    v_d_next = shifted(v_d, -1)
    forward, inverse = tables(energies, peers)

    idx = pltpu.SMEM((groups,), jnp.int32)
    square = pltpu.VMEM((size, size), F32)
    strip = pltpu.VMEM((live, size), F32)
    total = pltpu.VMEM((size // LANES, flat, LANES), F32)
    turn = pltpu.VMEM((4, size // LANES, RG * planes, LANES), F32)
    big = planes * size * size * 2

    def call(kernel, outs, ins, scratch, units, mib):
        many = isinstance(outs, list)
        return pl.pallas_call(
            kernel,
            out_shape=outs,
            in_specs=ins,
            out_specs=[vmem() for _ in outs] if many else vmem(),
            scratch_shapes=scratch,
            compiler_params=pltpu.CompilerParams(vmem_limit_bytes=mib * 2**20),
            cost_estimate=pl.CostEstimate(
                flops=int(units * 2 * planes * live * size * size), bytes_accessed=int(big), transcendentals=0
            ),
        )

    def array(*shape, dtype=BF16):
        return jax.ShapeDtypeStruct(shape, dtype)

    whole = pltpu.VMEM((planes, size, size), BF16)
    sems = pltpu.SemaphoreType.DMA((2, planes))
    inner, p_u_here = call(
        inner_kernel,
        [array(planes, size, size)] * 2,
        [smem()] + [vmem()] * 2 + [hbm()] * 2,
        [whole, sems],
        3.2,
        12,
    )(v_pattern, v_d, v_u, p_d, p_u)
    outward = call(
        outward_kernel,
        [array(n, size) for n in sizes] * 2,
        [smem()] * 3 + [vmem()] * 4,
        [idx, idx, square, strip, total, total],
        2,
        18,
    )(present_next, present_prev, v_pattern, v_u, v_u_prev, p_u_here, inner)
    chunks = len(ROWS)
    before = [shifted(piece, 1) for piece in outward[:chunks]]
    after = [shifted(piece, -1) for piece in outward[chunks:]]

    held = pltpu.VMEM((LIVE, planes, RG, size), BF16)
    held_sem = pltpu.SemaphoreType.DMA((LIVE,))
    send_green = call(
        pack_kernel, array(peers, RG, planes, size), [smem(), hbm()], [idx, turn, held, held_sem], 0.3, 8
    )(present, green)
    got_green = routed(send_green)

    own = call(
        local_kernel,
        [array(n, size, dtype=F32) for n in sizes],
        [smem()] * 2 + [vmem()] * 3 + [hbm()] * 2,
        [idx, square, strip, strip, total, total, total, whole, whole, sems],
        5,
        22,
    )(present, v_pattern, v_u, v_d, v_d_next, p_d, p_u)

    green_freq = call(
        functools.partial(spectrum_kernel, 1.0 / (energies * math.sqrt(energies))),
        [array(rows, 2 * energies, size, dtype=F32) for rows in ROWS],
        [vmem(), vmem()],
        [],
        0.5,
        8,
    )(forward, got_green)

    returned = []
    for chunk, rows in enumerate(ROWS):
        send = call(
            join_kernel,
            array(peers * rows * planes, size),
            [smem()] + [vmem()] * 4,
            [],
            rows / RG,
            8,
        )(v_pattern, own[chunk], before[chunk], after[chunk], v_u)
        got = routed(send.reshape(peers, rows, planes, size))
        result = call(
            convolve_kernel, array(peers, rows, planes, size), [vmem()] * 4, [], rows / RG, 10
        )(forward, inverse, green_freq[chunk], got)
        back = routed(result)
        returned.append(back.reshape(peers * rows * planes, size))

    sigma = call(
        unpack_kernel, array(planes, size, size), [smem()] + [vmem()] * chunks, [idx, turn], 0.3, 8
    )(present, *returned)
    return sigma.reshape(halves, local, 1, size, size)


def solution(mesh):
    in_specs = (
        P(None, "energy", "space", None, None),
        P(None, "energy", "space", None, None),
        P(None, "energy", "space", None, None),
        P("space", None, None),
        P("space", None, None),
        P("space"),
        P("space", None),
    )
    out_specs = P(None, "energy", "space", None, None)

    return jax.shard_map(per_device, mesh=mesh, in_specs=in_specs, out_specs=out_specs, check_vma=False)
```

time: 144 us -> 147 us (1.021)
  Pallas kernels: 54.6 us -> 34.5 us
  waiting for transfers between devices: 29.5 us -> 46.5 us
  local copies, waits for them, and re-layouts: 3.51 us -> 12.1 us
    pallas_call x8, Pallas kernels: 54.6 us -> 34.5 us  [the longest x1 9.35 us: per_device(): call(local_kernel, [array(n, size, dtype=F32) for n in sizes], [smem()] *...]
    ppermute x6, waiting for transfers between devices: 10.7 us -> 25.9 us  [shifted(): return lax.ppermute(value, 'space', pairs)]
    unnamed x14 -> x28, local copies, waits for them, and re-layouts: 3.51 us -> 12.1 us
    all_to_all x2, waiting for transfers between devices: 18.8 us -> 20.6 us  [routed(): lax.all_to_all(value, 'energy', split_axis=0, concat_axis=0, tiled=True)]
  transfers between devices with their start and end apart: 8 -> 8, of which waited for: 3 -> 2; matrix products, arithmetic and copies ran while one was open for 0% -> 0% of each run, Pallas kernels for 31% -> 15%
where the time goes in v1:
time: 147 us
  waiting for transfers between devices  46.5 us (32%)
  Pallas kernels  34.5 us (23%)
  starting transfers between devices  26.5 us (18%)
  blocking collectives  26.4 us (18%)
  local copies, waits for them, and re-layouts  12.1 us (8%)
    all_to_all x1, blocking collectives, routed(): lax.all_to_all(value, 'energy', split_axis=0, concat_axis=0, tiled=True)  26.4 us
    ppermute x6, waiting for transfers between devices, shifted(): return lax.ppermute(value, 'space', pairs)  25.9 us
    all_to_all x2, waiting for transfers between devices, routed(): lax.all_to_all(value, 'energy', split_axis=0, concat_axis=0, tiled=True)  20.6 us
    all_to_all x2, starting transfers between devices, routed(): lax.all_to_all(value, 'energy', split_axis=0, concat_axis=0, tiled=True)  18.1 us
    unnamed x28, local copies, waits for them, and re-layouts  12.1 us
    pallas_call x1, Pallas kernels, per_device(): call(local_kernel, [array(n, size, dtype=F32) for n in sizes], [smem()] *...  9.35 us
    ppermute x6, starting transfers between devices, shifted(): return lax.ppermute(value, 'space', pairs)  8.35 us
    pallas_call x1, Pallas kernels, per_device(): call(outward_kernel, [array(n, size) for n in sizes] * 2, [smem()] * 3 +...  5.4 us
  transfers between devices with their start and end apart: 8, of which 2 were waited for; matrix products, arithmetic and copies ran while one was open for 0% of the time, Pallas kernels for 15%

profile of v1, /device:TPU:33, one launch (start us, length us, event | category | flops | bytes accessed | tf_op | source)
XLA Modules:
  0.0 146.9 jit_solution(630281752952972116)
XLA Ops:
  0.0 1.6 %collective-permute-start.3 = (bf16[384,384]{1,0:T(8,128)(2,1)}, bf16[384,384]{1,0:T(8,128)(2,1)S(1)}, u32[]{:S(2)}, u32[]{:S(2)}) collective-permute-start(bf16[384,384]{1,0:T(8,128)(2,1)} %bitcast.13), channel_id=1, source_target_pairs={{0,1},{1,2},{2,3},{3,4},{4,5},{5,6},{6,7},{7,0},{8,9},{9,10},{10,1... | collective-permute-start | bytes 884744 | tf_op jit(solution)/shard_map/ppermute | solution.py:37
  1.6 0.0 collective-permute-start.1
  1.6 1.6 %collective-permute-start.2 = (s32[48]{0:T(128)}, s32[48]{0:T(128)S(1)}, u32[]{:S(2)}, u32[]{:S(2)}) collective-permute-start(s32[48]{0:T(128)} %bitcast.19), channel_id=1, source_target_pairs={{0,1},{1,2},{2,3},{3,4},{4,5},{5,6},{6,7},{7,0},{8,9},{9,10},{10,1... | collective-permute-start | bytes 584 | tf_op jit(solution)/shard_map/ppermute | solution.py:37
  3.9 0.0 copy-start.3
  3.9 1.0 copy-done.3
  4.9 0.0 copy-start.8
  4.9 1.7 %copy-done.8 = bf16[2,4,1,384,384]{4,3,2,1,0:T(8,128)(2,1)S(1)} copy-done((bf16[2,4,1,384,384]{4,3,2,1,0:T(8,128)(2,1)S(1)}, bf16[2,4,1,384,384]{4,3,2,1,0:T(8,128)(2,1)}, u32[]{:S(2)}) %copy-start.8) | copy-done | bytes 2359320
  6.6 0.0 copy-start.10
  6.6 1.7 %copy-done.10 = bf16[2,4,1,384,384]{4,3,2,1,0:T(8,128)(2,1)S(1)} copy-done((bf16[2,4,1,384,384]{4,3,2,1,0:T(8,128)(2,1)S(1)}, bf16[2,4,1,384,384]{4,3,2,1,0:T(8,128)(2,1)}, u32[]{:S(2)}) %copy-start.10) | copy-done | bytes 2359320
  8.2 0.0 copy-start.12
  8.2 1.0 copy-done.12
  9.2 0.0 copy-start.4
  9.2 5.1 %shard_map.94 = (bf16[8,384,384]{2,1,0:T(8,128)(2,1)S(1)}, bf16[8,384,384]{2,1,0:T(8,128)(2,1)S(1)}) custom-call(s32[1]{0:T(128)S(6)} %copy.11.pattern_ref, bf16[384,384]{1,0:T(8,128)(2,1)S(1)} %bitcast.28, bf16[384,384]{1,0:T(8,128)(2,1)S(1)} %bitcast.14, bf16[8,384,384]{2,1,0:T(8,128)(2,1)S(1)} %bitcast.23, bf16[8,384,384]{2,1,0:T(8,128)(2,1)S(1)} %bitcast.25), custom_call_target="tpu_custom_call" | custom-call | flops 1811939328 | bytes 2359296 | tf_op jit(solution)/shard_map/pallas_call | solution.py:323
  14.3 0.0 collective-permute-done.1.next_ref
  14.3 0.0 collective-permute-done.2.prev_ref
  14.3 0.0 collective-permute-done.3.vu_prev_ref
  14.3 0.0 copy-done.4
  14.3 0.0 copy-start.2
  14.3 0.0 copy-start.7
  14.3 5.4 %shard_map.95 = (bf16[1920,384]{1,0:T(8,128)(2,1)}, bf16[1920,384]{1,0:T(8,128)(2,1)}) custom-call(s32[48]{0:T(128)S(1)} %collective-permute-done.1.next_ref, s32[48]{0:T(128)S(1)} %collective-permute-done.2.prev_ref, s32[1]{0:T(128)S(6)} %copy.11.pattern_ref, bf16[384,384]{1,0:T(8,128)(2,1)S(1)} %bitcast.15, ...), custom_call_target="tpu_custom_call" | custom-call | flops 1132462080 | bytes 2359296 | tf_op jit(solution)/shard_map/pallas_call | solution.py:331
  19.7 2.9 %collective-permute-start.4 = (bf16[1920,384]{1,0:T(8,128)(2,1)}, bf16[1920,384]{1,0:T(8,128)(2,1)S(1)}, u32[]{:S(2)}, u32[]{:S(2)}) collective-permute-start(bf16[1920,384]{1,0:T(8,128)(2,1)} %get-tuple-element.11), channel_id=1, source_target_pairs={{0,1},{1,2},{2,3},{3,4},{4,5},{5,6},{6,7},{7,0},{8,9},{9,10},{10,1... | collective-permute-start | bytes 4423688 | tf_op jit(solution)/shard_map/ppermute | solution.py:37
  22.6 0.0 collective-permute-start.5
  22.6 0.0 copy-done.2
  22.6 0.0 copy-done.7
  22.6 3.3 %shard_map.91 = bf16[32,8,8,384]{3,2,1,0:T(8,128)(2,1)} custom-call(s32[48]{0:T(128)S(1)} %bitcast.20, bf16[8,384,384]{2,1,0:T(8,128)(2,1)S(1)} %bitcast.12), custom_call_target="tpu_custom_call" | custom-call | flops 169869312 | bytes 2359296 | tf_op jit(solution)/shard_map/pallas_call | solution.py:345
  25.9 8.6 %all-to-all-start = ((bf16[32,8,8,384]{3,2,1,0:T(8,128)(2,1)}), bf16[32,8,8,384]{3,2,1,0:T(8,128)(2,1)S(1)}, u32[]{:S(2)}, u32[]{:S(2)}) async-start(bf16[32,8,8,384]{3,2,1,0:T(8,128)(2,1)} %shard_map.91), calls=%async_computation | async-start | bytes 3145728 | tf_op jit(solution)/shard_map/all_to_all | solution.py:41
  34.5 2.2 %collective-permute-start = (bf16[384,384]{1,0:T(8,128)(2,1)}, bf16[384,384]{1,0:T(8,128)(2,1)S(1)}, u32[]{:S(2)}, u32[]{:S(2)}) collective-permute-start(bf16[384,384]{1,0:T(8,128)(2,1)} %bitcast.27), channel_id=1, source_target_pairs={{0,7},{1,0},{2,1},{3,2},{4,3},{5,4},{6,5},{7,6},{8,15},{9,8},{10,9... | collective-permute-start | bytes 884744 | tf_op jit(solution)/shard_map/ppermute | solution.py:37
  36.7 25.9 %collective-permute-done.vd_next_ref = bf16[384,384]{1,0:T(8,128)(2,1)S(1)} collective-permute-done((bf16[384,384]{1,0:T(8,128)(2,1)}, bf16[384,384]{1,0:T(8,128)(2,1)S(1)}, u32[]{:S(2)}, u32[]{:S(2)}) %collective-permute-start) | collective-permute-done | bytes 294944 | tf_op jit(solution)/shard_map/ppermute | solution.py:37
  62.6 0.0 copy-start.9
  62.6 1.7 %copy-done.9 = bf16[2,4,1,384,384]{4,3,2,1,0:T(8,128)(2,1)S(1)} copy-done((bf16[2,4,1,384,384]{4,3,2,1,0:T(8,128)(2,1)S(1)}, bf16[2,4,1,384,384]{4,3,2,1,0:T(8,128)(2,1)}, u32[]{:S(2)}) %copy-start.9) | copy-done | bytes 2359320
  64.3 0.0 copy-start.11
  64.3 1.7 %copy-done.11 = bf16[2,4,1,384,384]{4,3,2,1,0:T(8,128)(2,1)S(1)} copy-done((bf16[2,4,1,384,384]{4,3,2,1,0:T(8,128)(2,1)S(1)}, bf16[2,4,1,384,384]{4,3,2,1,0:T(8,128)(2,1)}, u32[]{:S(2)}) %copy-start.11) | copy-done | bytes 2359320
  66.0 0.0 copy-start.13
  66.0 1.0 copy-done.13
  66.9 9.3 %shard_map.93.local_ref = f32[1920,384]{1,0:T(8,128)S(1)} custom-call(s32[48]{0:T(128)S(1)} %bitcast.21, s32[1]{0:T(128)S(6)} %copy.11.pattern_ref, bf16[384,384]{1,0:T(8,128)(2,1)S(1)} %bitcast.16, bf16[384,384]{1,0:T(8,128)(2,1)S(1)} %bitcast.29, bf16[384,384]{1,0:T(8,128)(2,1)S(1)} %collective-permute-done.vd_next_ref, bf16[8,384,384]{2,1,0:T(8,128)(2,1)S(1)} %bitcast.24, ...), custom_call_target="tpu_custom_call" | custom-call | flops 2831155200 | bytes 2359296 | tf_op jit(solution)/shard_map/pallas_call | solution.py:350
  76.3 0.0 collective-permute-done.4.before_ref
  76.3 0.0 collective-permute-done.5.after_ref
  76.3 3.8 %shard_map.96 = bf16[2048,384]{1,0:T(8,128)(2,1)} custom-call(s32[1]{0:T(128)S(6)} %copy.11.pattern_ref, f32[1920,384]{1,0:T(8,128)S(1)} %shard_map.93.local_ref, bf16[1920,384]{1,0:T(8,128)(2,1)S(1)} %collective-permute-done.4.before_ref, bf16[1920,384]{1,0:T(8,128)(2,1)} %collective-permute-done.5.after_ref, bf16[384,384]{1,0:T(8,128)(2,1)S(1)} %bitcast.17), custom_call_target="tpu_custom_call" | custom-call | flops 566231040 | bytes 2359296 | tf_op jit(solution)/shard_map/pallas_call | solution.py:370
  80.1 0.0 all-to-all-done.got_ref
  80.2 0.0 copy-start
  80.2 0.0 copy-start.5
  80.2 1.1 copy-done
  81.3 9.5 %all-to-all-start.1 = ((bf16[32,8,8,384]{3,2,1,0:T(8,128)(2,1)}), bf16[32,8,8,384]{3,2,1,0:T(8,128)(2,1)}, u32[]{:S(2)}, u32[]{:S(2)}) async-start(bf16[32,8,8,384]{3,2,1,0:T(8,128)(2,1)} %bitcast.6), calls=%async_computation.1 | async-start | bytes 3145728 | tf_op jit(solution)/shard_map/all_to_all | solution.py:41
  90.8 0.0 copy-done.5
  90.8 0.0 copy-start.1
  90.8 1.4 copy-done.1
  92.2 0.0 copy-start.6
  92.2 0.7 shard_map.92.green_ref
  92.9 20.6 %all-to-all-done.1.got_ref = bf16[32,8,8,384]{3,2,1,0:T(8,128)(2,1)} async-done(((bf16[32,8,8,384]{3,2,1,0:T(8,128)(2,1)}), bf16[32,8,8,384]{3,2,1,0:T(8,128)(2,1)}, u32[]{:S(2)}, u32[]{:S(2)}) %all-to-all-start.1) | async-done | bytes 1572896 | tf_op jit(solution)/shard_map/all_to_all | solution.py:41
  113.5 0.0 copy-done.6
  113.5 3.9 %shard_map.97 = bf16[32,8,8,384]{3,2,1,0:T(8,128)(2,1)S(1)} custom-call(bf16[256,256]{1,0:T(8,128)(2,1)S(1)} %copy-done.5, bf16[256,256]{1,0:T(8,128)(2,1)S(1)} %copy-done.6, f32[8,256,384]{2,1,0:T(8,128)S(1)} %shard_map.92.green_ref, bf16[32,8,8,384]{3,2,1,0:T(8,128)(2,1)} %all-to-all-done.1.got_ref), custom_call_target="tpu_custom_call" | custom-call | flops 566231040 | bytes 2359296 | tf_op jit(solution)/shard_map/pallas_call | solution.py:379
  117.4 26.4 %all_to_all.15 = bf16[32,8,8,384]{3,2,1,0:T(8,128)(2,1)S(1)} all-to-all(bf16[32,8,8,384]{3,2,1,0:T(8,128)(2,1)S(1)} %shard_map.97), channel_id=1, replica_groups=mesh['energy'=32,'space'=8] {'energy'}, dimensions={0} | all-to-all | bytes 3145728 | tf_op jit(solution)/shard_map/all_to_all | solution.py:41
  143.8 3.0 %shard_map.98 = bf16[8,384,384]{2,1,0:T(8,128)(2,1)} custom-call(s32[48]{0:T(128)S(1)} %bitcast.22, bf16[2048,384]{1,0:T(8,128)(2,1)S(1)} %bitcast.11), custom_call_target="tpu_custom_call" | custom-call | flops 169869312 | bytes 2359296 | tf_op jit(solution)/shard_map/pallas_call | solution.py:385
Async XLA Ops:
  0.0 14.3 %collective-permute-start.3 = (bf16[384,384]{1,0:T(8,128)(2,1)}, bf16[384,384]{1,0:T(8,128)(2,1)S(1)}, u32[]{:S(2)}, u32[]{:S(2)}) collective-permute-start(bf16[384,384]{1,0:T(8,128)(2,1)} %bitcast.13), channel_id=1, source_target_pairs={{0,1},{1,2},{2,3},{3,4},{4,5},{5,6},{6,7},{7,0},{8,9},{9,10},{10,1... | collective-permute-start | bytes 884744 | tf_op jit(solution)/shard_map/ppermute | solution.py:37
  1.6 12.6 %collective-permute-start.1 = (s32[48]{0:T(128)}, s32[48]{0:T(128)S(1)}, u32[]{:S(2)}, u32[]{:S(2)}) collective-permute-start(s32[48]{0:T(128)} %bitcast.18), channel_id=1, source_target_pairs={{0,7},{1,0},{2,1},{3,2},{4,3},{5,4},{6,5},{7,6},{8,15},{9,8},{10,9... | collective-permute-start | bytes 584 | tf_op jit(solution)/shard_map/ppermute | solution.py:37
  1.6 12.6 %collective-permute-start.2 = (s32[48]{0:T(128)}, s32[48]{0:T(128)S(1)}, u32[]{:S(2)}, u32[]{:S(2)}) collective-permute-start(s32[48]{0:T(128)} %bitcast.19), channel_id=1, source_target_pairs={{0,1},{1,2},{2,3},{3,4},{4,5},{5,6},{6,7},{7,0},{8,9},{9,10},{10,1... | collective-permute-start | bytes 584 | tf_op jit(solution)/shard_map/ppermute | solution.py:37
  3.9 1.0 copy-start.3
  4.9 1.7 %copy-start.8 = (bf16[2,4,1,384,384]{4,3,2,1,0:T(8,128)(2,1)S(1)}, bf16[2,4,1,384,384]{4,3,2,1,0:T(8,128)(2,1)}, u32[]{:S(2)}) copy-start(bf16[2,4,1,384,384]{4,3,2,1,0:T(8,128)(2,1)} %param.10) | copy-start | bytes 7077892
  6.6 1.7 %copy-start.10 = (bf16[2,4,1,384,384]{4,3,2,1,0:T(8,128)(2,1)S(1)}, bf16[2,4,1,384,384]{4,3,2,1,0:T(8,128)(2,1)}, u32[]{:S(2)}) copy-start(bf16[2,4,1,384,384]{4,3,2,1,0:T(8,128)(2,1)} %param.11) | copy-start | bytes 7077892
  8.2 1.0 copy-start.12
  9.2 5.1 %copy-start.4 = (bf16[1,384,384]{2,1,0:T(8,128)(2,1)S(1)}, bf16[1,384,384]{2,1,0:T(8,128)(2,1)}, u32[]{:S(2)}) copy-start(bf16[1,384,384]{2,1,0:T(8,128)(2,1)} %param.13) | copy-start | bytes 884740
  14.3 8.3 %copy-start.2 = (bf16[2,4,1,384,384]{4,3,2,1,0:T(8,128)(2,1)S(1)}, bf16[2,4,1,384,384]{4,3,2,1,0:T(8,128)(2,1)}, u32[]{:S(2)}) copy-start(bf16[2,4,1,384,384]{4,3,2,1,0:T(8,128)(2,1)} %param.9) | copy-start | bytes 7077892
  14.3 8.3 %copy-start.7 = (s32[1,48]{1,0:T(1,128)S(1)}, s32[1,48]{1,0:T(1,128)}, u32[]{:S(2)}) copy-start(s32[1,48]{1,0:T(1,128)} %param.15) | copy-start | bytes 580
  19.7 56.6 %collective-permute-start.4 = (bf16[1920,384]{1,0:T(8,128)(2,1)}, bf16[1920,384]{1,0:T(8,128)(2,1)S(1)}, u32[]{:S(2)}, u32[]{:S(2)}) collective-permute-start(bf16[1920,384]{1,0:T(8,128)(2,1)} %get-tuple-element.11), channel_id=1, source_target_pairs={{0,1},{1,2},{2,3},{3,4},{4,5},{5,6},{6,7},{7,0},{8,9},{9,10},{10,1... | collective-permute-start | bytes 4423688 | tf_op jit(solution)/shard_map/ppermute | solution.py:37
  22.6 53.7 %collective-permute-start.5 = (bf16[1920,384]{1,0:T(8,128)(2,1)}, bf16[1920,384]{1,0:T(8,128)(2,1)}, u32[]{:S(2)}, u32[]{:S(2)}) collective-permute-start(bf16[1920,384]{1,0:T(8,128)(2,1)} %get-tuple-element.12), channel_id=1, source_target_pairs={{0,7},{1,0},{2,1},{3,2},{4,3},{5,4},{6,5},{7,6},{8,15},{9,8},{10,9... | collective-permute-start | bytes 4423688 | tf_op jit(solution)/shard_map/ppermute | solution.py:37
  25.9 54.3 %all-to-all-start = ((bf16[32,8,8,384]{3,2,1,0:T(8,128)(2,1)}), bf16[32,8,8,384]{3,2,1,0:T(8,128)(2,1)S(1)}, u32[]{:S(2)}, u32[]{:S(2)}) async-start(bf16[32,8,8,384]{3,2,1,0:T(8,128)(2,1)} %shard_map.91), calls=%async_computation | async-start | bytes 3145728 | tf_op jit(solution)/shard_map/all_to_all | solution.py:41
  34.5 28.1 %collective-permute-start = (bf16[384,384]{1,0:T(8,128)(2,1)}, bf16[384,384]{1,0:T(8,128)(2,1)S(1)}, u32[]{:S(2)}, u32[]{:S(2)}) collective-permute-start(bf16[384,384]{1,0:T(8,128)(2,1)} %bitcast.27), channel_id=1, source_target_pairs={{0,7},{1,0},{2,1},{3,2},{4,3},{5,4},{6,5},{7,6},{8,15},{9,8},{10,9... | collective-permute-start | bytes 884744 | tf_op jit(solution)/shard_map/ppermute | solution.py:37
  62.6 1.7 %copy-start.9 = (bf16[2,4,1,384,384]{4,3,2,1,0:T(8,128)(2,1)S(1)}, bf16[2,4,1,384,384]{4,3,2,1,0:T(8,128)(2,1)}, u32[]{:S(2)}) copy-start(bf16[2,4,1,384,384]{4,3,2,1,0:T(8,128)(2,1)} %param.10) | copy-start | bytes 7077892
  64.3 1.7 %copy-start.11 = (bf16[2,4,1,384,384]{4,3,2,1,0:T(8,128)(2,1)S(1)}, bf16[2,4,1,384,384]{4,3,2,1,0:T(8,128)(2,1)}, u32[]{:S(2)}) copy-start(bf16[2,4,1,384,384]{4,3,2,1,0:T(8,128)(2,1)} %param.11) | copy-start | bytes 7077892
  66.0 1.0 copy-start.13
  80.2 1.1 copy-start
  80.2 10.7 %copy-start.5 = (bf16[256,256]{1,0:T(8,128)(2,1)S(1)}, bf16[256,256]{1,0:T(8,128)(2,1)}, u32[]{:S(2)}) copy-start(bf16[256,256]{1,0:T(8,128)(2,1)} %constant.4.clone.forward_ref) | copy-start | bytes 393220
  81.3 32.2 %all-to-all-start.1 = ((bf16[32,8,8,384]{3,2,1,0:T(8,128)(2,1)}), bf16[32,8,8,384]{3,2,1,0:T(8,128)(2,1)}, u32[]{:S(2)}, u32[]{:S(2)}) async-start(bf16[32,8,8,384]{3,2,1,0:T(8,128)(2,1)} %bitcast.6), calls=%async_computation.1 | async-start | bytes 3145728 | tf_op jit(solution)/shard_map/all_to_all | solution.py:41
  90.8 1.4 copy-start.1
  92.2 21.3 %copy-start.6 = (bf16[256,256]{1,0:T(8,128)(2,1)S(1)}, bf16[256,256]{1,0:T(8,128)(2,1)}, u32[]{:S(2)}) copy-start(bf16[256,256]{1,0:T(8,128)(2,1)} %constant.5.clone.inverse_ref) | copy-start | bytes 393220

commit v2 on v1

--- a/solution.py
+++ b/solution.py
@@ -66,6 +66,18 @@
     return jnp.asarray(forward, BF16), jnp.asarray(inverse, BF16)
 
 
+def fetch(sources, targets, sems):
+    copies = [pltpu.make_async_copy(a, b, sem) for a, b, sem in zip(sources, targets, sems)]
+    for copy in copies:
+        copy.start()
+    return copies
+
+
+def arrive(copies):
+    for copy in copies:
+        copy.wait()
+
+
 def spread(dest_ref, plane, planes, value):
     rows = value.shape[0]
     for j in range(value.shape[1] // LANES):
@@ -130,66 +142,72 @@
         out_ref[peer] = jnp.zeros(out_ref.shape[1:], BF16)
 
 
-def inner_kernel(pattern_ref, vd_ref, vu_ref, pd_hbm, pu_hbm, out_ref, pu_ref, pd_ref, sem):
+def inner_kernel(
+    pattern_ref, vd_hbm, vu_hbm, pd_hbm, pu_hbm, out_ref, pu_ref, pd_ref, vd_ref, vu_ref, sem, v_sem
+):
     planes = pu_ref.shape[0]
-    copies = []
-    for plane in range(planes):
-        copies.append(
-            (
-                pltpu.make_async_copy(pd_hbm.at[plane], pd_ref.at[plane], sem.at[0, plane]),
-                pltpu.make_async_copy(pu_hbm.at[plane], pu_ref.at[plane], sem.at[1, plane]),
-            )
-        )
-        for copy in copies[-1]:
-            copy.start()
+    small = fetch([vd_hbm, vu_hbm], [vd_ref, vu_ref], [v_sem.at[0], v_sem.at[1]])
+    copies = [
+        fetch(
+            [pd_hbm.at[plane], pu_hbm.at[plane]],
+            [pd_ref.at[plane], pu_ref.at[plane]],
+            [sem.at[0, plane], sem.at[1, plane]],
+        )
+        for plane in range(planes)
+    ]
+    arrive(small)
     scale = pattern_ref[0].astype(F32)
     turned = ((vu_ref[...].astype(F32) * scale).T).astype(BF16)
     right = jnp.concatenate([vd_ref[...], turned], axis=0)
     for plane in range(planes):
-        for copy in copies[plane]:
-            copy.wait()
+        arrive(copies[plane])
         left = jnp.concatenate([pd_ref[plane], pu_ref[plane]], axis=1)
         out_ref[plane] = dot(left, right).astype(BF16)
 
 
-def outward_kernel(next_ref, prev_ref, pattern_ref, vu_ref, vu_prev_ref, pu_ref, inner_ref, *refs):
+def outward_kernel(next_ref, prev_ref, pattern_ref, vu_hbm, vu_prev_ref, pu_ref, inner_ref, *refs):
     chunks = len(ROWS)
     to_next, to_prev = refs[:chunks], refs[chunks : 2 * chunks]
-    idx_next, idx_prev, wide, picked, total_next, total_prev = refs[2 * chunks :]
+    idx_next, idx_prev, vu_ref, wide, picked, total, ready, v_sem, sem = refs[2 * chunks :]
     planes = pu_ref.shape[0]
+    small = fetch([vu_hbm], [vu_ref], [v_sem.at[0]])
+    scale = pattern_ref[0].astype(F32)
     live_list(prev_ref, idx_prev)
+    wide[0] = vu_prev_ref[...].astype(F32)
+    pick_rows(idx_prev, wide.at[0], picked.at[0])
     live_list(next_ref, idx_next)
-    wide[...] = vu_prev_ref[...].astype(F32)
-    pick_rows(idx_prev, wide, picked)
-    left_prev = picked[...].astype(BF16)
-    scale = pattern_ref[0].astype(F32)
-    wide[...] = (vu_ref[...].astype(F32) * scale).T
-    pick_rows(idx_next, wide, picked)
-    left_next = picked[...].astype(BF16)
-    for plane in range(planes):
-        spread(total_prev, plane, planes, dot(left_prev, inner_ref[plane]))
-        spread(total_next, plane, planes, dot(left_next, pu_ref[plane]))
-    for chunk, (start, end) in enumerate(pieces(planes)):
-        to_next[chunk][...] = joined(total_next.at[:, start:end]).astype(BF16)
-        to_prev[chunk][...] = joined(total_prev.at[:, start:end]).astype(BF16)
-
-
-def local_kernel(present_ref, pattern_ref, vu_ref, vd_ref, vd_next_ref, pd_hbm, pu_hbm, *refs):
+    arrive(small)
+    wide[1] = (vu_ref[...].astype(F32) * scale).T
+    pick_rows(idx_next, wide.at[1], picked.at[1])
+    copies = []
+    for way, (right_ref, outs) in enumerate(((inner_ref, to_prev), (pu_ref, to_next))):
+        left = picked[way].astype(BF16)
+        for plane in range(planes):
+            spread(total.at[way], plane, planes, dot(left, right_ref[plane]))
+        for chunk, (start, end) in enumerate(pieces(planes)):
+            ready[way, start:end] = joined(total.at[way, :, start:end]).astype(BF16)
+            copies += fetch([ready.at[way, start:end]], [outs[chunk]], [sem.at[way, chunk]])
+    arrive(copies)
+
+
+def local_kernel(present_ref, pattern_ref, vu_hbm, vd_hbm, vd_next_ref, pd_hbm, pu_hbm, *refs):
     chunks = len(ROWS)
     outs = refs[:chunks]
-    idx_ref, wide, picked_u, picked_d, same, one_up, bare, pd_ref, pu_ref, sem = refs[chunks:]
+    idx_ref, wide, picked_u, picked_d, same, one_up, bare, pd_ref, pu_ref, vd_ref, vu_ref, sem, v_sem = refs[
+        chunks:
+    ]
     planes = pu_ref.shape[0]
-    copies = []
-    for plane in range(planes):
-        copies.append(
-            (
-                pltpu.make_async_copy(pd_hbm.at[plane], pd_ref.at[plane], sem.at[0, plane]),
-                pltpu.make_async_copy(pu_hbm.at[plane], pu_ref.at[plane], sem.at[1, plane]),
-            )
-        )
-        for copy in copies[-1]:
-            copy.start()
+    small = fetch([vd_hbm, vu_hbm], [vd_ref, vu_ref], [v_sem.at[0], v_sem.at[1]])
+    copies = [
+        fetch(
+            [pd_hbm.at[plane], pu_hbm.at[plane]],
+            [pd_ref.at[plane], pu_ref.at[plane]],
+            [sem.at[0, plane], sem.at[1, plane]],
+        )
+        for plane in range(planes)
+    ]
     live_list(present_ref, idx_ref)
+    arrive(small)
     scale = pattern_ref[0].astype(F32)
     wide[...] = vu_ref[...].astype(F32) * scale
     masked = wide[...].astype(BF16)
@@ -200,8 +218,7 @@
     left_d = picked_d[...].astype(BF16)
     nothing = jnp.zeros(picked_u.shape, F32)
     for plane in range(planes):
-        for copy in copies[plane]:
-            copy.wait()
+        arrive(copies[plane])
         spread(same, plane, planes, dot(left_d, pd_ref[plane]) + dot_nt(left_u, pu_ref[plane]))
         spread(one_up, plane, planes, dot(left_d, pu_ref[plane]))
         spread(bare, plane, planes, picked_u[...] if plane < planes // 2 else nothing)
@@ -213,14 +230,31 @@
         )
 
 
-def join_kernel(pattern_ref, local_ref, before_ref, after_ref, vu_ref, out_ref):
+def join_kernel(pattern_ref, local_ref, before_hbm, after_hbm, vu_hbm, out_ref, before, after, vu_ref, sem, v_sem):
     scale = pattern_ref[0].astype(F32)
+    size = local_ref.shape[0]
+    parts = sem.shape[1]
+    step = size // parts
+    small = fetch([vu_hbm], [vu_ref], [v_sem.at[0]])
+    copies = []
+    for part in range(parts):
+        rows = slice(part * step, (part + 1) * step)
+        copies.append(
+            fetch(
+                [before_hbm.at[rows], after_hbm.at[rows]],
+                [before.at[rows], after.at[rows]],
+                [sem.at[0, part], sem.at[1, part]],
+            )
+        )
+    out_ref[size:, :] = jnp.zeros((out_ref.shape[0] - size, out_ref.shape[1]), BF16)
+    arrive(small)
     masked = (vu_ref[...].astype(F32) * scale).astype(BF16)
-    size = local_ref.shape[0]
-    out_ref[0:size, :] = (
-        local_ref[...] + dot(before_ref[...], masked) + after_ref[...].astype(F32) * scale
-    ).astype(BF16)
-    out_ref[size:, :] = jnp.zeros((out_ref.shape[0] - size, out_ref.shape[1]), BF16)
+    for part in range(parts):
+        rows = slice(part * step, (part + 1) * step)
+        arrive(copies[part])
+        out_ref[rows, :] = (
+            local_ref[rows, :] + dot(before[rows], masked) + after[rows].astype(F32) * scale
+        ).astype(BF16)
 
 
 def spectrum_kernel(scale, forward_ref, got_ref, *outs):
@@ -250,16 +284,41 @@
 
 def unpack_kernel(present_ref, *refs):
     chunks = len(ROWS)
-    got_refs, (out_ref, idx_ref, turn_ref) = refs[:chunks], refs[chunks:]
-    planes = out_ref.shape[0]
-    count = live_list(present_ref, idx_ref)
-    out_ref[...] = jnp.zeros(out_ref.shape, BF16)
+    got_refs, (out_hbm, idx_ref, rest_ref, turn_ref, ready, nothing, sem) = refs[:chunks], refs[chunks:]
+    groups = present_ref.shape[0]
+    planes = out_hbm.shape[0]
+    nothing[...] = jnp.zeros(nothing.shape, BF16)
+    for slot in range(LIVE):
+        idx_ref[slot] = 0
+    count = jnp.int32(0)
+    for group in range(groups):
+        live = jnp.where(present_ref[group] > 0, 1, 0)
+        idx_ref[count] = group
+        rest_ref[group - count] = group
+        count = count + live
+
+    def out_rows(group):
+        return out_hbm.at[:, pl.ds(pl.multiple_of(group * RG, RG), RG), :]
+
+    def blank(at):
+        group = rest_ref[at]
+        return pltpu.make_async_copy(nothing, out_rows(group), sem.at[group])
+
+    def start_blank(at, carry):
+        blank(at).start()
+        return carry
+
+    def wait_blank(at, carry):
+        blank(at).wait()
+        return carry
+
+    lax.fori_loop(0, groups - count, start_blank, 0)
     for slot in range(LIVE):
 
         @pl.when(slot < count)
         def _(slot=slot):
             turn = turn_ref.at[slot % turn_ref.shape[0]]
-            row = pl.multiple_of(idx_ref[slot] * RG, RG)
+            group = idx_ref[slot]
             for r in range(RG):
                 chunk, peer, inner = place(slot * RG + r)
                 at = (peer * ROWS[chunk] + inner) * planes
@@ -268,7 +327,16 @@
                     turn[j, r * planes : (r + 1) * planes] = value[:, j * LANES : (j + 1) * LANES]
             for plane in range(planes):
                 value = [turn[j, pl.ds(plane, RG, stride=planes), :] for j in range(turn.shape[0])]
-                out_ref[plane, pl.ds(row, RG), :] = jnp.concatenate(value, 1).astype(BF16)
+                ready[slot, plane] = jnp.concatenate(value, 1).astype(BF16)
+            pltpu.make_async_copy(ready.at[slot], out_rows(group), sem.at[group]).start()
+
+    def wait_live(slot, carry):
+        group = idx_ref[slot]
+        pltpu.make_async_copy(ready.at[slot], out_rows(group), sem.at[group]).wait()
+        return carry
+
+    lax.fori_loop(0, count, wait_live, 0)
+    lax.fori_loop(0, groups - count, wait_blank, 0)
 
 
 def per_device(g_upper, p_diag, p_upper, v_diag, v_upper, v_pattern, element_present):
@@ -280,11 +348,12 @@
     flat = live * planes
     sizes = [end - start for start, end in pieces(planes)]
 
-    green = g_upper.reshape(planes, size, size)
-    p_d = p_diag.reshape(planes, size, size)
-    p_u = p_upper.reshape(planes, size, size)
-    v_d = v_diag.reshape(size, size)
-    v_u = v_upper.reshape(size, size)
+    def stay(value):
+        return pltpu.with_memory_space_constraint(value, pltpu.HBM)
+
+    green, p_d, p_u = (stay(x.reshape(planes, size, size)) for x in (g_upper, p_diag, p_upper))
+    v_d, v_u = (x.reshape(size, size) for x in (v_diag, v_upper))
+    v_d_here, v_u_here = stay(v_d), stay(v_u)
     present = element_present.reshape(-1)
     groups = present.shape[0]
 
@@ -301,13 +370,13 @@
     turn = pltpu.VMEM((4, size // LANES, RG * planes, LANES), F32)
     big = planes * size * size * 2
 
-    def call(kernel, outs, ins, scratch, units, mib):
+    def call(kernel, outs, ins, scratch, units, mib, place_out=vmem):
         many = isinstance(outs, list)
         return pl.pallas_call(
             kernel,
             out_shape=outs,
             in_specs=ins,
-            out_specs=[vmem() for _ in outs] if many else vmem(),
+            out_specs=[place_out() for _ in outs] if many else place_out(),
             scratch_shapes=scratch,
             compiler_params=pltpu.CompilerParams(vmem_limit_bytes=mib * 2**20),
             cost_estimate=pl.CostEstimate(
@@ -320,22 +389,35 @@
 
     whole = pltpu.VMEM((planes, size, size), BF16)
     sems = pltpu.SemaphoreType.DMA((2, planes))
-    inner, p_u_here = call(
+    pair = pltpu.SemaphoreType.DMA((2,))
+    block = pltpu.VMEM((size, size), BF16)
+    inner, p_u_held = call(
         inner_kernel,
         [array(planes, size, size)] * 2,
-        [smem()] + [vmem()] * 2 + [hbm()] * 2,
-        [whole, sems],
+        [smem()] + [hbm()] * 4,
+        [whole, block, block, sems, pair],
         3.2,
         12,
-    )(v_pattern, v_d, v_u, p_d, p_u)
+    )(v_pattern, v_d_here, v_u_here, p_d, p_u)
     outward = call(
         outward_kernel,
         [array(n, size) for n in sizes] * 2,
-        [smem()] * 3 + [vmem()] * 4,
-        [idx, idx, square, strip, total, total],
+        [smem()] * 3 + [hbm()] + [vmem()] * 3,
+        [
+            idx,
+            idx,
+            block,
+            pltpu.VMEM((2, size, size), F32),
+            pltpu.VMEM((2, live, size), F32),
+            pltpu.VMEM((2, size // LANES, flat, LANES), F32),
+            pltpu.VMEM((2, flat, size), BF16),
+            pair,
+            pltpu.SemaphoreType.DMA((2, len(ROWS))),
+        ],
         2,
-        18,
-    )(present_next, present_prev, v_pattern, v_u, v_u_prev, p_u_here, inner)
+        20,
+        hbm,
+    )(present_next, present_prev, v_pattern, v_u_here, v_u_prev, p_u_held, inner)
     chunks = len(ROWS)
     before = [shifted(piece, 1) for piece in outward[:chunks]]
     after = [shifted(piece, -1) for piece in outward[chunks:]]
@@ -350,11 +432,11 @@
     own = call(
         local_kernel,
         [array(n, size, dtype=F32) for n in sizes],
-        [smem()] * 2 + [vmem()] * 3 + [hbm()] * 2,
-        [idx, square, strip, strip, total, total, total, whole, whole, sems],
+        [smem()] * 2 + [hbm()] * 2 + [vmem()] + [hbm()] * 2,
+        [idx, square, strip, strip, total, total, total, whole, whole, block, block, sems, pair],
         5,
         22,
-    )(present, v_pattern, v_u, v_d, v_d_next, p_d, p_u)
+    )(present, v_pattern, v_u_here, v_d_here, v_d_next, p_d, p_u)
 
     green_freq = call(
         functools.partial(spectrum_kernel, 1.0 / (energies * math.sqrt(energies))),
@@ -370,11 +452,17 @@
         send = call(
             join_kernel,
             array(peers * rows * planes, size),
-            [smem()] + [vmem()] * 4,
-            [],
+            [smem(), vmem()] + [hbm()] * 3,
+            [
+                pltpu.VMEM((sizes[chunk], size), BF16),
+                pltpu.VMEM((sizes[chunk], size), BF16),
+                block,
+                pltpu.SemaphoreType.DMA((2, 5)),
+                pair,
+            ],
             rows / RG,
-            8,
-        )(v_pattern, own[chunk], before[chunk], after[chunk], v_u)
+            10,
+        )(v_pattern, own[chunk], stay(before[chunk]), stay(after[chunk]), v_u_here)
         got = routed(send.reshape(peers, rows, planes, size))
         result = call(
             convolve_kernel, array(peers, rows, planes, size), [vmem()] * 4, [], rows / RG, 10
@@ -383,7 +471,20 @@
         returned.append(back.reshape(peers * rows * planes, size))
 
     sigma = call(
-        unpack_kernel, array(planes, size, size), [smem()] + [vmem()] * chunks, [idx, turn], 0.3, 8
+        unpack_kernel,
+        array(planes, size, size),
+        [smem()] + [vmem()] * chunks,
+        [
+            idx,
+            idx,
+            turn,
+            held,
+            pltpu.VMEM((planes, RG, size), BF16),
+            pltpu.SemaphoreType.DMA((groups,)),
+        ],
+        0.3,
+        8,
+        hbm,
     )(present, *returned)
     return sigma.reshape(halves, local, 1, size, size)
 

time: 147 us -> 142 us (0.966)
  local copies, waits for them, and re-layouts: 12.1 us -> 2.55 us
  Pallas kernels: 34.5 us -> 39.5 us
    unnamed x28 -> x12, local copies, waits for them, and re-layouts: 12.1 us -> 2.55 us
    pallas_call x2, Pallas kernels: 8.9 us -> 11.5 us  [the longest x1 6.52 us: per_device(): call(inner_kernel, [array(planes, size, size)] * 2, [smem()] + [hbm()] *...]
  transfers between devices with their start and end apart: 8 -> 8, of which waited for: 2 -> 2; matrix products, arithmetic and copies ran while one was open for 0% -> 0% of each run, Pallas kernels for 15% -> 19%
where the time goes in v2:
time: 142 us
  waiting for transfers between devices  45.1 us (32%)
  Pallas kernels  39.5 us (28%)
  starting transfers between devices  27.4 us (19%)
  blocking collectives  26.4 us (19%)
  local copies, waits for them, and re-layouts  2.55 us (2%)
    all_to_all x1, blocking collectives, routed(): lax.all_to_all(value, 'energy', split_axis=0, concat_axis=0, tiled=True)  26.4 us
    ppermute x6, waiting for transfers between devices, shifted(): return lax.ppermute(value, 'space', pairs)  24.5 us
    all_to_all x2, waiting for transfers between devices, routed(): lax.all_to_all(value, 'energy', split_axis=0, concat_axis=0, tiled=True)  20.6 us
    all_to_all x2, starting transfers between devices, routed(): lax.all_to_all(value, 'energy', split_axis=0, concat_axis=0, tiled=True)  18.2 us
    pallas_call x1, Pallas kernels, per_device(): call(local_kernel, [array(n, size, dtype=F32) for n in sizes], [smem()] *...  10.7 us
    ppermute x6, starting transfers between devices, shifted(): return lax.ppermute(value, 'space', pairs)  9.12 us
    pallas_call x1, Pallas kernels, per_device(): call(inner_kernel, [array(planes, size, size)] * 2, [smem()] + [hbm()] *...  6.52 us
    pallas_call x1, Pallas kernels, per_device(): call(outward_kernel, [array(n, size) for n in sizes] * 2, [smem()] * 3 +...  6.14 us
  transfers between devices with their start and end apart: 8, of which 2 were waited for; matrix products, arithmetic and copies ran while one was open for 0% of the time, Pallas kernels for 19%

profile of v2, /device:TPU:33, one launch (start us, length us, event | category | flops | bytes accessed | tf_op | source)
XLA Modules:
  0.0 141.9 jit_solution(8263824549788125615)
XLA Ops:
  0.0 1.6 %collective-permute-start.3 = (bf16[384,384]{1,0:T(8,128)(2,1)}, bf16[384,384]{1,0:T(8,128)(2,1)S(1)}, u32[]{:S(2)}, u32[]{:S(2)}) collective-permute-start(bf16[384,384]{1,0:T(8,128)(2,1)} %bitcast.18), channel_id=1, source_target_pairs={{0,1},{1,2},{2,3},{3,4},{4,5},{5,6},{6,7},{7,0},{8,9},{9,10},{10,1... | collective-permute-start | bytes 884744 | tf_op jit(solution)/shard_map/ppermute | solution.py:37
  1.6 0.0 collective-permute-start.1
  1.6 1.6 %collective-permute-start.2 = (s32[48]{0:T(128)}, s32[48]{0:T(128)S(1)}, u32[]{:S(2)}, u32[]{:S(2)}) collective-permute-start(s32[48]{0:T(128)} %bitcast.13), channel_id=1, source_target_pairs={{0,1},{1,2},{2,3},{3,4},{4,5},{5,6},{6,7},{7,0},{8,9},{9,10},{10,1... | collective-permute-start | bytes 584 | tf_op jit(solution)/shard_map/ppermute | solution.py:37
  3.9 6.5 %shard_map.94 = (bf16[8,384,384]{2,1,0:T(8,128)(2,1)S(1)}, bf16[8,384,384]{2,1,0:T(8,128)(2,1)S(1)}) custom-call(s32[1]{0:T(128)S(6)} %copy.11.pattern_ref, bf16[384,384]{1,0:T(8,128)(2,1)} %bitcast.27, bf16[384,384]{1,0:T(8,128)(2,1)} %bitcast.19, bf16[8,384,384]{2,1,0:T(8,128)(2,1)} %bitcast.23, bf16[8,384,384]{2,1,0:T(8,128)(2,1)} %bitcast.25), custom_call_target="tpu_custom_call" | custom-call | flops 1811939328 | bytes 2359296 | tf_op jit(solution)/shard_map/pallas_call | solution.py:394
  10.5 0.0 collective-permute-done.1.next_ref
  10.5 0.0 collective-permute-done.2.prev_ref
  10.5 0.0 collective-permute-done.3.vu_prev_ref
  10.5 0.0 copy-start.4
  10.5 6.1 %shard_map.95 = (bf16[1920,384]{1,0:T(8,128)(2,1)}, bf16[1920,384]{1,0:T(8,128)(2,1)S(1)}) custom-call(s32[48]{0:T(128)S(1)} %collective-permute-done.1.next_ref, s32[48]{0:T(128)S(1)} %collective-permute-done.2.prev_ref, s32[1]{0:T(128)S(6)} %copy.11.pattern_ref, bf16[384,384]{1,0:T(8,128)(2,1)} %bitcast.20, ...), custom_call_target="tpu_custom_call" | custom-call | flops 1132462080 | bytes 2359296 | tf_op jit(solution)/shard_map/pallas_call | solution.py:402
  16.6 2.9 %collective-permute-start.4 = (bf16[1920,384]{1,0:T(8,128)(2,1)}, bf16[1920,384]{1,0:T(8,128)(2,1)}, u32[]{:S(2)}, u32[]{:S(2)}) collective-permute-start(bf16[1920,384]{1,0:T(8,128)(2,1)} %get-tuple-element.11), channel_id=1, source_target_pairs={{0,1},{1,2},{2,3},{3,4},{4,5},{5,6},{6,7},{7,0},{8,9},{9,10},{10,1... | collective-permute-start | bytes 4423688 | tf_op jit(solution)/shard_map/ppermute | solution.py:37
  19.6 0.0 collective-permute-start.5
  19.6 0.0 copy-done.4
  19.6 3.7 %shard_map.91 = bf16[32,8,8,384]{3,2,1,0:T(8,128)(2,1)} custom-call(s32[48]{0:T(128)S(1)} %bitcast.14, bf16[8,384,384]{2,1,0:T(8,128)(2,1)} %bitcast.17), custom_call_target="tpu_custom_call" | custom-call | flops 169869312 | bytes 2359296 | tf_op jit(solution)/shard_map/pallas_call | solution.py:427
  23.3 0.0 copy-start.5
  23.3 8.7 %all-to-all-start = ((bf16[32,8,8,384]{3,2,1,0:T(8,128)(2,1)}), bf16[32,8,8,384]{3,2,1,0:T(8,128)(2,1)S(1)}, u32[]{:S(2)}, u32[]{:S(2)}) async-start(bf16[32,8,8,384]{3,2,1,0:T(8,128)(2,1)} %shard_map.91), calls=%async_computation | async-start | bytes 3145728 | tf_op jit(solution)/shard_map/all_to_all | solution.py:41
  32.0 0.0 copy-done.5
  32.0 2.9 %collective-permute-start = (bf16[384,384]{1,0:T(8,128)(2,1)S(1)}, bf16[384,384]{1,0:T(8,128)(2,1)S(1)}, u32[]{:S(2)}, u32[]{:S(2)}) collective-permute-start(bf16[384,384]{1,0:T(8,128)(2,1)S(1)} %bitcast.29), channel_id=1, source_target_pairs={{0,7},{1,0},{2,1},{3,2},{4,3},{5,4},{6,5},{7,6},{8,15},{9,8},{10,9... | collective-permute-start | bytes 884744 | tf_op jit(solution)/shard_map/ppermute | solution.py:37
  34.9 24.5 %collective-permute-done.vd_next_ref = bf16[384,384]{1,0:T(8,128)(2,1)S(1)} collective-permute-done((bf16[384,384]{1,0:T(8,128)(2,1)S(1)}, bf16[384,384]{1,0:T(8,128)(2,1)S(1)}, u32[]{:S(2)}, u32[]{:S(2)}) %collective-permute-start) | collective-permute-done | bytes 294944 | tf_op jit(solution)/shard_map/ppermute | solution.py:37
  59.4 10.7 %shard_map.93.local_ref = f32[1920,384]{1,0:T(8,128)S(1)} custom-call(s32[48]{0:T(128)S(1)} %bitcast.15, s32[1]{0:T(128)S(6)} %copy.11.pattern_ref, bf16[384,384]{1,0:T(8,128)(2,1)} %bitcast.21, bf16[384,384]{1,0:T(8,128)(2,1)} %bitcast.28, bf16[384,384]{1,0:T(8,128)(2,1)S(1)} %collective-permute-done.vd_next_ref, bf16[8,384,384]{2,1,0:T(8,128)(2,1)} %bitcast.24, ...), custom_call_target="tpu_custom_call" | custom-call | flops 2831155200 | bytes 2359296 | tf_op jit(solution)/shard_map/pallas_call | solution.py:432
  70.1 0.0 collective-permute-done.4.before_hbm
  70.1 0.0 collective-permute-done.5.after_hbm
  70.2 5.0 %shard_map.96 = bf16[2048,384]{1,0:T(8,128)(2,1)} custom-call(s32[1]{0:T(128)S(6)} %copy.11.pattern_ref, f32[1920,384]{1,0:T(8,128)S(1)} %shard_map.93.local_ref, bf16[1920,384]{1,0:T(8,128)(2,1)} %collective-permute-done.4.before_hbm, bf16[1920,384]{1,0:T(8,128)(2,1)} %collective-permute-done.5.after_hbm, bf16[384,384]{1,0:T(8,128)(2,1)} %bitcast.22), custom_call_target="tpu_custom_call" | custom-call | flops 566231040 | bytes 2359296 | tf_op jit(solution)/shard_map/pallas_call | solution.py:452
  75.2 0.0 all-to-all-done.got_ref
  75.2 0.0 copy-start
  75.2 0.0 copy-start.2
  75.2 1.1 copy-done
  76.3 9.5 %all-to-all-start.1 = ((bf16[32,8,8,384]{3,2,1,0:T(8,128)(2,1)}), bf16[32,8,8,384]{3,2,1,0:T(8,128)(2,1)}, u32[]{:S(2)}, u32[]{:S(2)}) async-start(bf16[32,8,8,384]{3,2,1,0:T(8,128)(2,1)} %bitcast.6), calls=%async_computation.1 | async-start | bytes 3145728 | tf_op jit(solution)/shard_map/all_to_all | solution.py:41
  85.8 0.0 copy-done.2
  85.9 0.0 copy-start.1
  85.9 1.4 copy-done.1
  87.3 0.0 copy-start.3
  87.3 0.7 shard_map.92.green_ref
  88.0 20.6 %all-to-all-done.1.got_ref = bf16[32,8,8,384]{3,2,1,0:T(8,128)(2,1)} async-done(((bf16[32,8,8,384]{3,2,1,0:T(8,128)(2,1)}), bf16[32,8,8,384]{3,2,1,0:T(8,128)(2,1)}, u32[]{:S(2)}, u32[]{:S(2)}) %all-to-all-start.1) | async-done | bytes 1572896 | tf_op jit(solution)/shard_map/all_to_all | solution.py:41
  108.6 0.0 copy-done.3
  108.6 3.9 %shard_map.97 = bf16[32,8,8,384]{3,2,1,0:T(8,128)(2,1)S(1)} custom-call(bf16[256,256]{1,0:T(8,128)(2,1)S(1)} %copy-done.2, bf16[256,256]{1,0:T(8,128)(2,1)S(1)} %copy-done.3, f32[8,256,384]{2,1,0:T(8,128)S(1)} %shard_map.92.green_ref, bf16[32,8,8,384]{3,2,1,0:T(8,128)(2,1)} %all-to-all-done.1.got_ref), custom_call_target="tpu_custom_call" | custom-call | flops 566231040 | bytes 2359296 | tf_op jit(solution)/shard_map/pallas_call | solution.py:467
  112.4 26.4 %all_to_all.15 = bf16[32,8,8,384]{3,2,1,0:T(8,128)(2,1)S(1)} all-to-all(bf16[32,8,8,384]{3,2,1,0:T(8,128)(2,1)S(1)} %shard_map.97), channel_id=1, replica_groups=mesh['energy'=32,'space'=8] {'energy'}, dimensions={0} | all-to-all | bytes 3145728 | tf_op jit(solution)/shard_map/all_to_all | solution.py:41
  138.9 2.9 %shard_map.98 = bf16[8,384,384]{2,1,0:T(8,128)(2,1)} custom-call(s32[48]{0:T(128)S(1)} %bitcast.16, bf16[2048,384]{1,0:T(8,128)(2,1)S(1)} %bitcast.11), custom_call_target="tpu_custom_call" | custom-call | flops 169869312 | bytes 2359296 | tf_op jit(solution)/shard_map/pallas_call | solution.py:473
Async XLA Ops:
  0.0 10.5 %collective-permute-start.3 = (bf16[384,384]{1,0:T(8,128)(2,1)}, bf16[384,384]{1,0:T(8,128)(2,1)S(1)}, u32[]{:S(2)}, u32[]{:S(2)}) collective-permute-start(bf16[384,384]{1,0:T(8,128)(2,1)} %bitcast.18), channel_id=1, source_target_pairs={{0,1},{1,2},{2,3},{3,4},{4,5},{5,6},{6,7},{7,0},{8,9},{9,10},{10,1... | collective-permute-start | bytes 884744 | tf_op jit(solution)/shard_map/ppermute | solution.py:37
  1.6 8.8 %collective-permute-start.1 = (s32[48]{0:T(128)}, s32[48]{0:T(128)S(1)}, u32[]{:S(2)}, u32[]{:S(2)}) collective-permute-start(s32[48]{0:T(128)} %bitcast.12), channel_id=1, source_target_pairs={{0,7},{1,0},{2,1},{3,2},{4,3},{5,4},{6,5},{7,6},{8,15},{9,8},{10,9... | collective-permute-start | bytes 584 | tf_op jit(solution)/shard_map/ppermute | solution.py:37
  1.6 8.8 %collective-permute-start.2 = (s32[48]{0:T(128)}, s32[48]{0:T(128)S(1)}, u32[]{:S(2)}, u32[]{:S(2)}) collective-permute-start(s32[48]{0:T(128)} %bitcast.13), channel_id=1, source_target_pairs={{0,1},{1,2},{2,3},{3,4},{4,5},{5,6},{6,7},{7,0},{8,9},{9,10},{10,1... | collective-permute-start | bytes 584 | tf_op jit(solution)/shard_map/ppermute | solution.py:37
  10.5 9.1 %copy-start.4 = (s32[1,48]{1,0:T(1,128)S(1)}, s32[1,48]{1,0:T(1,128)}, u32[]{:S(2)}) copy-start(s32[1,48]{1,0:T(1,128)} %param.15) | copy-start | bytes 580
  16.6 53.5 %collective-permute-start.4 = (bf16[1920,384]{1,0:T(8,128)(2,1)}, bf16[1920,384]{1,0:T(8,128)(2,1)}, u32[]{:S(2)}, u32[]{:S(2)}) collective-permute-start(bf16[1920,384]{1,0:T(8,128)(2,1)} %get-tuple-element.11), channel_id=1, source_target_pairs={{0,1},{1,2},{2,3},{3,4},{4,5},{5,6},{6,7},{7,0},{8,9},{9,10},{10,1... | collective-permute-start | bytes 4423688 | tf_op jit(solution)/shard_map/ppermute | solution.py:37
  19.6 50.6 %collective-permute-start.5 = (bf16[1920,384]{1,0:T(8,128)(2,1)S(1)}, bf16[1920,384]{1,0:T(8,128)(2,1)}, u32[]{:S(2)}, u32[]{:S(2)}) collective-permute-start(bf16[1920,384]{1,0:T(8,128)(2,1)S(1)} %get-tuple-element.12), channel_id=1, source_target_pairs={{0,7},{1,0},{2,1},{3,2},{4,3},{5,4},{6,5},{7,6},{8,15},{9,8},{10,9... | collective-permute-start | bytes 4423688 | tf_op jit(solution)/shard_map/ppermute | solution.py:37
  23.3 8.8 %copy-start.5 = (bf16[1,384,384]{2,1,0:T(8,128)(2,1)S(1)}, bf16[1,384,384]{2,1,0:T(8,128)(2,1)}, u32[]{:S(2)}) copy-start(bf16[1,384,384]{2,1,0:T(8,128)(2,1)} %param.12) | copy-start | bytes 884740
  23.3 51.9 %all-to-all-start = ((bf16[32,8,8,384]{3,2,1,0:T(8,128)(2,1)}), bf16[32,8,8,384]{3,2,1,0:T(8,128)(2,1)S(1)}, u32[]{:S(2)}, u32[]{:S(2)}) async-start(bf16[32,8,8,384]{3,2,1,0:T(8,128)(2,1)} %shard_map.91), calls=%async_computation | async-start | bytes 3145728 | tf_op jit(solution)/shard_map/all_to_all | solution.py:41
  32.0 27.4 %collective-permute-start = (bf16[384,384]{1,0:T(8,128)(2,1)S(1)}, bf16[384,384]{1,0:T(8,128)(2,1)S(1)}, u32[]{:S(2)}, u32[]{:S(2)}) collective-permute-start(bf16[384,384]{1,0:T(8,128)(2,1)S(1)} %bitcast.29), channel_id=1, source_target_pairs={{0,7},{1,0},{2,1},{3,2},{4,3},{5,4},{6,5},{7,6},{8,15},{9,8},{10,9... | collective-permute-start | bytes 884744 | tf_op jit(solution)/shard_map/ppermute | solution.py:37
  75.2 1.1 copy-start
  75.2 10.7 %copy-start.2 = (bf16[256,256]{1,0:T(8,128)(2,1)S(1)}, bf16[256,256]{1,0:T(8,128)(2,1)}, u32[]{:S(2)}) copy-start(bf16[256,256]{1,0:T(8,128)(2,1)} %constant.4.clone.forward_ref) | copy-start | bytes 393220
  76.3 32.2 %all-to-all-start.1 = ((bf16[32,8,8,384]{3,2,1,0:T(8,128)(2,1)}), bf16[32,8,8,384]{3,2,1,0:T(8,128)(2,1)}, u32[]{:S(2)}, u32[]{:S(2)}) async-start(bf16[32,8,8,384]{3,2,1,0:T(8,128)(2,1)} %bitcast.6), calls=%async_computation.1 | async-start | bytes 3145728 | tf_op jit(solution)/shard_map/all_to_all | solution.py:41
  85.9 1.4 copy-start.1
  87.3 21.3 %copy-start.3 = (bf16[256,256]{1,0:T(8,128)(2,1)S(1)}, bf16[256,256]{1,0:T(8,128)(2,1)}, u32[]{:S(2)}) copy-start(bf16[256,256]{1,0:T(8,128)(2,1)} %constant.5.clone.inverse_ref) | copy-start | bytes 393220

commit v3 on v2

--- a/solution.py
+++ b/solution.py
@@ -14,6 +14,7 @@
 RG = 8
 LANES = 128
 ROWS = (8,)
+PARTS = (0, 120, 240)
 
 F32 = jnp.float32
 BF16 = jnp.bfloat16
@@ -113,11 +114,6 @@
         start += LIVE * rows
 
 
-def pieces(planes):
-    starts = np.concatenate([[0], np.cumsum(ROWS)]) * LIVE * planes
-    return [(int(x), int(y)) for x, y in zip(starts[:-1], starts[1:])]
-
-
 def pack_kernel(present_ref, g_ref, out_ref, idx_ref, turn_ref, held_ref, sem):
     planes = g_ref.shape[0]
     live_list(present_ref, idx_ref)
@@ -142,59 +138,45 @@
         out_ref[peer] = jnp.zeros(out_ref.shape[1:], BF16)
 
 
-def inner_kernel(
-    pattern_ref, vd_hbm, vu_hbm, pd_hbm, pu_hbm, out_ref, pu_ref, pd_ref, vd_ref, vu_ref, sem, v_sem
-):
-    planes = pu_ref.shape[0]
-    small = fetch([vd_hbm, vu_hbm], [vd_ref, vu_ref], [v_sem.at[0], v_sem.at[1]])
-    copies = [
-        fetch(
-            [pd_hbm.at[plane], pu_hbm.at[plane]],
-            [pd_ref.at[plane], pu_ref.at[plane]],
-            [sem.at[0, plane], sem.at[1, plane]],
-        )
-        for plane in range(planes)
-    ]
-    arrive(small)
+def inner_kernel(pattern_ref, vd_ref, vu_ref, pd_ref, pu_ref, out_ref):
     scale = pattern_ref[0].astype(F32)
     turned = ((vu_ref[...].astype(F32) * scale).T).astype(BF16)
     right = jnp.concatenate([vd_ref[...], turned], axis=0)
-    for plane in range(planes):
-        arrive(copies[plane])
+    for plane in range(pu_ref.shape[0]):
         left = jnp.concatenate([pd_ref[plane], pu_ref[plane]], axis=1)
         out_ref[plane] = dot(left, right).astype(BF16)
 
 
-def outward_kernel(next_ref, prev_ref, pattern_ref, vu_hbm, vu_prev_ref, pu_ref, inner_ref, *refs):
-    chunks = len(ROWS)
+def prepare_kernel(present_ref, pattern_ref, vu_ref, out_ref, idx_ref, wide, picked):
+    live_list(present_ref, idx_ref)
+    wide[...] = vu_ref[...].astype(F32) * pattern_ref[0].astype(F32)
+    pick_rows(idx_ref, wide, picked)
+    out_ref[...] = picked[...].astype(BF16)
+
+
+def outward_kernel(next_ref, pattern_ref, vu_ref, left_ref, pu_ref, inner_ref, *refs):
+    chunks = len(PARTS) - 1
     to_next, to_prev = refs[:chunks], refs[chunks : 2 * chunks]
-    idx_next, idx_prev, vu_ref, wide, picked, total, ready, v_sem, sem = refs[2 * chunks :]
+    idx_next, wide, picked, total_next, total_prev = refs[2 * chunks :]
     planes = pu_ref.shape[0]
-    small = fetch([vu_hbm], [vu_ref], [v_sem.at[0]])
-    scale = pattern_ref[0].astype(F32)
-    live_list(prev_ref, idx_prev)
-    wide[0] = vu_prev_ref[...].astype(F32)
-    pick_rows(idx_prev, wide.at[0], picked.at[0])
     live_list(next_ref, idx_next)
-    arrive(small)
-    wide[1] = (vu_ref[...].astype(F32) * scale).T
-    pick_rows(idx_next, wide.at[1], picked.at[1])
-    copies = []
-    for way, (right_ref, outs) in enumerate(((inner_ref, to_prev), (pu_ref, to_next))):
-        left = picked[way].astype(BF16)
-        for plane in range(planes):
-            spread(total.at[way], plane, planes, dot(left, right_ref[plane]))
-        for chunk, (start, end) in enumerate(pieces(planes)):
-            ready[way, start:end] = joined(total.at[way, :, start:end]).astype(BF16)
-            copies += fetch([ready.at[way, start:end]], [outs[chunk]], [sem.at[way, chunk]])
-    arrive(copies)
+    wide[...] = (vu_ref[...].astype(F32) * pattern_ref[0].astype(F32)).T
+    pick_rows(idx_next, wide, picked)
+    left_next = picked[...].astype(BF16)
+    left_prev = left_ref[...]
+    for plane in range(planes):
+        spread(total_prev, plane, planes, dot(left_prev, inner_ref[plane]))
+        spread(total_next, plane, planes, dot(left_next, pu_ref[plane]))
+    for chunk in range(chunks):
+        rows = slice(PARTS[chunk] * planes, PARTS[chunk + 1] * planes)
+        to_next[chunk][...] = joined(total_next.at[:, rows]).astype(BF16)
+        to_prev[chunk][...] = joined(total_prev.at[:, rows]).astype(BF16)
 
 
 def local_kernel(present_ref, pattern_ref, vu_hbm, vd_hbm, vd_next_ref, pd_hbm, pu_hbm, *refs):
-    chunks = len(ROWS)
-    outs = refs[:chunks]
+    outs = refs[: len(PARTS) - 1]
     idx_ref, wide, picked_u, picked_d, same, one_up, bare, pd_ref, pu_ref, vd_ref, vu_ref, sem, v_sem = refs[
-        chunks:
+        len(outs) :
     ]
     planes = pu_ref.shape[0]
     small = fetch([vd_hbm, vu_hbm], [vd_ref, vu_ref], [v_sem.at[0], v_sem.at[1]])
@@ -222,7 +204,8 @@
         spread(same, plane, planes, dot(left_d, pd_ref[plane]) + dot_nt(left_u, pu_ref[plane]))
         spread(one_up, plane, planes, dot(left_d, pu_ref[plane]))
         spread(bare, plane, planes, picked_u[...] if plane < planes // 2 else nothing)
-    for out_ref, (start, end) in zip(outs, pieces(planes)):
+    for part, out_ref in enumerate(outs):
+        start, end = PARTS[part] * planes, PARTS[part + 1] * planes
         out_ref[...] = (
             joined(bare.at[:, start:end])
             + dot(joined(same.at[:, start:end]).astype(BF16), masked)
@@ -230,29 +213,36 @@
         )
 
 
-def join_kernel(pattern_ref, local_ref, before_hbm, after_hbm, vu_hbm, out_ref, before, after, vu_ref, sem, v_sem):
+def join_kernel(part, pattern_ref, local_ref, before_hbm, after_hbm, vu_hbm, *refs):
+    done_ref = refs[0] if part else None
+    out_ref, before, after, vu_ref, sem, v_sem = refs[1 if part else 0 :]
     scale = pattern_ref[0].astype(F32)
     size = local_ref.shape[0]
     parts = sem.shape[1]
     step = size // parts
     small = fetch([vu_hbm], [vu_ref], [v_sem.at[0]])
     copies = []
-    for part in range(parts):
-        rows = slice(part * step, (part + 1) * step)
+    for at in range(parts):
+        rows = slice(at * step, (at + 1) * step)
         copies.append(
             fetch(
                 [before_hbm.at[rows], after_hbm.at[rows]],
                 [before.at[rows], after.at[rows]],
-                [sem.at[0, part], sem.at[1, part]],
+                [sem.at[0, at], sem.at[1, at]],
             )
         )
-    out_ref[size:, :] = jnp.zeros((out_ref.shape[0] - size, out_ref.shape[1]), BF16)
+    first = 0
+    if part:
+        first = done_ref.shape[0]
+        out_ref[:first, :] = done_ref[...]
+        tail = out_ref.shape[0] - first - size
+        out_ref[first + size :, :] = jnp.zeros((tail, out_ref.shape[1]), BF16)
     arrive(small)
     masked = (vu_ref[...].astype(F32) * scale).astype(BF16)
-    for part in range(parts):
-        rows = slice(part * step, (part + 1) * step)
-        arrive(copies[part])
-        out_ref[rows, :] = (
+    for at in range(parts):
+        rows = slice(at * step, (at + 1) * step)
+        arrive(copies[at])
+        out_ref[first + at * step : first + (at + 1) * step, :] = (
             local_ref[rows, :] + dot(before[rows], masked) + after[rows].astype(F32) * scale
         ).astype(BF16)
 
@@ -346,7 +336,7 @@
     energies = local * peers
     live = LIVE * RG
     flat = live * planes
-    sizes = [end - start for start, end in pieces(planes)]
+    sizes = [(end - start) * planes for start, end in zip(PARTS[:-1], PARTS[1:])]
 
     def stay(value):
         return pltpu.with_memory_space_constraint(value, pltpu.HBM)
@@ -354,14 +344,14 @@
     green, p_d, p_u = (stay(x.reshape(planes, size, size)) for x in (g_upper, p_diag, p_upper))
     v_d, v_u = (x.reshape(size, size) for x in (v_diag, v_upper))
     v_d_here, v_u_here = stay(v_d), stay(v_u)
+
+    def near(value):
+        return pltpu.with_memory_space_constraint(value, pltpu.VMEM)
+
+    p_d_near, p_u_near = near(p_diag.reshape(planes, size, size)), near(p_upper.reshape(planes, size, size))
+    v_d_near, v_u_near = near(v_d), near(v_u)
     present = element_present.reshape(-1)
     groups = present.shape[0]
-
-    present_prev = shifted(present, 1)
-    present_next = shifted(present, -1)
-    v_u_prev = shifted(v_u, 1)
-    v_d_next = shifted(v_d, -1)
-    forward, inverse = tables(energies, peers)
 
     idx = pltpu.SMEM((groups,), jnp.int32)
     square = pltpu.VMEM((size, size), F32)
@@ -387,38 +377,30 @@
     def array(*shape, dtype=BF16):
         return jax.ShapeDtypeStruct(shape, dtype)
 
+    chosen = call(
+        prepare_kernel, array(live, size), [smem()] * 2 + [vmem()], [idx, square, strip], 8, 6
+    )(present, v_pattern, v_u)
+    present_next = shifted(present, -1)
+    v_u_prev = shifted(chosen, 1)
+    v_d_next = shifted(v_d, -1)
+    forward, inverse = tables(energies, peers)
+
     whole = pltpu.VMEM((planes, size, size), BF16)
     sems = pltpu.SemaphoreType.DMA((2, planes))
     pair = pltpu.SemaphoreType.DMA((2,))
     block = pltpu.VMEM((size, size), BF16)
-    inner, p_u_held = call(
-        inner_kernel,
-        [array(planes, size, size)] * 2,
-        [smem()] + [hbm()] * 4,
-        [whole, block, block, sems, pair],
-        3.2,
-        12,
-    )(v_pattern, v_d_here, v_u_here, p_d, p_u)
+    inner = call(
+        inner_kernel, array(planes, size, size), [smem()] + [vmem()] * 4, [], 3.2, 12
+    )(v_pattern, v_d_near, v_u_near, p_d_near, p_u_near)
     outward = call(
         outward_kernel,
         [array(n, size) for n in sizes] * 2,
-        [smem()] * 3 + [hbm()] + [vmem()] * 3,
-        [
-            idx,
-            idx,
-            block,
-            pltpu.VMEM((2, size, size), F32),
-            pltpu.VMEM((2, live, size), F32),
-            pltpu.VMEM((2, size // LANES, flat, LANES), F32),
-            pltpu.VMEM((2, flat, size), BF16),
-            pair,
-            pltpu.SemaphoreType.DMA((2, len(ROWS))),
-        ],
+        [smem()] * 2 + [vmem()] * 4,
+        [idx, square, strip, total, total],
         2,
-        20,
-        hbm,
-    )(present_next, present_prev, v_pattern, v_u_here, v_u_prev, p_u_held, inner)
-    chunks = len(ROWS)
+        18,
+    )(present_next, v_pattern, v_u_near, v_u_prev, p_u_near, inner)
+    chunks = len(sizes)
     before = [shifted(piece, 1) for piece in outward[:chunks]]
     after = [shifted(piece, -1) for piece in outward[chunks:]]
 
@@ -447,33 +429,35 @@
         8,
     )(forward, got_green)
 
-    returned = []
-    for chunk, rows in enumerate(ROWS):
-        send = call(
-            join_kernel,
-            array(peers * rows * planes, size),
-            [smem(), vmem()] + [hbm()] * 3,
-            [
-                pltpu.VMEM((sizes[chunk], size), BF16),
-                pltpu.VMEM((sizes[chunk], size), BF16),
-                block,
-                pltpu.SemaphoreType.DMA((2, 5)),
-                pair,
-            ],
-            rows / RG,
-            10,
-        )(v_pattern, own[chunk], stay(before[chunk]), stay(after[chunk]), v_u_here)
-        got = routed(send.reshape(peers, rows, planes, size))
-        result = call(
-            convolve_kernel, array(peers, rows, planes, size), [vmem()] * 4, [], rows / RG, 10
-        )(forward, inverse, green_freq[chunk], got)
-        back = routed(result)
-        returned.append(back.reshape(peers * rows * planes, size))
+    joined_parts = []
+    for part, rows in enumerate(sizes):
+        last = part == len(sizes) - 1
+        joined_parts.append(
+            call(
+                functools.partial(join_kernel, part),
+                array(peers * RG * planes if last else rows, size),
+                [smem(), vmem()] + [hbm()] * 3 + [vmem()] * part,
+                [
+                    pltpu.VMEM((rows, size), BF16),
+                    pltpu.VMEM((rows, size), BF16),
+                    block,
+                    pltpu.SemaphoreType.DMA((2, 3)),
+                    pair,
+                ],
+                0.5,
+                8,
+            )(v_pattern, own[part], stay(before[part]), stay(after[part]), v_u_here, *joined_parts)
+        )
+    got = routed(joined_parts[-1].reshape(peers, RG, planes, size))
+    result = call(
+        convolve_kernel, array(peers, RG, planes, size), [vmem()] * 4, [], 1, 10
+    )(forward, inverse, green_freq[0], got)
+    returned = [routed(result).reshape(peers * RG * planes, size)]
 
     sigma = call(
         unpack_kernel,
         array(planes, size, size),
-        [smem()] + [vmem()] * chunks,
+        [smem()] + [vmem()] * len(returned),
         [
             idx,
             idx,

time: 142 us -> 155 us (1.092)
  the two profiles are of different devices: /device:TPU:33 before, /device:TPU:1 now
where the time goes in v3:
time: 155 us; the launch traced here: 154 us
  waiting for transfers between devices  56.8 us (37%)
  Pallas kernels  35.8 us (23%)
  starting transfers between devices  28.7 us (19%)
  blocking collectives  26.4 us (17%)
  local copies, waits for them, and re-layouts  5.42 us (3%)
    ppermute x7, waiting for transfers between devices, shifted(): return lax.ppermute(value, 'space', pairs)  36.2 us
    all_to_all x1, blocking collectives, routed(): lax.all_to_all(value, 'energy', split_axis=0, concat_axis=0, tiled=True)  26.4 us
    all_to_all x2, waiting for transfers between devices, routed(): lax.all_to_all(value, 'energy', split_axis=0, concat_axis=0, tiled=True)  20.6 us
    all_to_all x2, starting transfers between devices, routed(): lax.all_to_all(value, 'energy', split_axis=0, concat_axis=0, tiled=True)  17.6 us
    ppermute x7, starting transfers between devices, shifted(): return lax.ppermute(value, 'space', pairs)  11.2 us
    pallas_call x1, Pallas kernels, per_device(): call(local_kernel, [array(n, size, dtype=F32) for n in sizes], [smem()] *...  10.7 us
    pallas_call x2, Pallas kernels, per_device(): call(functools.partial(join_kernel, part), array(peers * RG * planes if l...  6.5 us
    unnamed x28, local copies, waits for them, and re-layouts  5.42 us
  transfers between devices with their start and end apart: 9, of which 3 were waited for; matrix products, arithmetic and copies ran while one was open for 0% of the time, Pallas kernels for 16%

profile of v3, /device:TPU:1, one launch (start us, length us, event | category | flops | bytes accessed | tf_op | source)
XLA Modules:
  0.0 154.3 jit_solution(9535120634681262376)
XLA Ops:
  0.0 0.0 copy-start.8
  0.0 0.7 copy-done.8
  0.7 4.3 %shard_map.91 = bf16[32,8,8,384]{3,2,1,0:T(8,128)(2,1)} custom-call(s32[48]{0:T(128)S(1)} %bitcast.26, bf16[8,384,384]{2,1,0:T(8,128)(2,1)} %bitcast.31), custom_call_target="tpu_custom_call" | custom-call | flops 169869312 | bytes 2359296 | tf_op jit(solution)/shard_map/pallas_call | solution.py:409
  4.9 0.0 copy-start.3
  4.9 0.0 copy-start.9
  5.0 8.7 %all-to-all-start = ((bf16[32,8,8,384]{3,2,1,0:T(8,128)(2,1)}), bf16[32,8,8,384]{3,2,1,0:T(8,128)(2,1)S(1)}, u32[]{:S(2)}, u32[]{:S(2)}) async-start(bf16[32,8,8,384]{3,2,1,0:T(8,128)(2,1)} %shard_map.91), calls=%async_computation | async-start | bytes 3145728 | tf_op jit(solution)/shard_map/all_to_all | solution.py:42
  14.3 0.0 copy-done.3
  14.3 0.0 copy-done.9
  14.4 0.0 copy-start
  14.4 0.0 copy-start.4
  14.4 0.0 copy-start.6
  14.4 0.7 shard_map.94
  15.1 1.1 collective-permute-start.2
  16.2 4.6 %collective-permute-start.1 = (s32[48]{0:T(128)S(1)}, s32[48]{0:T(128)S(1)}, u32[]{:S(2)}, u32[]{:S(2)}) collective-permute-start(s32[48]{0:T(128)S(1)} %bitcast.28), channel_id=1, source_target_pairs={{0,7},{1,0},{2,1},{3,2},{4,3},{5,4},{6,5},{7,6},{8,15},{9,8},{10,9... | collective-permute-start | bytes 584 | tf_op jit(solution)/shard_map/ppermute | solution.py:38
  20.8 0.0 copy-done
  20.8 0.0 copy-done.4
  20.9 0.0 copy-done.6
  20.9 2.6 %shard_map.95.inner_ref = bf16[8,384,384]{2,1,0:T(8,128)(2,1)S(1)} custom-call(s32[1]{0:T(128)S(6)} %copy.11.pattern_ref, bf16[384,384]{1,0:T(8,128)(2,1)S(1)} %bitcast.24, bf16[384,384]{1,0:T(8,128)(2,1)S(1)} %bitcast.19, bf16[8,384,384]{2,1,0:T(8,128)(2,1)S(1)} %bitcast.22, bf16[8,384,384]{2,1,0:T(8,128)(2,1)S(1)} %bitcast.12), custom_call_target="tpu_custom_call" | custom-call | flops 1811939328 | bytes 2359296 | tf_op jit(solution)/shard_map/pallas_call | solution.py:392
  23.5 0.0 collective-permute-done.1.next_ref
  23.5 2.0 %collective-permute-done.2.left_ref = bf16[240,384]{1,0:T(8,128)(2,1)S(1)} collective-permute-done((bf16[240,384]{1,0:T(8,128)(2,1)S(1)}, bf16[240,384]{1,0:T(8,128)(2,1)S(1)}, u32[]{:S(2)}, u32[]{:S(2)}) %collective-permute-start.2) | collective-permute-done | bytes 184352 | tf_op jit(solution)/shard_map/ppermute | solution.py:38
  25.5 3.8 %shard_map.96 = (bf16[960,384]{1,0:T(8,128)(2,1)S(1)}, bf16[960,384]{1,0:T(8,128)(2,1)S(1)}, bf16[960,384]{1,0:T(8,128)(2,1)S(1)}, bf16[960,384]{1,0:T(8,128)(2,1)S(1)}) custom-call(s32[48]{0:T(128)S(1)} %collective-permute-done.1.next_ref, s32[1]{0:T(128)S(6)} %copy.11.pattern_ref, bf16[384,384]{1,0:T(8,128)(2,1)S(1)} %bitcast.20, ...), custom_call_target="tpu_custom_call" | custom-call | flops 1132462080 | bytes 2359296 | tf_op jit(solution)/shard_map/pallas_call | solution.py:395
  29.3 0.1 collective-permute-start.5
  29.4 2.7 %collective-permute-start.6 = (bf16[960,384]{1,0:T(8,128)(2,1)S(1)}, bf16[960,384]{1,0:T(8,128)(2,1)S(1)}, u32[]{:S(2)}, u32[]{:S(2)}) collective-permute-start(bf16[960,384]{1,0:T(8,128)(2,1)S(1)} %get-tuple-element.16), channel_id=1, source_target_pairs={{0,7},{1,0},{2,1},{3,2},{4,3},{5,4},{6,5},{7,6},{8,15},{9,8},{10,9... | collective-permute-start | bytes 2211848 | tf_op jit(solution)/shard_map/ppermute | solution.py:38
  32.1 0.0 collective-permute-start.3
  32.1 2.7 %collective-permute-start.4 = (bf16[960,384]{1,0:T(8,128)(2,1)S(1)}, bf16[960,384]{1,0:T(8,128)(2,1)S(1)}, u32[]{:S(2)}, u32[]{:S(2)}) collective-permute-start(bf16[960,384]{1,0:T(8,128)(2,1)S(1)} %get-tuple-element.13), channel_id=1, source_target_pairs={{0,7},{1,0},{2,1},{3,2},{4,3},{5,4},{6,5},{7,6},{8,15},{9,8},{10,9... | collective-permute-start | bytes 2211848 | tf_op jit(solution)/shard_map/ppermute | solution.py:38
  34.7 0.0 collective-permute-start
  34.8 34.2 %collective-permute-done.vd_next_ref = bf16[384,384]{1,0:T(8,128)(2,1)S(1)} collective-permute-done((bf16[384,384]{1,0:T(8,128)(2,1)S(1)}, bf16[384,384]{1,0:T(8,128)(2,1)S(1)}, u32[]{:S(2)}, u32[]{:S(2)}) %collective-permute-start) | collective-permute-done | bytes 294944 | tf_op jit(solution)/shard_map/ppermute | solution.py:38
  68.9 10.7 %shard_map.93 = (f32[960,384]{1,0:T(8,128)S(1)}, f32[960,384]{1,0:T(8,128)S(1)}) custom-call(s32[48]{0:T(128)S(1)} %bitcast.29, s32[1]{0:T(128)S(6)} %copy.11.pattern_ref, bf16[384,384]{1,0:T(8,128)(2,1)} %bitcast.15, bf16[384,384]{1,0:T(8,128)(2,1)} %bitcast.23, bf16[384,384]{1,0:T(8,128)(2,1)S(1)} %collective-permute-done.vd_next_ref, ...), custom_call_target="tpu_custom_call" | custom-call | flops 2831155200 | bytes 2359296 | tf_op jit(solution)/shard_map/pallas_call | solution.py:414
  79.6 0.0 collective-permute-done.5.before_hbm
  79.6 0.0 copy-start.12
  79.6 0.0 collective-permute-done.6.after_hbm
  79.6 0.0 copy-start.13
  79.6 0.8 copy-done.12
  80.5 0.3 copy-done.13
  80.8 2.7 %shard_map.97.refs_0_ = bf16[960,384]{1,0:T(8,128)(2,1)S(1)} custom-call(s32[1]{0:T(128)S(6)} %copy.11.pattern_ref, f32[960,384]{1,0:T(8,128)S(1)} %get-tuple-element.14.local_ref, bf16[960,384]{1,0:T(8,128)(2,1)} %copy-done.12, bf16[960,384]{1,0:T(8,128)(2,1)} %copy-done.13, bf16[384,384]{1,0:T(8,128)(2,1)} %bitcast.16), custom_call_target="tpu_custom_call" | custom-call | flops 283115520 | bytes 2359296 | tf_op jit(solution)/shard_map/pallas_call | solution.py:436
  83.4 0.0 collective-permute-done.3.before_hbm
  83.4 0.0 copy-start.10
  83.4 0.0 collective-permute-done.4.after_hbm
  83.5 0.0 copy-start.11
  83.5 0.8 copy-done.10
  84.3 0.2 copy-done.11
  84.5 3.8 %shard_map.98 = bf16[2048,384]{1,0:T(8,128)(2,1)} custom-call(s32[1]{0:T(128)S(6)} %copy.11.pattern_ref, f32[960,384]{1,0:T(8,128)S(1)} %get-tuple-element.11.local_ref, bf16[960,384]{1,0:T(8,128)(2,1)} %copy-done.10, bf16[960,384]{1,0:T(8,128)(2,1)} %copy-done.11, bf16[384,384]{1,0:T(8,128)(2,1)} %bitcast.17, bf16[960,384]{1,0:T(8,128)(2,1)S(1)} %shard_map.97.refs_0_), custom_call_target="tpu_custom_call" | custom-call | flops 283115520 | bytes 2359296 | tf_op jit(solution)/shard_map/pallas_call | solution.py:436
  88.4 0.0 all-to-all-done.got_ref
  88.4 0.0 copy-start.1
  88.4 0.0 copy-start.5
  88.4 1.1 copy-done.1
  89.6 8.8 %all-to-all-start.1 = ((bf16[32,8,8,384]{3,2,1,0:T(8,128)(2,1)}), bf16[32,8,8,384]{3,2,1,0:T(8,128)(2,1)}, u32[]{:S(2)}, u32[]{:S(2)}) async-start(bf16[32,8,8,384]{3,2,1,0:T(8,128)(2,1)} %bitcast.6), calls=%async_computation.1 | async-start | bytes 3145728 | tf_op jit(solution)/shard_map/all_to_all | solution.py:42
  98.4 0.0 copy-done.5
  98.4 0.0 copy-start.2
  98.4 1.4 copy-done.2
  99.8 0.0 copy-start.7
  99.8 0.7 shard_map.92.green_ref
  100.5 20.6 %all-to-all-done.1.got_ref = bf16[32,8,8,384]{3,2,1,0:T(8,128)(2,1)} async-done(((bf16[32,8,8,384]{3,2,1,0:T(8,128)(2,1)}), bf16[32,8,8,384]{3,2,1,0:T(8,128)(2,1)}, u32[]{:S(2)}, u32[]{:S(2)}) %all-to-all-start.1) | async-done | bytes 1572896 | tf_op jit(solution)/shard_map/all_to_all | solution.py:42
  121.1 0.0 copy-done.7
  121.1 3.8 %shard_map.99 = bf16[32,8,8,384]{3,2,1,0:T(8,128)(2,1)S(1)} custom-call(bf16[256,256]{1,0:T(8,128)(2,1)S(1)} %copy-done.5, bf16[256,256]{1,0:T(8,128)(2,1)S(1)} %copy-done.7, f32[8,256,384]{2,1,0:T(8,128)S(1)} %shard_map.92.green_ref, bf16[32,8,8,384]{3,2,1,0:T(8,128)(2,1)} %all-to-all-done.1.got_ref), custom_call_target="tpu_custom_call" | custom-call | flops 566231040 | bytes 2359296 | tf_op jit(solution)/shard_map/pallas_call | solution.py:452
  125.0 26.4 %all_to_all.15 = bf16[32,8,8,384]{3,2,1,0:T(8,128)(2,1)S(1)} all-to-all(bf16[32,8,8,384]{3,2,1,0:T(8,128)(2,1)S(1)} %shard_map.99), channel_id=1, replica_groups=mesh['energy'=32,'space'=8] {'energy'}, dimensions={0} | all-to-all | bytes 3145728 | tf_op jit(solution)/shard_map/all_to_all | solution.py:42
  151.4 2.7 %shard_map.100 = bf16[8,384,384]{2,1,0:T(8,128)(2,1)} custom-call(s32[48]{0:T(128)S(1)} %bitcast.30, bf16[2048,384]{1,0:T(8,128)(2,1)S(1)} %bitcast.14), custom_call_target="tpu_custom_call" | custom-call | flops 169869312 | bytes 2359296 | tf_op jit(solution)/shard_map/pallas_call | solution.py:457
Async XLA Ops:
  0.0 0.7 copy-start.8
  4.9 9.4 %copy-start.3 = (bf16[1,384,384]{2,1,0:T(8,128)(2,1)S(1)}, bf16[1,384,384]{2,1,0:T(8,128)(2,1)}, u32[]{:S(2)}) copy-start(bf16[1,384,384]{2,1,0:T(8,128)(2,1)} %param.13) | copy-start | bytes 884740
  4.9 9.4 %copy-start.9 = (s32[1,48]{1,0:T(1,128)S(1)}, s32[1,48]{1,0:T(1,128)}, u32[]{:S(2)}) copy-start(s32[1,48]{1,0:T(1,128)} %param.15) | copy-start | bytes 580
  5.0 83.4 %all-to-all-start = ((bf16[32,8,8,384]{3,2,1,0:T(8,128)(2,1)}), bf16[32,8,8,384]{3,2,1,0:T(8,128)(2,1)S(1)}, u32[]{:S(2)}, u32[]{:S(2)}) async-start(bf16[32,8,8,384]{3,2,1,0:T(8,128)(2,1)} %shard_map.91), calls=%async_computation | async-start | bytes 3145728 | tf_op jit(solution)/shard_map/all_to_all | solution.py:42
  14.4 6.5 %copy-start = (bf16[2,4,1,384,384]{4,3,2,1,0:T(8,128)(2,1)S(1)}, bf16[2,4,1,384,384]{4,3,2,1,0:T(8,128)(2,1)}, u32[]{:S(2)}) copy-start(bf16[2,4,1,384,384]{4,3,2,1,0:T(8,128)(2,1)} %param.11) | copy-start | bytes 7077892
  14.4 6.5 %copy-start.4 = (bf16[2,4,1,384,384]{4,3,2,1,0:T(8,128)(2,1)S(1)}, bf16[2,4,1,384,384]{4,3,2,1,0:T(8,128)(2,1)}, u32[]{:S(2)}) copy-start(bf16[2,4,1,384,384]{4,3,2,1,0:T(8,128)(2,1)} %param.10) | copy-start | bytes 7077892
  14.4 6.5 %copy-start.6 = (bf16[1,384,384]{2,1,0:T(8,128)(2,1)S(1)}, bf16[1,384,384]{2,1,0:T(8,128)(2,1)}, u32[]{:S(2)}) copy-start(bf16[1,384,384]{2,1,0:T(8,128)(2,1)} %param.12) | copy-start | bytes 884740
  15.1 10.4 %collective-permute-start.2 = (bf16[240,384]{1,0:T(8,128)(2,1)S(1)}, bf16[240,384]{1,0:T(8,128)(2,1)S(1)}, u32[]{:S(2)}, u32[]{:S(2)}) collective-permute-start(bf16[240,384]{1,0:T(8,128)(2,1)S(1)} %shard_map.94), channel_id=1, source_target_pairs={{0,1},{1,2},{2,3},{3,4},{4,5},{5,6},{6,7},{7,0},{8,9},{9,10},{10,1... | collective-permute-start | bytes 552968 | tf_op jit(solution)/shard_map/ppermute | solution.py:38
  16.2 7.3 %collective-permute-start.1 = (s32[48]{0:T(128)S(1)}, s32[48]{0:T(128)S(1)}, u32[]{:S(2)}, u32[]{:S(2)}) collective-permute-start(s32[48]{0:T(128)S(1)} %bitcast.28), channel_id=1, source_target_pairs={{0,7},{1,0},{2,1},{3,2},{4,3},{5,4},{6,5},{7,6},{8,15},{9,8},{10,9... | collective-permute-start | bytes 584 | tf_op jit(solution)/shard_map/ppermute | solution.py:38
  29.3 50.3 %collective-permute-start.5 = (bf16[960,384]{1,0:T(8,128)(2,1)S(1)}, bf16[960,384]{1,0:T(8,128)(2,1)S(1)}, u32[]{:S(2)}, u32[]{:S(2)}) collective-permute-start(bf16[960,384]{1,0:T(8,128)(2,1)S(1)} %get-tuple-element.15), channel_id=1, source_target_pairs={{0,1},{1,2},{2,3},{3,4},{4,5},{5,6},{6,7},{7,0},{8,9},{9,10},{10,1... | collective-permute-start | bytes 2211848 | tf_op jit(solution)/shard_map/ppermute | solution.py:38
  29.4 50.2 %collective-permute-start.6 = (bf16[960,384]{1,0:T(8,128)(2,1)S(1)}, bf16[960,384]{1,0:T(8,128)(2,1)S(1)}, u32[]{:S(2)}, u32[]{:S(2)}) collective-permute-start(bf16[960,384]{1,0:T(8,128)(2,1)S(1)} %get-tuple-element.16), channel_id=1, source_target_pairs={{0,7},{1,0},{2,1},{3,2},{4,3},{5,4},{6,5},{7,6},{8,15},{9,8},{10,9... | collective-permute-start | bytes 2211848 | tf_op jit(solution)/shard_map/ppermute | solution.py:38
  32.1 51.4 %collective-permute-start.3 = (bf16[960,384]{1,0:T(8,128)(2,1)S(1)}, bf16[960,384]{1,0:T(8,128)(2,1)S(1)}, u32[]{:S(2)}, u32[]{:S(2)}) collective-permute-start(bf16[960,384]{1,0:T(8,128)(2,1)S(1)} %get-tuple-element.12), channel_id=1, source_target_pairs={{0,1},{1,2},{2,3},{3,4},{4,5},{5,6},{6,7},{7,0},{8,9},{9,10},{10,1... | collective-permute-start | bytes 2211848 | tf_op jit(solution)/shard_map/ppermute | solution.py:38
  32.1 51.4 %collective-permute-start.4 = (bf16[960,384]{1,0:T(8,128)(2,1)S(1)}, bf16[960,384]{1,0:T(8,128)(2,1)S(1)}, u32[]{:S(2)}, u32[]{:S(2)}) collective-permute-start(bf16[960,384]{1,0:T(8,128)(2,1)S(1)} %get-tuple-element.13), channel_id=1, source_target_pairs={{0,7},{1,0},{2,1},{3,2},{4,3},{5,4},{6,5},{7,6},{8,15},{9,8},{10,9... | collective-permute-start | bytes 2211848 | tf_op jit(solution)/shard_map/ppermute | solution.py:38
  34.7 34.2 %collective-permute-start = (bf16[384,384]{1,0:T(8,128)(2,1)S(1)}, bf16[384,384]{1,0:T(8,128)(2,1)S(1)}, u32[]{:S(2)}, u32[]{:S(2)}) collective-permute-start(bf16[384,384]{1,0:T(8,128)(2,1)S(1)} %bitcast.25), channel_id=1, source_target_pairs={{0,7},{1,0},{2,1},{3,2},{4,3},{5,4},{6,5},{7,6},{8,15},{9,8},{10,9... | collective-permute-start | bytes 884744 | tf_op jit(solution)/shard_map/ppermute | solution.py:38
  79.6 0.9 copy-start.12
  79.6 1.1 copy-start.13
  83.4 0.9 copy-start.10
  83.5 1.1 copy-start.11
  88.4 1.1 copy-start.1
  88.4 10.0 %copy-start.5 = (bf16[256,256]{1,0:T(8,128)(2,1)S(1)}, bf16[256,256]{1,0:T(8,128)(2,1)}, u32[]{:S(2)}) copy-start(bf16[256,256]{1,0:T(8,128)(2,1)} %constant.4.clone.forward_ref) | copy-start | bytes 393220
  89.6 31.6 %all-to-all-start.1 = ((bf16[32,8,8,384]{3,2,1,0:T(8,128)(2,1)}), bf16[32,8,8,384]{3,2,1,0:T(8,128)(2,1)}, u32[]{:S(2)}, u32[]{:S(2)}) async-start(bf16[32,8,8,384]{3,2,1,0:T(8,128)(2,1)} %bitcast.6), calls=%async_computation.1 | async-start | bytes 3145728 | tf_op jit(solution)/shard_map/all_to_all | solution.py:42
  98.4 1.4 copy-start.2
  99.8 21.3 %copy-start.7 = (bf16[256,256]{1,0:T(8,128)(2,1)S(1)}, bf16[256,256]{1,0:T(8,128)(2,1)}, u32[]{:S(2)}) copy-start(bf16[256,256]{1,0:T(8,128)(2,1)} %constant.5.clone.inverse_ref) | copy-start | bytes 393220

commit v4 on v3

--- a/solution.py
+++ b/solution.py
@@ -14,7 +14,6 @@
 RG = 8
 LANES = 128
 ROWS = (8,)
-PARTS = (0, 120, 240)
 
 F32 = jnp.float32
 BF16 = jnp.bfloat16
@@ -114,22 +113,15 @@
         start += LIVE * rows
 
 
-def pack_kernel(present_ref, g_ref, out_ref, idx_ref, turn_ref, held_ref, sem):
+def pack_kernel(present_ref, g_ref, out_ref, idx_ref, turn_ref):
     planes = g_ref.shape[0]
     live_list(present_ref, idx_ref)
     firsts = np.concatenate([[0], np.cumsum(ROWS)])
-    copies = []
-    for slot in range(LIVE):
-        row = pl.multiple_of(idx_ref[slot] * RG, RG)
-        copies.append(
-            pltpu.make_async_copy(g_ref.at[:, pl.ds(row, RG), :], held_ref.at[slot], sem.at[slot])
-        )
-        copies[-1].start()
     for slot in range(LIVE):
         turn = turn_ref.at[slot % turn_ref.shape[0]]
-        copies[slot].wait()
+        row = pl.multiple_of(idx_ref[slot] * RG, RG)
         for plane in range(planes):
-            spread(turn, plane, planes, held_ref[slot, plane].astype(F32))
+            spread(turn, plane, planes, g_ref[plane, pl.ds(row, RG), :].astype(F32))
         value = joined(turn).astype(BF16)
         for r in range(RG):
             chunk, peer, inner = place(slot * RG + r)
@@ -154,31 +146,48 @@
     out_ref[...] = picked[...].astype(BF16)
 
 
-def outward_kernel(next_ref, pattern_ref, vu_ref, left_ref, pu_ref, inner_ref, *refs):
-    chunks = len(PARTS) - 1
-    to_next, to_prev = refs[:chunks], refs[chunks : 2 * chunks]
-    idx_next, wide, picked, total_next, total_prev = refs[2 * chunks :]
+def outward_kernel(
+    next_ref, pattern_ref, vu_ref, left_ref, pu_ref, inner_ref, to_next, to_prev, idx, wide, picked, ready, sem
+):
     planes = pu_ref.shape[0]
-    live_list(next_ref, idx_next)
+    live_list(next_ref, idx)
     wide[...] = (vu_ref[...].astype(F32) * pattern_ref[0].astype(F32)).T
-    pick_rows(idx_next, wide, picked)
+    pick_rows(idx, wide, picked)
     left_next = picked[...].astype(BF16)
     left_prev = left_ref[...]
+    copies = []
     for plane in range(planes):
-        spread(total_prev, plane, planes, dot(left_prev, inner_ref[plane]))
-        spread(total_next, plane, planes, dot(left_next, pu_ref[plane]))
-    for chunk in range(chunks):
-        rows = slice(PARTS[chunk] * planes, PARTS[chunk + 1] * planes)
-        to_next[chunk][...] = joined(total_next.at[:, rows]).astype(BF16)
-        to_prev[chunk][...] = joined(total_prev.at[:, rows]).astype(BF16)
-
-
-def local_kernel(present_ref, pattern_ref, vu_hbm, vd_hbm, vd_next_ref, pd_hbm, pu_hbm, *refs):
-    outs = refs[: len(PARTS) - 1]
-    idx_ref, wide, picked_u, picked_d, same, one_up, bare, pd_ref, pu_ref, vd_ref, vu_ref, sem, v_sem = refs[
-        len(outs) :
-    ]
+        ready[0, plane] = dot(left_prev, inner_ref[plane]).astype(BF16)
+        copies += fetch([ready.at[0, plane]], [to_prev.at[plane]], [sem.at[0, plane]])
+        ready[1, plane] = dot(left_next, pu_ref[plane]).astype(BF16)
+        copies += fetch([ready.at[1, plane]], [to_next.at[plane]], [sem.at[1, plane]])
+    arrive(copies)
+
+
+def local_kernel(
+    present_ref,
+    pattern_ref,
+    vu_hbm,
+    vd_hbm,
+    vd_next_ref,
+    pd_hbm,
+    pu_hbm,
+    out_ref,
+    idx_ref,
+    wide,
+    picked_u,
+    picked_d,
+    same,
+    one_up,
+    pd_ref,
+    pu_ref,
+    vd_ref,
+    vu_ref,
+    sem,
+    v_sem,
+):
     planes = pu_ref.shape[0]
+    rows = LIVE * RG
     small = fetch([vd_hbm, vu_hbm], [vd_ref, vu_ref], [v_sem.at[0], v_sem.at[1]])
     copies = [
         fetch(
@@ -190,61 +199,47 @@
     ]
     live_list(present_ref, idx_ref)
     arrive(small)
-    scale = pattern_ref[0].astype(F32)
-    wide[...] = vu_ref[...].astype(F32) * scale
+    wide[...] = vu_ref[...].astype(F32) * pattern_ref[0].astype(F32)
     masked = wide[...].astype(BF16)
     pick_rows(idx_ref, wide, picked_u)
     wide[...] = vd_ref[...].astype(F32)
     pick_rows(idx_ref, wide, picked_d)
     left_u = picked_u[...].astype(BF16)
     left_d = picked_d[...].astype(BF16)
-    nothing = jnp.zeros(picked_u.shape, F32)
     for plane in range(planes):
         arrive(copies[plane])
-        spread(same, plane, planes, dot(left_d, pd_ref[plane]) + dot_nt(left_u, pu_ref[plane]))
-        spread(one_up, plane, planes, dot(left_d, pu_ref[plane]))
-        spread(bare, plane, planes, picked_u[...] if plane < planes // 2 else nothing)
-    for part, out_ref in enumerate(outs):
-        start, end = PARTS[part] * planes, PARTS[part + 1] * planes
-        out_ref[...] = (
-            joined(bare.at[:, start:end])
-            + dot(joined(same.at[:, start:end]).astype(BF16), masked)
-            + dot(joined(one_up.at[:, start:end]).astype(BF16), vd_next_ref[...])
+        at = slice(plane * rows, (plane + 1) * rows)
+        same[at] = (dot(left_d, pd_ref[plane]) + dot_nt(left_u, pu_ref[plane])).astype(BF16)
+        one_up[at] = dot(left_d, pu_ref[plane]).astype(BF16)
+    for plane in range(planes):
+        at = slice(plane * rows, (plane + 1) * rows)
+        value = dot(same[at], masked) + dot(one_up[at], vd_next_ref[...])
+        if plane < planes // 2:
+            value = value + picked_u[...]
+        out_ref[plane] = value.astype(BF16)
+
+
+def join_kernel(pattern_ref, local_ref, before_hbm, after_hbm, vu_hbm, out_ref, before, after, vu_ref, total, sem, v_sem):
+    planes, rows, cols = local_ref.shape
+    size = planes * rows
+    scale = pattern_ref[0].astype(F32)
+    small = fetch([vu_hbm], [vu_ref], [v_sem.at[0]])
+    copies = [
+        fetch(
+            [before_hbm.at[plane], after_hbm.at[plane]],
+            [before.at[plane], after.at[plane]],
+            [sem.at[0, plane], sem.at[1, plane]],
         )
-
-
-def join_kernel(part, pattern_ref, local_ref, before_hbm, after_hbm, vu_hbm, *refs):
-    done_ref = refs[0] if part else None
-    out_ref, before, after, vu_ref, sem, v_sem = refs[1 if part else 0 :]
-    scale = pattern_ref[0].astype(F32)
-    size = local_ref.shape[0]
-    parts = sem.shape[1]
-    step = size // parts
-    small = fetch([vu_hbm], [vu_ref], [v_sem.at[0]])
-    copies = []
-    for at in range(parts):
-        rows = slice(at * step, (at + 1) * step)
-        copies.append(
-            fetch(
-                [before_hbm.at[rows], after_hbm.at[rows]],
-                [before.at[rows], after.at[rows]],
-                [sem.at[0, at], sem.at[1, at]],
-            )
-        )
-    first = 0
-    if part:
-        first = done_ref.shape[0]
-        out_ref[:first, :] = done_ref[...]
-        tail = out_ref.shape[0] - first - size
-        out_ref[first + size :, :] = jnp.zeros((tail, out_ref.shape[1]), BF16)
+        for plane in range(planes)
+    ]
+    out_ref[size:, :] = jnp.zeros((out_ref.shape[0] - size, cols), BF16)
     arrive(small)
     masked = (vu_ref[...].astype(F32) * scale).astype(BF16)
-    for at in range(parts):
-        rows = slice(at * step, (at + 1) * step)
-        arrive(copies[at])
-        out_ref[first + at * step : first + (at + 1) * step, :] = (
-            local_ref[rows, :] + dot(before[rows], masked) + after[rows].astype(F32) * scale
-        ).astype(BF16)
+    for plane in range(planes):
+        arrive(copies[plane])
+        value = dot(before[plane], masked) + after[plane].astype(F32) * scale
+        spread(total, plane, planes, value + local_ref[plane].astype(F32))
+    out_ref[:size, :] = joined(total).astype(BF16)
 
 
 def spectrum_kernel(scale, forward_ref, got_ref, *outs):
@@ -336,19 +331,20 @@
     energies = local * peers
     live = LIVE * RG
     flat = live * planes
-    sizes = [(end - start) * planes for start, end in zip(PARTS[:-1], PARTS[1:])]
 
     def stay(value):
         return pltpu.with_memory_space_constraint(value, pltpu.HBM)
 
-    green, p_d, p_u = (stay(x.reshape(planes, size, size)) for x in (g_upper, p_diag, p_upper))
+    p_d, p_u = (stay(x.reshape(planes, size, size)) for x in (p_diag, p_upper))
     v_d, v_u = (x.reshape(size, size) for x in (v_diag, v_upper))
     v_d_here, v_u_here = stay(v_d), stay(v_u)
 
     def near(value):
         return pltpu.with_memory_space_constraint(value, pltpu.VMEM)
 
-    p_d_near, p_u_near = near(p_diag.reshape(planes, size, size)), near(p_upper.reshape(planes, size, size))
+    p_d_near, p_u_near, green = (
+        near(x.reshape(planes, size, size)) for x in (p_diag, p_upper, g_upper)
+    )
     v_d_near, v_u_near = near(v_d), near(v_u)
     present = element_present.reshape(-1)
     groups = present.shape[0]
@@ -392,32 +388,33 @@
     inner = call(
         inner_kernel, array(planes, size, size), [smem()] + [vmem()] * 4, [], 3.2, 12
     )(v_pattern, v_d_near, v_u_near, p_d_near, p_u_near)
-    outward = call(
+    parcel = pltpu.VMEM((planes, live, size), BF16)
+    to_next, to_prev = call(
         outward_kernel,
-        [array(n, size) for n in sizes] * 2,
+        [array(planes, live, size)] * 2,
         [smem()] * 2 + [vmem()] * 4,
-        [idx, square, strip, total, total],
+        [idx, square, strip, pltpu.VMEM((2, planes, live, size), BF16), sems],
         2,
-        18,
+        10,
+        hbm,
     )(present_next, v_pattern, v_u_near, v_u_prev, p_u_near, inner)
-    chunks = len(sizes)
-    before = [shifted(piece, 1) for piece in outward[:chunks]]
-    after = [shifted(piece, -1) for piece in outward[chunks:]]
+    after = shifted(to_prev, -1)
+    before = shifted(to_next, 1)
 
     held = pltpu.VMEM((LIVE, planes, RG, size), BF16)
-    held_sem = pltpu.SemaphoreType.DMA((LIVE,))
     send_green = call(
-        pack_kernel, array(peers, RG, planes, size), [smem(), hbm()], [idx, turn, held, held_sem], 0.3, 8
+        pack_kernel, array(peers, RG, planes, size), [smem(), vmem()], [idx, turn], 0.3, 8
     )(present, green)
     got_green = routed(send_green)
 
+    stacked = pltpu.VMEM((flat, size), BF16)
     own = call(
         local_kernel,
-        [array(n, size, dtype=F32) for n in sizes],
+        array(planes, live, size),
         [smem()] * 2 + [hbm()] * 2 + [vmem()] + [hbm()] * 2,
-        [idx, square, strip, strip, total, total, total, whole, whole, block, block, sems, pair],
+        [idx, square, strip, strip, stacked, stacked, whole, whole, block, block, sems, pair],
         5,
-        22,
+        16,
     )(present, v_pattern, v_u_here, v_d_here, v_d_next, p_d, p_u)
 
     green_freq = call(
@@ -429,26 +426,15 @@
         8,
     )(forward, got_green)
 
-    joined_parts = []
-    for part, rows in enumerate(sizes):
-        last = part == len(sizes) - 1
-        joined_parts.append(
-            call(
-                functools.partial(join_kernel, part),
-                array(peers * RG * planes if last else rows, size),
-                [smem(), vmem()] + [hbm()] * 3 + [vmem()] * part,
-                [
-                    pltpu.VMEM((rows, size), BF16),
-                    pltpu.VMEM((rows, size), BF16),
-                    block,
-                    pltpu.SemaphoreType.DMA((2, 3)),
-                    pair,
-                ],
-                0.5,
-                8,
-            )(v_pattern, own[part], stay(before[part]), stay(after[part]), v_u_here, *joined_parts)
-        )
-    got = routed(joined_parts[-1].reshape(peers, RG, planes, size))
+    send = call(
+        join_kernel,
+        array(peers * RG * planes, size),
+        [smem(), vmem()] + [hbm()] * 3,
+        [parcel, parcel, block, total, sems, pair],
+        1,
+        12,
+    )(v_pattern, own, stay(before), stay(after), v_u_here)
+    got = routed(send.reshape(peers, RG, planes, size))
     result = call(
         convolve_kernel, array(peers, RG, planes, size), [vmem()] * 4, [], 1, 10
     )(forward, inverse, green_freq[0], got)

time: 155 us -> 140 us (0.903)
  waiting for transfers between devices: 56.8 us -> 46.9 us
  Pallas kernels: 35.8 us -> 33.3 us
  local copies, waits for them, and re-layouts: 5.42 us -> 3.52 us
    ppermute x7 -> x5, waiting for transfers between devices: 36.2 us -> 26.3 us  [shifted(): return lax.ppermute(value, 'space', pairs)]
    pallas_call x5 -> x4, Pallas kernels: 25.2 us -> 22.3 us  [the longest x1 10 us: per_device(): call(local_kernel, array(planes, live, size), [smem()] * 2 + [hbm()] * 2...]
    unnamed x28 -> x20, local copies, waits for them, and re-layouts: 5.42 us -> 3.52 us
    ppermute x7 -> x5, starting transfers between devices: 11.2 us -> 9.81 us  [shifted(): return lax.ppermute(value, 'space', pairs)]
  transfers between devices with their start and end apart: 9 -> 7, of which waited for: 3 -> 3; matrix products, arithmetic and copies ran while one was open for 0% -> 0% of each run, Pallas kernels for 16% -> 16%
where the time goes in v4:
time: 140 us; the launch traced here: 139 us
  waiting for transfers between devices  46.9 us (34%)
  Pallas kernels  33.3 us (24%)
  starting transfers between devices  28.2 us (20%)
  blocking collectives  26.4 us (19%)
  local copies, waits for them, and re-layouts  3.52 us (3%)
    all_to_all x1, blocking collectives, routed(): lax.all_to_all(value, 'energy', split_axis=0, concat_axis=0, tiled=True)  26.4 us
    ppermute x5, waiting for transfers between devices, shifted(): return lax.ppermute(value, 'space', pairs)  26.3 us
    all_to_all x2, waiting for transfers between devices, routed(): lax.all_to_all(value, 'energy', split_axis=0, concat_axis=0, tiled=True)  20.6 us
    all_to_all x2, starting transfers between devices, routed(): lax.all_to_all(value, 'energy', split_axis=0, concat_axis=0, tiled=True)  18.4 us
    pallas_call x1, Pallas kernels, per_device(): call(local_kernel, array(planes, live, size), [smem()] * 2 + [hbm()] * 2...  10 us
    ppermute x5, starting transfers between devices, shifted(): return lax.ppermute(value, 'space', pairs)  9.81 us
    pallas_call x1, Pallas kernels, per_device(): call(join_kernel, array(peers * RG * planes, size), [smem(), vmem()] + [h...  6.04 us
    pallas_call x1, Pallas kernels, per_device(): call(convolve_kernel, array(peers, RG, planes, size), [vmem()] * 4, [], 1...  3.81 us
  transfers between devices with their start and end apart: 7, of which 3 were waited for; matrix products, arithmetic and copies ran while one was open for 0% of the time, Pallas kernels for 16%

profile of v4, /device:TPU:1, one launch (start us, length us, event | category | flops | bytes accessed | tf_op | source)
XLA Modules:
  0.0 139.3 jit_solution(15810692606082268020)
XLA Ops:
  0.7 0.0 copy-start.3
  0.7 1.0 copy-done.3
  1.6 0.0 copy-start
  1.6 0.0 copy-start.4
  1.6 0.0 copy-start.6
  1.6 0.0 copy-start.8
  1.6 1.0 shard_map.94
  2.6 2.5 %collective-permute-start.2 = (bf16[240,384]{1,0:T(8,128)(2,1)S(1)}, bf16[240,384]{1,0:T(8,128)(2,1)S(1)}, u32[]{:S(2)}, u32[]{:S(2)}) collective-permute-start(bf16[240,384]{1,0:T(8,128)(2,1)S(1)} %shard_map.94), channel_id=1, source_target_pairs={{0,1},{1,2},{2,3},{3,4},{4,5},{5,6},{6,7},{7,0},{8,9},{9,10},{10,1... | collective-permute-start | bytes 552968 | tf_op jit(solution)/shard_map/ppermute | solution.py:37
  5.1 4.0 %collective-permute-start.1 = (s32[48]{0:T(128)}, s32[48]{0:T(128)S(1)}, u32[]{:S(2)}, u32[]{:S(2)}) collective-permute-start(s32[48]{0:T(128)} %bitcast.present_ref), channel_id=1, source_target_pairs={{0,7},{1,0},{2,1},{3,2},{4,3},{5,4},{6,5},{7,6},{8,15},{9,8},{10,9... | collective-permute-start | bytes 584 | tf_op jit(solution)/shard_map/ppermute | solution.py:37
  9.2 0.0 copy-done
  9.2 0.0 copy-done.4
  9.2 0.0 copy-done.6
  9.2 0.0 copy-done.8
  9.2 2.6 %shard_map.95.inner_ref = bf16[8,384,384]{2,1,0:T(8,128)(2,1)S(1)} custom-call(s32[1]{0:T(128)S(6)} %copy.11.pattern_ref, bf16[384,384]{1,0:T(8,128)(2,1)S(1)} %bitcast.24, bf16[384,384]{1,0:T(8,128)(2,1)S(1)} %bitcast.18, bf16[8,384,384]{2,1,0:T(8,128)(2,1)S(1)} %bitcast.22, bf16[8,384,384]{2,1,0:T(8,128)(2,1)S(1)} %bitcast.12), custom_call_target="tpu_custom_call" | custom-call | flops 1811939328 | bytes 2359296 | tf_op jit(solution)/shard_map/pallas_call | solution.py:388
  11.8 0.0 copy-start.5
  11.8 0.0 collective-permute-done.1.next_ref
  11.8 1.6 %collective-permute-done.2.left_ref = bf16[240,384]{1,0:T(8,128)(2,1)S(1)} collective-permute-done((bf16[240,384]{1,0:T(8,128)(2,1)S(1)}, bf16[240,384]{1,0:T(8,128)(2,1)S(1)}, u32[]{:S(2)}, u32[]{:S(2)}) %collective-permute-start.2) | collective-permute-done | bytes 184352 | tf_op jit(solution)/shard_map/ppermute | solution.py:37
  13.4 3.7 %shard_map.96 = (bf16[8,240,384]{2,1,0:T(8,128)(2,1)}, bf16[8,240,384]{2,1,0:T(8,128)(2,1)}) custom-call(s32[48]{0:T(128)S(1)} %collective-permute-done.1.next_ref, s32[1]{0:T(128)S(6)} %copy.11.pattern_ref, bf16[384,384]{1,0:T(8,128)(2,1)S(1)} %bitcast.19, bf16[240,384]{1,0:T(8,128)(2,1)S(1)} %collective-permute-done.2.left_ref, ...), custom_call_target="tpu_custom_call" | custom-call | flops 1132462080 | bytes 2359296 | tf_op jit(solution)/shard_map/pallas_call | solution.py:392
  17.1 0.1 collective-permute-start.3
  17.2 2.7 %collective-permute-start.4 = (bf16[8,240,384]{2,1,0:T(8,128)(2,1)}, bf16[8,240,384]{2,1,0:T(8,128)(2,1)}, u32[]{:S(2)}, u32[]{:S(2)}) collective-permute-start(bf16[8,240,384]{2,1,0:T(8,128)(2,1)} %get-tuple-element.8), channel_id=1, source_target_pairs={{0,7},{1,0},{2,1},{3,2},{4,3},{5,4},{6,5},{7,6},{8,15},{9,8},{10,9... | collective-permute-start | bytes 4423688 | tf_op jit(solution)/shard_map/ppermute | solution.py:37
  19.9 0.0 copy-done.5
  19.9 2.5 %shard_map.91 = bf16[32,8,8,384]{3,2,1,0:T(8,128)(2,1)} custom-call(s32[48]{0:T(128)} %bitcast.present_ref, bf16[8,384,384]{2,1,0:T(8,128)(2,1)S(1)} %bitcast.20), custom_call_target="tpu_custom_call" | custom-call | flops 169869312 | bytes 2359296 | tf_op jit(solution)/shard_map/pallas_call | solution.py:405
  22.4 8.9 %all-to-all-start = ((bf16[32,8,8,384]{3,2,1,0:T(8,128)(2,1)}), bf16[32,8,8,384]{3,2,1,0:T(8,128)(2,1)S(1)}, u32[]{:S(2)}, u32[]{:S(2)}) async-start(bf16[32,8,8,384]{3,2,1,0:T(8,128)(2,1)} %shard_map.91), calls=%async_computation | async-start | bytes 3145728 | tf_op jit(solution)/shard_map/all_to_all | solution.py:41
  31.3 0.5 collective-permute-start
  31.8 24.7 %collective-permute-done.vd_next_ref = bf16[384,384]{1,0:T(8,128)(2,1)S(1)} collective-permute-done((bf16[384,384]{1,0:T(8,128)(2,1)S(1)}, bf16[384,384]{1,0:T(8,128)(2,1)S(1)}, u32[]{:S(2)}, u32[]{:S(2)}) %collective-permute-start) | collective-permute-done | bytes 294944 | tf_op jit(solution)/shard_map/ppermute | solution.py:37
  56.5 10.0 %shard_map.93.local_ref = bf16[8,240,384]{2,1,0:T(8,128)(2,1)S(1)} custom-call(s32[48]{0:T(128)} %bitcast.present_ref, s32[1]{0:T(128)S(6)} %copy.11.pattern_ref, bf16[384,384]{1,0:T(8,128)(2,1)} %bitcast.15, bf16[384,384]{1,0:T(8,128)(2,1)} %bitcast.23, bf16[384,384]{1,0:T(8,128)(2,1)S(1)} %collective-permute-done.vd_next_ref, ...), custom_call_target="tpu_custom_call" | custom-call | flops 2831155200 | bytes 2359296 | tf_op jit(solution)/shard_map/pallas_call | solution.py:411
  66.6 0.0 collective-permute-done.3.before_hbm
  66.6 0.0 collective-permute-done.4.after_hbm
  66.6 6.0 %shard_map.97 = bf16[2048,384]{1,0:T(8,128)(2,1)} custom-call(s32[1]{0:T(128)S(6)} %copy.11.pattern_ref, bf16[8,240,384]{2,1,0:T(8,128)(2,1)S(1)} %shard_map.93.local_ref, bf16[8,240,384]{2,1,0:T(8,128)(2,1)} %collective-permute-done.3.before_hbm, bf16[8,240,384]{2,1,0:T(8,128)(2,1)} %collective-permute-done.4.after_hbm, bf16[384,384]{1,0:T(8,128)(2,1)} %bitcast.16), custom_call_target="tpu_custom_call" | custom-call | flops 566231040 | bytes 2359296 | tf_op jit(solution)/shard_map/pallas_call | solution.py:429
  72.7 0.0 all-to-all-done.got_ref
  72.7 0.0 copy-start.1
  72.7 0.0 copy-start.7
  72.7 1.1 copy-done.1
  73.8 9.5 %all-to-all-start.1 = ((bf16[32,8,8,384]{3,2,1,0:T(8,128)(2,1)}), bf16[32,8,8,384]{3,2,1,0:T(8,128)(2,1)}, u32[]{:S(2)}, u32[]{:S(2)}) async-start(bf16[32,8,8,384]{3,2,1,0:T(8,128)(2,1)} %bitcast.6), calls=%async_computation.1 | async-start | bytes 3145728 | tf_op jit(solution)/shard_map/all_to_all | solution.py:41
  83.4 0.0 copy-done.7
  83.4 0.0 copy-start.2
  83.4 1.4 %copy-done.2 = bf16[32,8,8,384]{3,2,1,0:T(8,128)(2,1)S(1)} copy-done((bf16[32,8,8,384]{3,2,1,0:T(8,128)(2,1)S(1)}, bf16[32,8,8,384]{3,2,1,0:T(8,128)(2,1)}, u32[]{:S(2)}) %copy-start.2) | copy-done | bytes 1572888
  84.8 0.0 copy-start.9
  84.8 0.7 shard_map.92.green_ref
  85.5 20.6 %all-to-all-done.1.got_ref = bf16[32,8,8,384]{3,2,1,0:T(8,128)(2,1)} async-done(((bf16[32,8,8,384]{3,2,1,0:T(8,128)(2,1)}), bf16[32,8,8,384]{3,2,1,0:T(8,128)(2,1)}, u32[]{:S(2)}, u32[]{:S(2)}) %all-to-all-start.1) | async-done | bytes 1572896 | tf_op jit(solution)/shard_map/all_to_all | solution.py:41
  106.1 0.0 copy-done.9
  106.1 3.8 %shard_map.98 = bf16[32,8,8,384]{3,2,1,0:T(8,128)(2,1)S(1)} custom-call(bf16[256,256]{1,0:T(8,128)(2,1)S(1)} %copy-done.7, bf16[256,256]{1,0:T(8,128)(2,1)S(1)} %copy-done.9, f32[8,256,384]{2,1,0:T(8,128)S(1)} %shard_map.92.green_ref, bf16[32,8,8,384]{3,2,1,0:T(8,128)(2,1)} %all-to-all-done.1.got_ref), custom_call_target="tpu_custom_call" | custom-call | flops 566231040 | bytes 2359296 | tf_op jit(solution)/shard_map/pallas_call | solution.py:438
  109.9 26.4 %all_to_all.15 = bf16[32,8,8,384]{3,2,1,0:T(8,128)(2,1)S(1)} all-to-all(bf16[32,8,8,384]{3,2,1,0:T(8,128)(2,1)S(1)} %shard_map.98), channel_id=1, replica_groups=mesh['energy'=32,'space'=8] {'energy'}, dimensions={0} | all-to-all | bytes 3145728 | tf_op jit(solution)/shard_map/all_to_all | solution.py:41
  136.3 2.8 %shard_map.99 = bf16[8,384,384]{2,1,0:T(8,128)(2,1)} custom-call(s32[48]{0:T(128)} %bitcast.present_ref, bf16[2048,384]{1,0:T(8,128)(2,1)S(1)} %bitcast.14), custom_call_target="tpu_custom_call" | custom-call | flops 169869312 | bytes 2359296 | tf_op jit(solution)/shard_map/pallas_call | solution.py:443
Async XLA Ops:
  0.7 1.0 copy-start.3
  1.6 7.6 %copy-start = (bf16[2,4,1,384,384]{4,3,2,1,0:T(8,128)(2,1)S(1)}, bf16[2,4,1,384,384]{4,3,2,1,0:T(8,128)(2,1)}, u32[]{:S(2)}) copy-start(bf16[2,4,1,384,384]{4,3,2,1,0:T(8,128)(2,1)} %param.11) | copy-start | bytes 7077892
  1.6 7.6 %copy-start.4 = (bf16[1,384,384]{2,1,0:T(8,128)(2,1)S(1)}, bf16[1,384,384]{2,1,0:T(8,128)(2,1)}, u32[]{:S(2)}) copy-start(bf16[1,384,384]{2,1,0:T(8,128)(2,1)} %param.13) | copy-start | bytes 884740
  1.6 7.6 %copy-start.6 = (bf16[2,4,1,384,384]{4,3,2,1,0:T(8,128)(2,1)S(1)}, bf16[2,4,1,384,384]{4,3,2,1,0:T(8,128)(2,1)}, u32[]{:S(2)}) copy-start(bf16[2,4,1,384,384]{4,3,2,1,0:T(8,128)(2,1)} %param.10) | copy-start | bytes 7077892
  1.6 7.6 %copy-start.8 = (bf16[1,384,384]{2,1,0:T(8,128)(2,1)S(1)}, bf16[1,384,384]{2,1,0:T(8,128)(2,1)}, u32[]{:S(2)}) copy-start(bf16[1,384,384]{2,1,0:T(8,128)(2,1)} %param.12) | copy-start | bytes 884740
  2.6 10.8 %collective-permute-start.2 = (bf16[240,384]{1,0:T(8,128)(2,1)S(1)}, bf16[240,384]{1,0:T(8,128)(2,1)S(1)}, u32[]{:S(2)}, u32[]{:S(2)}) collective-permute-start(bf16[240,384]{1,0:T(8,128)(2,1)S(1)} %shard_map.94), channel_id=1, source_target_pairs={{0,1},{1,2},{2,3},{3,4},{4,5},{5,6},{6,7},{7,0},{8,9},{9,10},{10,1... | collective-permute-start | bytes 552968 | tf_op jit(solution)/shard_map/ppermute | solution.py:37
  5.1 6.7 %collective-permute-start.1 = (s32[48]{0:T(128)}, s32[48]{0:T(128)S(1)}, u32[]{:S(2)}, u32[]{:S(2)}) collective-permute-start(s32[48]{0:T(128)} %bitcast.present_ref), channel_id=1, source_target_pairs={{0,7},{1,0},{2,1},{3,2},{4,3},{5,4},{6,5},{7,6},{8,15},{9,8},{10,9... | collective-permute-start | bytes 584 | tf_op jit(solution)/shard_map/ppermute | solution.py:37
  11.8 8.1 %copy-start.5 = (bf16[2,4,1,384,384]{4,3,2,1,0:T(8,128)(2,1)S(1)}, bf16[2,4,1,384,384]{4,3,2,1,0:T(8,128)(2,1)}, u32[]{:S(2)}) copy-start(bf16[2,4,1,384,384]{4,3,2,1,0:T(8,128)(2,1)} %param.9) | copy-start | bytes 7077892
  17.1 49.5 %collective-permute-start.3 = (bf16[8,240,384]{2,1,0:T(8,128)(2,1)}, bf16[8,240,384]{2,1,0:T(8,128)(2,1)}, u32[]{:S(2)}, u32[]{:S(2)}) collective-permute-start(bf16[8,240,384]{2,1,0:T(8,128)(2,1)} %get-tuple-element.7), channel_id=1, source_target_pairs={{0,1},{1,2},{2,3},{3,4},{4,5},{5,6},{6,7},{7,0},{8,9},{9,10},{10,1... | collective-permute-start | bytes 4423688 | tf_op jit(solution)/shard_map/ppermute | solution.py:37
  17.2 49.4 %collective-permute-start.4 = (bf16[8,240,384]{2,1,0:T(8,128)(2,1)}, bf16[8,240,384]{2,1,0:T(8,128)(2,1)}, u32[]{:S(2)}, u32[]{:S(2)}) collective-permute-start(bf16[8,240,384]{2,1,0:T(8,128)(2,1)} %get-tuple-element.8), channel_id=1, source_target_pairs={{0,7},{1,0},{2,1},{3,2},{4,3},{5,4},{6,5},{7,6},{8,15},{9,8},{10,9... | collective-permute-start | bytes 4423688 | tf_op jit(solution)/shard_map/ppermute | solution.py:37
  22.4 50.2 %all-to-all-start = ((bf16[32,8,8,384]{3,2,1,0:T(8,128)(2,1)}), bf16[32,8,8,384]{3,2,1,0:T(8,128)(2,1)S(1)}, u32[]{:S(2)}, u32[]{:S(2)}) async-start(bf16[32,8,8,384]{3,2,1,0:T(8,128)(2,1)} %shard_map.91), calls=%async_computation | async-start | bytes 3145728 | tf_op jit(solution)/shard_map/all_to_all | solution.py:41
  31.3 25.2 %collective-permute-start = (bf16[384,384]{1,0:T(8,128)(2,1)S(1)}, bf16[384,384]{1,0:T(8,128)(2,1)S(1)}, u32[]{:S(2)}, u32[]{:S(2)}) collective-permute-start(bf16[384,384]{1,0:T(8,128)(2,1)S(1)} %bitcast.25), channel_id=1, source_target_pairs={{0,7},{1,0},{2,1},{3,2},{4,3},{5,4},{6,5},{7,6},{8,15},{9,8},{10,9... | collective-permute-start | bytes 884744 | tf_op jit(solution)/shard_map/ppermute | solution.py:37
  72.7 1.1 copy-start.1
  72.7 10.7 %copy-start.7 = (bf16[256,256]{1,0:T(8,128)(2,1)S(1)}, bf16[256,256]{1,0:T(8,128)(2,1)}, u32[]{:S(2)}) copy-start(bf16[256,256]{1,0:T(8,128)(2,1)} %constant.4.clone.forward_ref) | copy-start | bytes 393220
  73.8 32.3 %all-to-all-start.1 = ((bf16[32,8,8,384]{3,2,1,0:T(8,128)(2,1)}), bf16[32,8,8,384]{3,2,1,0:T(8,128)(2,1)}, u32[]{:S(2)}, u32[]{:S(2)}) async-start(bf16[32,8,8,384]{3,2,1,0:T(8,128)(2,1)} %bitcast.6), calls=%async_computation.1 | async-start | bytes 3145728 | tf_op jit(solution)/shard_map/all_to_all | solution.py:41
  83.4 1.4 %copy-start.2 = (bf16[32,8,8,384]{3,2,1,0:T(8,128)(2,1)S(1)}, bf16[32,8,8,384]{3,2,1,0:T(8,128)(2,1)}, u32[]{:S(2)}) copy-start(bf16[32,8,8,384]{3,2,1,0:T(8,128)(2,1)} %copy-done.1) | copy-start | bytes 4718596
  84.8 21.3 %copy-start.9 = (bf16[256,256]{1,0:T(8,128)(2,1)S(1)}, bf16[256,256]{1,0:T(8,128)(2,1)}, u32[]{:S(2)}) copy-start(bf16[256,256]{1,0:T(8,128)(2,1)} %constant.5.clone.inverse_ref) | copy-start | bytes 393220

commit v5 on v4

v5 whole, which is shorter than its diff:
```python
import functools
import math

import jax
import jax.numpy as jnp
import numpy as np
from jax import lax
from jax.experimental import pallas as pl
from jax.experimental.pallas import tpu as pltpu
from jax.sharding import PartitionSpec as P


LIVE = 30
RG = 8
LANES = 128

F32 = jnp.float32
BF16 = jnp.bfloat16


def smem():
    return pl.BlockSpec(memory_space=pltpu.SMEM)


def vmem():
    return pl.BlockSpec(memory_space=pltpu.VMEM)


def hbm():
    return pl.BlockSpec(memory_space=pltpu.HBM)


def shifted(value, steps):
    count = lax.axis_size("space")
    pairs = [(source, (source + steps) % count) for source in range(count)]
    return lax.ppermute(value, "space", pairs)


def routed(value):
    return lax.all_to_all(value, "energy", split_axis=0, concat_axis=0, tiled=True)


def dot(left, right):
    return lax.dot_general(left, right, (((1,), (0,)), ((), ())), preferred_element_type=F32)


def dot_nt(left, right):
    return lax.dot_general(left, right, (((1,), (1,)), ((), ())), preferred_element_type=F32)


def tables(energies, peers):
    local = energies // peers
    src, half, step = np.meshgrid(np.arange(peers), np.arange(2), np.arange(local), indexing="ij")
    time = (src * local + step).reshape(-1)
    half = half.reshape(-1)
    freq = np.arange(energies)
    angles = 2.0 * math.pi / energies * ((freq[:, None] * time[None, :]) % energies)
    cosine, sine = np.cos(angles), np.sin(angles)
    real_part = np.where(half == 0, cosine, sine)
    imag_part = np.where(half == 0, -sine, cosine)
    forward = np.concatenate([real_part, imag_part], 0)
    real_out = np.concatenate([-sine, -cosine], 0).T
    imag_out = np.concatenate([cosine, -sine], 0).T
    inverse = np.where((half == 0)[:, None], real_out, imag_out)
    return jnp.asarray(forward, BF16), jnp.asarray(inverse, BF16)


def fetch(sources, targets, sems):
    copies = [pltpu.make_async_copy(a, b, sem) for a, b, sem in zip(sources, targets, sems)]
    for copy in copies:
        copy.start()
    return copies


def arrive(copies):
    for copy in copies:
        copy.wait()


def spread(dest_ref, plane, planes, value):
    rows = value.shape[0]
    for j in range(value.shape[1] // LANES):
        dest_ref[j, pl.ds(plane, rows, stride=planes), :] = value[:, j * LANES : (j + 1) * LANES]


def live_list(present_ref, idx_ref):
    for slot in range(LIVE):
        idx_ref[slot] = 0
    count = jnp.int32(0)
    for group in range(present_ref.shape[0]):
        idx_ref[count] = group
        count = count + jnp.where(present_ref[group] > 0, 1, 0)
    return count


def pick_rows(idx_ref, source_ref, dest_ref):
    for slot in range(LIVE):
        row = pl.multiple_of(idx_ref[slot] * RG, RG)
        dest_ref[slot * RG : (slot + 1) * RG, :] = source_ref[pl.ds(row, RG), :]


def pack_kernel(present_ref, g_ref, out_hbm, idx_ref, turn_ref, ready, sem):
    planes = g_ref.shape[0]
    tiles = g_ref.shape[2] // LANES
    span = LIVE * RG * planes
    live_list(present_ref, idx_ref)
    copies = []
    for tile in range(tiles):
        cols = slice(tile * LANES, (tile + 1) * LANES)
        for slot in range(LIVE):
            turn = turn_ref.at[slot % turn_ref.shape[0]]
            row = pl.multiple_of(idx_ref[slot] * RG, RG)
            for plane in range(planes):
                turn[pl.ds(plane, RG, stride=planes), :] = g_ref[plane, pl.ds(row, RG), cols].astype(F32)
            at = tile * span + slot * RG * planes
            ready[at : at + RG * planes, :] = turn[...].astype(BF16)
        end = (tile + 1) * span
        if tile == tiles - 1:
            ready[end:, :] = jnp.zeros((ready.shape[0] - end, LANES), BF16)
            end = ready.shape[0]
        rows = slice(tile * span, end)
        copies += fetch([ready.at[rows]], [out_hbm.at[rows]], [sem.at[tile]])
    arrive(copies)


def inner_kernel(pattern_ref, vd_ref, vu_ref, pd_ref, pu_ref, out_ref, turned_ref):
    scale = pattern_ref[0].astype(F32)
    turned = (vu_ref[...].astype(F32) * scale).T
    turned_ref[...] = turned
    right = jnp.concatenate([vd_ref[...], turned.astype(BF16)], axis=0)
    for plane in range(pu_ref.shape[0]):
        left = jnp.concatenate([pd_ref[plane], pu_ref[plane]], axis=1)
        out_ref[plane] = dot(left, right).astype(BF16)


def prepare_kernel(present_ref, pattern_ref, vu_ref, out_ref, idx_ref, wide, picked):
    live_list(present_ref, idx_ref)
    wide[...] = vu_ref[...].astype(F32) * pattern_ref[0].astype(F32)
    pick_rows(idx_ref, wide, picked)
    out_ref[...] = picked[...].astype(BF16)


def outward_kernel(next_ref, turned_ref, left_ref, pu_ref, inner_ref, to_next, to_prev, idx, picked, ready, sem):
    planes = pu_ref.shape[0]
    group = planes // sem.shape[1]
    left_prev = left_ref[...]
    copies = []
    for way, (right_ref, out_hbm) in enumerate(((inner_ref, to_prev), (pu_ref, to_next))):
        left = left_prev
        if way == 1:
            live_list(next_ref, idx)
            pick_rows(idx, turned_ref, picked)
            left = picked[...].astype(BF16)
        for plane in range(planes):
            ready[way, plane] = dot(left, right_ref[plane]).astype(BF16)
            if plane % group == group - 1:
                some = slice(plane + 1 - group, plane + 1)
                at = sem.at[way, plane // group]
                copies += fetch([ready.at[way, some]], [out_hbm.at[some]], [at])
    arrive(copies)


def local_kernel(
    present_ref,
    pattern_ref,
    vu_hbm,
    vd_hbm,
    vd_next_ref,
    pd_hbm,
    pu_hbm,
    out_ref,
    idx_ref,
    wide,
    picked_u,
    picked_d,
    same,
    one_up,
    pd_ref,
    pu_ref,
    vd_ref,
    vu_ref,
    sem,
    v_sem,
):
    planes = pu_ref.shape[0]
    rows = LIVE * RG
    small = fetch([vd_hbm, vu_hbm], [vd_ref, vu_ref], [v_sem.at[0], v_sem.at[1]])
    copies = [
        fetch(
            [pd_hbm.at[plane], pu_hbm.at[plane]],
            [pd_ref.at[plane], pu_ref.at[plane]],
            [sem.at[0, plane], sem.at[1, plane]],
        )
        for plane in range(planes)
    ]
    live_list(present_ref, idx_ref)
    arrive(small)
    wide[...] = vu_ref[...].astype(F32) * pattern_ref[0].astype(F32)
    masked = wide[...].astype(BF16)
    pick_rows(idx_ref, wide, picked_u)
    wide[...] = vd_ref[...].astype(F32)
    pick_rows(idx_ref, wide, picked_d)
    left_u = picked_u[...].astype(BF16)
    left_d = picked_d[...].astype(BF16)
    for plane in range(planes):
        arrive(copies[plane])
        at = slice(plane * rows, (plane + 1) * rows)
        same[at] = (dot(left_d, pd_ref[plane]) + dot_nt(left_u, pu_ref[plane])).astype(BF16)
        one_up[at] = dot(left_d, pu_ref[plane]).astype(BF16)
    for plane in range(planes):
        at = slice(plane * rows, (plane + 1) * rows)
        value = dot(same[at], masked) + dot(one_up[at], vd_next_ref[...])
        if plane < planes // 2:
            value = value + picked_u[...]
        out_ref[plane] = value.astype(BF16)


def join_kernel(pattern_ref, local_ref, before_hbm, after_hbm, vu_hbm, out_ref, before, after, vu_ref, total, sem, v_sem):
    planes, rows, cols = local_ref.shape
    parts = sem.shape[1]
    group = planes // parts
    scale = pattern_ref[0].astype(F32)
    small = fetch([vu_hbm], [vu_ref], [v_sem.at[0]])
    copies = []
    for part in range(parts):
        some = slice(part * group, (part + 1) * group)
        copies.append(
            fetch(
                [before_hbm.at[some], after_hbm.at[some]],
                [before.at[some], after.at[some]],
                [sem.at[0, part], sem.at[1, part]],
            )
        )
    size = total.shape[0] * total.shape[1]
    out_ref[size:, :] = jnp.zeros((out_ref.shape[0] - size, LANES), BF16)
    arrive(small)
    masked = (vu_ref[...].astype(F32) * scale).astype(BF16)
    for part in range(parts):
        some = slice(part * group, (part + 1) * group)
        arrive(copies[part])
        value = dot(before[some].reshape(group * rows, cols), masked)
        for inner in range(group):
            plane = part * group + inner
            rest = after[plane].astype(F32) * scale + local_ref[plane].astype(F32)
            spread(total, plane, planes, value[inner * rows : (inner + 1) * rows] + rest)
    for tile in range(total.shape[0]):
        at = slice(tile * total.shape[1], (tile + 1) * total.shape[1])
        out_ref[at, :] = total[tile].astype(BF16)


def unit_pairs(got_ref):
    peers, units, planes, lanes = got_ref.shape
    for first in range(0, units, 2):
        some = range(first, min(first + 2, units))
        yield first, [got_ref[:, unit].reshape(peers * planes, lanes) for unit in some]


def spectrum_kernel(scale, forward_ref, got_ref, out_ref):
    for first, values in unit_pairs(got_ref):
        width = LANES * len(values)
        out_ref[first // 2, :, :width] = dot(forward_ref[...], jnp.concatenate(values, 1)) * scale


def convolve_kernel(forward_ref, inverse_ref, green_ref, got_ref, out_ref):
    peers, _, planes, lanes = got_ref.shape
    half = forward_ref.shape[0] // 2
    for first, values in unit_pairs(got_ref):
        width = LANES * len(values)
        freq = dot(forward_ref[...], jnp.concatenate(values, 1))
        green_re, green_im = green_ref[first // 2, :half, :width], green_ref[first // 2, half:, :width]
        screen_re, screen_im = freq[:half], freq[half:]
        mixed = jnp.concatenate(
            [green_re * screen_re - green_im * screen_im, green_re * screen_im + green_im * screen_re], 0
        )
        result = dot(inverse_ref[...], mixed.astype(BF16)).astype(BF16)
        for at in range(len(values)):
            out_ref[:, first + at] = result[:, at * lanes : (at + 1) * lanes].reshape(peers, planes, lanes)


def unpack_kernel(present_ref, got_ref, out_hbm, turn_ref, ready, sem):
    groups = present_ref.shape[0]
    planes, _, cols = ready.shape
    tiles = cols // LANES
    span = LIVE * RG * planes
    batch = groups // sem.shape[0]
    copies = []
    slot = jnp.int32(0)
    for group in range(groups):
        rows = slice(group * RG, (group + 1) * RG)

        @pl.when(present_ref[group] > 0)
        def _(slot=slot, rows=rows):
            for tile in range(tiles):
                turn = turn_ref.at[tile]
                at = pl.multiple_of(tile * span + slot * RG * planes, RG * planes)
                turn[...] = got_ref[pl.ds(at, RG * planes), :].astype(F32)
                for plane in range(planes):
                    value = turn[pl.ds(plane, RG, stride=planes), :]
                    ready[plane, rows, tile * LANES : (tile + 1) * LANES] = value.astype(BF16)

        @pl.when(present_ref[group] <= 0)
        def _(rows=rows):
            ready[:, rows, :] = jnp.zeros((planes, RG, cols), BF16)

        slot = slot + jnp.where(present_ref[group] > 0, 1, 0)
        if group % batch == batch - 1:
            some = slice((group + 1 - batch) * RG, (group + 1) * RG)
            copies += fetch([ready.at[:, some]], [out_hbm.at[:, some]], [sem.at[group // batch]])
    arrive(copies)


def per_device(g_upper, p_diag, p_upper, v_diag, v_upper, v_pattern, element_present):
    peers = lax.axis_size("energy")
    halves, local, _, size, _ = g_upper.shape
    planes = halves * local
    energies = local * peers
    live = LIVE * RG
    flat = live * planes

    def stay(value):
        return pltpu.with_memory_space_constraint(value, pltpu.HBM)

    p_d, p_u = (stay(x.reshape(planes, size, size)) for x in (p_diag, p_upper))
    v_d, v_u = (x.reshape(size, size) for x in (v_diag, v_upper))
    v_d_here, v_u_here = stay(v_d), stay(v_u)

    def near(value):
        return pltpu.with_memory_space_constraint(value, pltpu.VMEM)

    p_d_near, p_u_near, green = (
        near(x.reshape(planes, size, size)) for x in (p_diag, p_upper, g_upper)
    )
    v_d_near, v_u_near = near(v_d), near(v_u)
    present = element_present.reshape(-1)
    groups = present.shape[0]
    tiles = size // LANES
    units = -(-live * tiles // peers)
    routes = peers * units * planes

    idx = pltpu.SMEM((groups,), jnp.int32)
    square = pltpu.VMEM((size, size), F32)
    strip = pltpu.VMEM((live, size), F32)
    total = pltpu.VMEM((size // LANES, flat, LANES), F32)
    turn = pltpu.VMEM((6, RG * planes, LANES), F32)
    big = planes * size * size * 2

    def call(kernel, outs, ins, scratch, units, mib, place_out=vmem):
        many = isinstance(outs, list)
        return pl.pallas_call(
            kernel,
            out_shape=outs,
            in_specs=ins,
            out_specs=[place_out() for _ in outs] if many else place_out(),
            scratch_shapes=scratch,
            compiler_params=pltpu.CompilerParams(vmem_limit_bytes=mib * 2**20),
            cost_estimate=pl.CostEstimate(
                flops=int(units * 2 * planes * live * size * size), bytes_accessed=int(big), transcendentals=0
            ),
        )

    def array(*shape, dtype=BF16):
        return jax.ShapeDtypeStruct(shape, dtype)

    chosen = call(
        prepare_kernel, array(live, size), [smem()] * 2 + [vmem()], [idx, square, strip], 8, 6
    )(present, v_pattern, v_u)
    v_u_prev = shifted(chosen, 1)
    present_next = shifted(present, -1)
    v_d_next = shifted(v_d, -1)
    forward, inverse = tables(energies, peers)

    whole = pltpu.VMEM((planes, size, size), BF16)
    sems = pltpu.SemaphoreType.DMA((2, planes))
    pair = pltpu.SemaphoreType.DMA((2,))
    block = pltpu.VMEM((size, size), BF16)
    inner, turned = call(
        inner_kernel, [array(planes, size, size), array(size, size, dtype=F32)], [smem()] + [vmem()] * 4, [], 3.2, 12
    )(v_pattern, v_d_near, v_u_near, p_d_near, p_u_near)
    parcel = pltpu.VMEM((planes, live, size), BF16)
    to_next, to_prev = call(
        outward_kernel,
        [array(planes, live, size)] * 2,
        [smem()] + [vmem()] * 4,
        [idx, strip, pltpu.VMEM((2, planes, live, size), BF16), pltpu.SemaphoreType.DMA((2, 4))],
        2,
        10,
        hbm,
    )(present_next, turned, v_u_prev, p_u_near, inner)
    after = shifted(to_prev, -1)
    before = shifted(to_next, 1)

    send_green = call(
        pack_kernel,
        array(routes, LANES),
        [smem(), vmem()],
        [idx, turn, pltpu.VMEM((routes, LANES), BF16), pltpu.SemaphoreType.DMA((tiles,))],
        0.3,
        8,
        hbm,
    )(present, green)
    got_green = routed(send_green.reshape(peers, units, planes, LANES))

    stacked = pltpu.VMEM((flat, size), BF16)
    own = call(
        local_kernel,
        array(planes, live, size),
        [smem()] * 2 + [hbm()] * 2 + [vmem()] + [hbm()] * 2,
        [idx, square, strip, strip, stacked, stacked, whole, whole, block, block, sems, pair],
        5,
        16,
    )(present, v_pattern, v_u_here, v_d_here, v_d_next, p_d, p_u)

    green_freq = call(
        functools.partial(spectrum_kernel, 1.0 / (energies * math.sqrt(energies))),
        array(-(-units // 2), 2 * energies, 2 * LANES, dtype=F32),
        [vmem(), vmem()],
        [],
        0.5,
        8,
    )(forward, got_green)

    send = call(
        join_kernel,
        array(routes, LANES),
        [smem(), vmem()] + [hbm()] * 3,
        [parcel, parcel, block, total, pltpu.SemaphoreType.DMA((2, 2)), pair],
        1,
        12,
    )(v_pattern, own, stay(before), stay(after), v_u_here)
    got = routed(send.reshape(peers, units, planes, LANES))
    result = call(
        convolve_kernel, array(peers, units, planes, LANES), [vmem()] * 4, [], 1, 10
    )(forward, inverse, green_freq, got)
    returned = routed(result).reshape(routes, LANES)

    sigma = call(
        unpack_kernel,
        array(planes, size, size),
        [smem(), vmem()],
        [turn, whole, pltpu.SemaphoreType.DMA((4,))],
        0.3,
        8,
        hbm,
    )(present, returned)
    return sigma.reshape(halves, local, 1, size, size)


def solution(mesh):
    in_specs = (
        P(None, "energy", "space", None, None),
        P(None, "energy", "space", None, None),
        P(None, "energy", "space", None, None),
        P("space", None, None),
        P("space", None, None),
        P("space"),
        P("space", None),
    )
    out_specs = P(None, "energy", "space", None, None)

    return jax.shard_map(per_device, mesh=mesh, in_specs=in_specs, out_specs=out_specs, check_vma=False)
```

time: 140 us -> 137 us (0.979)
  Pallas kernels: 33.3 us -> 31.6 us
    pallas_call x6, Pallas kernels: 21.6 us -> 20 us  [the longest x1 4.93 us: per_device(): call(outward_kernel, [array(planes, live, size)] * 2, [smem()] + [vmem()]...]
  transfers between devices with their start and end apart: 7 -> 7, of which waited for: 3 -> 3; matrix products, arithmetic and copies ran while one was open for 0% -> 0% of each run, Pallas kernels for 16% -> 15%
where the time goes in v5:
time: 137 us; the launch traced here: 136 us
  waiting for transfers between devices  46.2 us (34%)
  Pallas kernels  31.6 us (23%)
  starting transfers between devices  28.2 us (21%)
  blocking collectives  25.8 us (19%)
  local copies, waits for them, and re-layouts  3.47 us (3%)
    ppermute x5, waiting for transfers between devices, shifted(): return lax.ppermute(value, 'space', pairs)  26.2 us
    all_to_all x1, blocking collectives, routed(): lax.all_to_all(value, 'energy', split_axis=0, concat_axis=0, tiled=True)  25.8 us
    all_to_all x2, waiting for transfers between devices, routed(): lax.all_to_all(value, 'energy', split_axis=0, concat_axis=0, tiled=True)  20 us
    all_to_all x2, starting transfers between devices, routed(): lax.all_to_all(value, 'energy', split_axis=0, concat_axis=0, tiled=True)  18.4 us
    pallas_call x1, Pallas kernels, per_device(): call(local_kernel, array(planes, live, size), [smem()] * 2 + [hbm()] * 2...  10.1 us
    ppermute x5, starting transfers between devices, shifted(): return lax.ppermute(value, 'space', pairs)  9.82 us
    pallas_call x1, Pallas kernels, per_device(): call(outward_kernel, [array(planes, live, size)] * 2, [smem()] + [vmem()]...  4.93 us
    pallas_call x1, Pallas kernels, per_device(): call(join_kernel, array(routes, LANES), [smem(), vmem()] + [hbm()] * 3, [...  4.69 us
  transfers between devices with their start and end apart: 7, of which 3 were waited for; matrix products, arithmetic and copies ran while one was open for 0% of the time, Pallas kernels for 15%

profile of v5, /device:TPU:1, one launch (start us, length us, event | category | flops | bytes accessed | tf_op | source)
XLA Modules:
  0.0 136.2 jit_solution(11375808695645697083)
XLA Ops:
  0.7 0.0 copy-start.5
  0.7 1.0 copy-done.5
  1.6 0.0 copy-start.3
  1.6 0.0 copy-start.6
  1.6 0.0 copy-start.8
  1.6 0.0 copy-start.9
  1.6 1.0 shard_map.95
  2.6 2.5 %collective-permute-start.2 = (bf16[240,384]{1,0:T(8,128)(2,1)S(1)}, bf16[240,384]{1,0:T(8,128)(2,1)S(1)}, u32[]{:S(2)}, u32[]{:S(2)}) collective-permute-start(bf16[240,384]{1,0:T(8,128)(2,1)S(1)} %shard_map.95), channel_id=1, source_target_pairs={{0,1},{1,2},{2,3},{3,4},{4,5},{5,6},{6,7},{7,0},{8,9},{9,10},{10,1... | collective-permute-start | bytes 552968 | tf_op jit(solution)/shard_map/ppermute | solution.py:36
  5.1 4.0 %collective-permute-start.1 = (s32[48]{0:T(128)}, s32[48]{0:T(128)S(1)}, u32[]{:S(2)}, u32[]{:S(2)}) collective-permute-start(s32[48]{0:T(128)} %bitcast.present_ref), channel_id=1, source_target_pairs={{0,7},{1,0},{2,1},{3,2},{4,3},{5,4},{6,5},{7,6},{8,15},{9,8},{10,9... | collective-permute-start | bytes 584 | tf_op jit(solution)/shard_map/ppermute | solution.py:36
  9.2 0.0 copy-done.3
  9.2 0.0 copy-done.6
  9.2 0.0 copy-done.8
  9.2 0.0 copy-done.9
  9.2 2.6 %shard_map.94 = (bf16[8,384,384]{2,1,0:T(8,128)(2,1)S(1)}, f32[384,384]{1,0:T(8,128)S(1)}) custom-call(s32[1]{0:T(128)S(6)} %copy.11.pattern_ref, bf16[384,384]{1,0:T(8,128)(2,1)S(1)} %bitcast.24, bf16[384,384]{1,0:T(8,128)(2,1)S(1)} %bitcast.20, bf16[8,384,384]{2,1,0:T(8,128)(2,1)S(1)} %bitcast.22, bf16[8,384,384]{2,1,0:T(8,128)(2,1)S(1)} %bitcast.15), custom_call_target="tpu_custom_call" | custom-call | flops 1811939328 | bytes 2359296 | tf_op jit(solution)/shard_map/pallas_call | solution.py:376
  11.8 0.0 collective-permute-done.1.next_ref
  11.8 1.6 %collective-permute-done.2.left_ref = bf16[240,384]{1,0:T(8,128)(2,1)S(1)} collective-permute-done((bf16[240,384]{1,0:T(8,128)(2,1)S(1)}, bf16[240,384]{1,0:T(8,128)(2,1)S(1)}, u32[]{:S(2)}, u32[]{:S(2)}) %collective-permute-start.2) | collective-permute-done | bytes 184352 | tf_op jit(solution)/shard_map/ppermute | solution.py:36
  13.4 0.0 copy-start.2
  13.4 4.9 %shard_map.96 = (bf16[8,240,384]{2,1,0:T(8,128)(2,1)}, bf16[8,240,384]{2,1,0:T(8,128)(2,1)S(1)}) custom-call(s32[48]{0:T(128)S(1)} %collective-permute-done.1.next_ref, f32[384,384]{1,0:T(8,128)S(1)} %get-tuple-element.9.turned_ref, bf16[240,384]{1,0:T(8,128)(2,1)S(1)} %collective-permute-done.2.left_ref, bf16[8,384,384]{2,1,0:T(8,128)(2,1)S(1)} %bitcast.16, ...), custom_call_target="tpu_custom_call" | custom-call | flops 1132462080 | bytes 2359296 | tf_op jit(solution)/shard_map/pallas_call | solution.py:380
  18.4 0.1 collective-permute-start.3
  18.5 2.7 %collective-permute-start.4 = (bf16[8,240,384]{2,1,0:T(8,128)(2,1)S(1)}, bf16[8,240,384]{2,1,0:T(8,128)(2,1)}, u32[]{:S(2)}, u32[]{:S(2)}) collective-permute-start(bf16[8,240,384]{2,1,0:T(8,128)(2,1)S(1)} %get-tuple-element.12), channel_id=1, source_target_pairs={{0,7},{1,0},{2,1},{3,2},{4,3},{5,4},{6,5},{7,6},{8,15},{9,8},{10,9... | collective-permute-start | bytes 4423688 | tf_op jit(solution)/shard_map/ppermute | solution.py:36
  21.1 0.0 copy-done.2
  21.1 2.4 %shard_map.91 = bf16[5888,128]{1,0:T(8,128)(2,1)} custom-call(s32[48]{0:T(128)} %bitcast.present_ref, bf16[8,384,384]{2,1,0:T(8,128)(2,1)S(1)} %bitcast.13), custom_call_target="tpu_custom_call" | custom-call | flops 169869312 | bytes 2359296 | tf_op jit(solution)/shard_map/pallas_call | solution.py:392
  23.5 8.9 %all-to-all-start = ((bf16[32,23,8,128]{3,2,1,0:T(8,128)(2,1)}), bf16[32,23,8,128]{3,2,1,0:T(8,128)(2,1)S(1)}, u32[]{:S(2)}, u32[]{:S(2)}) async-start(bf16[32,23,8,128]{3,2,1,0:T(8,128)(2,1)} %bitcast.2), calls=%async_computation | async-start | bytes 3014656 | tf_op jit(solution)/shard_map/all_to_all | solution.py:40
  32.5 0.5 collective-permute-start
  33.0 24.6 %collective-permute-done.vd_next_ref = bf16[384,384]{1,0:T(8,128)(2,1)S(1)} collective-permute-done((bf16[384,384]{1,0:T(8,128)(2,1)S(1)}, bf16[384,384]{1,0:T(8,128)(2,1)S(1)}, u32[]{:S(2)}, u32[]{:S(2)}) %collective-permute-start) | collective-permute-done | bytes 294944 | tf_op jit(solution)/shard_map/ppermute | solution.py:36
  57.6 10.1 %shard_map.93.local_ref = bf16[8,240,384]{2,1,0:T(8,128)(2,1)S(1)} custom-call(s32[48]{0:T(128)} %bitcast.present_ref, s32[1]{0:T(128)S(6)} %copy.11.pattern_ref, bf16[384,384]{1,0:T(8,128)(2,1)} %bitcast.17, bf16[384,384]{1,0:T(8,128)(2,1)} %bitcast.23, bf16[384,384]{1,0:T(8,128)(2,1)S(1)} %collective-permute-done.vd_next_ref, ...), custom_call_target="tpu_custom_call" | custom-call | flops 2831155200 | bytes 2359296 | tf_op jit(solution)/shard_map/pallas_call | solution.py:404
  67.6 0.0 collective-permute-done.3.before_hbm
  67.6 0.0 collective-permute-done.4.after_hbm
  67.7 4.7 %shard_map.97 = bf16[5888,128]{1,0:T(8,128)(2,1)} custom-call(s32[1]{0:T(128)S(6)} %copy.11.pattern_ref, bf16[8,240,384]{2,1,0:T(8,128)(2,1)S(1)} %shard_map.93.local_ref, bf16[8,240,384]{2,1,0:T(8,128)(2,1)} %collective-permute-done.3.before_hbm, bf16[8,240,384]{2,1,0:T(8,128)(2,1)} %collective-permute-done.4.after_hbm, bf16[384,384]{1,0:T(8,128)(2,1)} %bitcast.18), custom_call_target="tpu_custom_call" | custom-call | flops 566231040 | bytes 2359296 | tf_op jit(solution)/shard_map/pallas_call | solution.py:422
  72.3 0.0 all-to-all-done.got_ref
  72.4 0.0 copy-start
  72.4 0.0 copy-start.4
  72.4 1.1 copy-done
  73.5 9.5 %all-to-all-start.1 = ((bf16[32,23,8,128]{3,2,1,0:T(8,128)(2,1)}), bf16[32,23,8,128]{3,2,1,0:T(8,128)(2,1)}, u32[]{:S(2)}, u32[]{:S(2)}) async-start(bf16[32,23,8,128]{3,2,1,0:T(8,128)(2,1)} %bitcast.7), calls=%async_computation.1 | async-start | bytes 3014656 | tf_op jit(solution)/shard_map/all_to_all | solution.py:40
  83.0 0.0 copy-done.4
  83.0 0.0 copy-start.1
  83.0 1.4 %copy-done.1 = bf16[32,23,8,128]{3,2,1,0:T(8,128)(2,1)S(1)} copy-done((bf16[32,23,8,128]{3,2,1,0:T(8,128)(2,1)S(1)}, bf16[32,23,8,128]{3,2,1,0:T(8,128)(2,1)}, u32[]{:S(2)}) %copy-start.1) | copy-done | bytes 1507352
  84.4 0.0 copy-start.7
  84.4 0.6 shard_map.92.green_ref
  85.0 20.0 %all-to-all-done.1.got_ref = bf16[32,23,8,128]{3,2,1,0:T(8,128)(2,1)} async-done(((bf16[32,23,8,128]{3,2,1,0:T(8,128)(2,1)}), bf16[32,23,8,128]{3,2,1,0:T(8,128)(2,1)}, u32[]{:S(2)}, u32[]{:S(2)}) %all-to-all-start.1) | async-done | bytes 1507360 | tf_op jit(solution)/shard_map/all_to_all | solution.py:40
  105.0 0.0 copy-done.7
  105.0 2.6 %shard_map.98 = bf16[32,23,8,128]{3,2,1,0:T(8,128)(2,1)S(1)} custom-call(bf16[256,256]{1,0:T(8,128)(2,1)S(1)} %copy-done.4, bf16[256,256]{1,0:T(8,128)(2,1)S(1)} %copy-done.7, f32[12,256,256]{2,1,0:T(8,128)S(1)} %shard_map.92.green_ref, bf16[32,23,8,128]{3,2,1,0:T(8,128)(2,1)} %all-to-all-done.1.got_ref), custom_call_target="tpu_custom_call" | custom-call | flops 566231040 | bytes 2359296 | tf_op jit(solution)/shard_map/pallas_call | solution.py:431
  107.6 25.8 %all_to_all.15 = bf16[32,23,8,128]{3,2,1,0:T(8,128)(2,1)S(1)} all-to-all(bf16[32,23,8,128]{3,2,1,0:T(8,128)(2,1)S(1)} %shard_map.98), channel_id=1, replica_groups=mesh['energy'=32,'space'=8] {'energy'}, dimensions={0} | all-to-all | bytes 3014656 | tf_op jit(solution)/shard_map/all_to_all | solution.py:40
  133.3 2.7 %shard_map.99 = bf16[8,384,384]{2,1,0:T(8,128)(2,1)} custom-call(s32[48]{0:T(128)} %bitcast.present_ref, bf16[5888,128]{1,0:T(8,128)(2,1)S(1)} %bitcast.12), custom_call_target="tpu_custom_call" | custom-call | flops 169869312 | bytes 2359296 | tf_op jit(solution)/shard_map/pallas_call | solution.py:436
Async XLA Ops:
  0.7 1.0 copy-start.5
  1.6 7.6 %copy-start.3 = (bf16[2,4,1,384,384]{4,3,2,1,0:T(8,128)(2,1)S(1)}, bf16[2,4,1,384,384]{4,3,2,1,0:T(8,128)(2,1)}, u32[]{:S(2)}) copy-start(bf16[2,4,1,384,384]{4,3,2,1,0:T(8,128)(2,1)} %param.11) | copy-start | bytes 7077892
  1.6 7.6 %copy-start.6 = (bf16[1,384,384]{2,1,0:T(8,128)(2,1)S(1)}, bf16[1,384,384]{2,1,0:T(8,128)(2,1)}, u32[]{:S(2)}) copy-start(bf16[1,384,384]{2,1,0:T(8,128)(2,1)} %param.13) | copy-start | bytes 884740
  1.6 7.6 %copy-start.8 = (bf16[2,4,1,384,384]{4,3,2,1,0:T(8,128)(2,1)S(1)}, bf16[2,4,1,384,384]{4,3,2,1,0:T(8,128)(2,1)}, u32[]{:S(2)}) copy-start(bf16[2,4,1,384,384]{4,3,2,1,0:T(8,128)(2,1)} %param.10) | copy-start | bytes 7077892
  1.6 7.6 %copy-start.9 = (bf16[1,384,384]{2,1,0:T(8,128)(2,1)S(1)}, bf16[1,384,384]{2,1,0:T(8,128)(2,1)}, u32[]{:S(2)}) copy-start(bf16[1,384,384]{2,1,0:T(8,128)(2,1)} %param.12) | copy-start | bytes 884740
  2.6 10.8 %collective-permute-start.2 = (bf16[240,384]{1,0:T(8,128)(2,1)S(1)}, bf16[240,384]{1,0:T(8,128)(2,1)S(1)}, u32[]{:S(2)}, u32[]{:S(2)}) collective-permute-start(bf16[240,384]{1,0:T(8,128)(2,1)S(1)} %shard_map.95), channel_id=1, source_target_pairs={{0,1},{1,2},{2,3},{3,4},{4,5},{5,6},{6,7},{7,0},{8,9},{9,10},{10,1... | collective-permute-start | bytes 552968 | tf_op jit(solution)/shard_map/ppermute | solution.py:36
  5.1 6.7 %collective-permute-start.1 = (s32[48]{0:T(128)}, s32[48]{0:T(128)S(1)}, u32[]{:S(2)}, u32[]{:S(2)}) collective-permute-start(s32[48]{0:T(128)} %bitcast.present_ref), channel_id=1, source_target_pairs={{0,7},{1,0},{2,1},{3,2},{4,3},{5,4},{6,5},{7,6},{8,15},{9,8},{10,9... | collective-permute-start | bytes 584 | tf_op jit(solution)/shard_map/ppermute | solution.py:36
  13.4 7.7 %copy-start.2 = (bf16[2,4,1,384,384]{4,3,2,1,0:T(8,128)(2,1)S(1)}, bf16[2,4,1,384,384]{4,3,2,1,0:T(8,128)(2,1)}, u32[]{:S(2)}) copy-start(bf16[2,4,1,384,384]{4,3,2,1,0:T(8,128)(2,1)} %param.9) | copy-start | bytes 7077892
  18.4 49.3 %collective-permute-start.3 = (bf16[8,240,384]{2,1,0:T(8,128)(2,1)}, bf16[8,240,384]{2,1,0:T(8,128)(2,1)}, u32[]{:S(2)}, u32[]{:S(2)}) collective-permute-start(bf16[8,240,384]{2,1,0:T(8,128)(2,1)} %get-tuple-element.11), channel_id=1, source_target_pairs={{0,1},{1,2},{2,3},{3,4},{4,5},{5,6},{6,7},{7,0},{8,9},{9,10},{10,1... | collective-permute-start | bytes 4423688 | tf_op jit(solution)/shard_map/ppermute | solution.py:36
  18.5 49.2 %collective-permute-start.4 = (bf16[8,240,384]{2,1,0:T(8,128)(2,1)S(1)}, bf16[8,240,384]{2,1,0:T(8,128)(2,1)}, u32[]{:S(2)}, u32[]{:S(2)}) collective-permute-start(bf16[8,240,384]{2,1,0:T(8,128)(2,1)S(1)} %get-tuple-element.12), channel_id=1, source_target_pairs={{0,7},{1,0},{2,1},{3,2},{4,3},{5,4},{6,5},{7,6},{8,15},{9,8},{10,9... | collective-permute-start | bytes 4423688 | tf_op jit(solution)/shard_map/ppermute | solution.py:36
  23.5 48.8 %all-to-all-start = ((bf16[32,23,8,128]{3,2,1,0:T(8,128)(2,1)}), bf16[32,23,8,128]{3,2,1,0:T(8,128)(2,1)S(1)}, u32[]{:S(2)}, u32[]{:S(2)}) async-start(bf16[32,23,8,128]{3,2,1,0:T(8,128)(2,1)} %bitcast.2), calls=%async_computation | async-start | bytes 3014656 | tf_op jit(solution)/shard_map/all_to_all | solution.py:40
  32.5 25.1 %collective-permute-start = (bf16[384,384]{1,0:T(8,128)(2,1)S(1)}, bf16[384,384]{1,0:T(8,128)(2,1)S(1)}, u32[]{:S(2)}, u32[]{:S(2)}) collective-permute-start(bf16[384,384]{1,0:T(8,128)(2,1)S(1)} %bitcast.25), channel_id=1, source_target_pairs={{0,7},{1,0},{2,1},{3,2},{4,3},{5,4},{6,5},{7,6},{8,15},{9,8},{10,9... | collective-permute-start | bytes 884744 | tf_op jit(solution)/shard_map/ppermute | solution.py:36
  72.4 1.1 copy-start
  72.4 10.6 %copy-start.4 = (bf16[256,256]{1,0:T(8,128)(2,1)S(1)}, bf16[256,256]{1,0:T(8,128)(2,1)}, u32[]{:S(2)}) copy-start(bf16[256,256]{1,0:T(8,128)(2,1)} %constant.4.clone.forward_ref) | copy-start | bytes 393220
  73.5 31.5 %all-to-all-start.1 = ((bf16[32,23,8,128]{3,2,1,0:T(8,128)(2,1)}), bf16[32,23,8,128]{3,2,1,0:T(8,128)(2,1)}, u32[]{:S(2)}, u32[]{:S(2)}) async-start(bf16[32,23,8,128]{3,2,1,0:T(8,128)(2,1)} %bitcast.7), calls=%async_computation.1 | async-start | bytes 3014656 | tf_op jit(solution)/shard_map/all_to_all | solution.py:40
  83.0 1.4 %copy-start.1 = (bf16[32,23,8,128]{3,2,1,0:T(8,128)(2,1)S(1)}, bf16[32,23,8,128]{3,2,1,0:T(8,128)(2,1)}, u32[]{:S(2)}) copy-start(bf16[32,23,8,128]{3,2,1,0:T(8,128)(2,1)} %copy-done) | copy-start | bytes 4521988
  84.4 20.6 %copy-start.7 = (bf16[256,256]{1,0:T(8,128)(2,1)S(1)}, bf16[256,256]{1,0:T(8,128)(2,1)}, u32[]{:S(2)}) copy-start(bf16[256,256]{1,0:T(8,128)(2,1)} %constant.5.clone.inverse_ref) | copy-start | bytes 393220

commit v6 on v5

--- a/solution.py
+++ b/solution.py
@@ -140,23 +140,28 @@
     out_ref[...] = picked[...].astype(BF16)
 
 
-def outward_kernel(next_ref, turned_ref, left_ref, pu_ref, inner_ref, to_next, to_prev, idx, picked, ready, sem):
-    planes = pu_ref.shape[0]
-    group = planes // sem.shape[1]
+def outward_kernel(half, *refs):
+    if half == 0:
+        next_ref, turned_ref, left_ref, pu_ref, inner_ref, to_next, to_prev, picked_ref, idx, picked, ready, sem = refs
+    else:
+        picked_ref, left_ref, pu_ref, inner_ref, to_next, to_prev, ready, sem = refs
+    planes = ready.shape[1]
     left_prev = left_ref[...]
     copies = []
     for way, (right_ref, out_hbm) in enumerate(((inner_ref, to_prev), (pu_ref, to_next))):
         left = left_prev
-        if way == 1:
+        if way == 1 and half == 0:
             live_list(next_ref, idx)
             pick_rows(idx, turned_ref, picked)
             left = picked[...].astype(BF16)
+            picked_ref[...] = left
+        elif way == 1:
+            left = picked_ref[...]
         for plane in range(planes):
-            ready[way, plane] = dot(left, right_ref[plane]).astype(BF16)
-            if plane % group == group - 1:
-                some = slice(plane + 1 - group, plane + 1)
-                at = sem.at[way, plane // group]
-                copies += fetch([ready.at[way, some]], [out_hbm.at[some]], [at])
+            ready[way, plane] = dot(left, right_ref[half * planes + plane]).astype(BF16)
+            if plane % 2 == 1:
+                some = slice(plane - 1, plane + 1)
+                copies += fetch([ready.at[way, some]], [out_hbm.at[some]], [sem.at[way, plane // 2]])
     arrive(copies)
 
 
@@ -168,7 +173,8 @@
     vd_next_ref,
     pd_hbm,
     pu_hbm,
-    out_ref,
+    low_ref,
+    high_ref,
     idx_ref,
     wide,
     picked_u,
@@ -212,40 +218,39 @@
         value = dot(same[at], masked) + dot(one_up[at], vd_next_ref[...])
         if plane < planes // 2:
             value = value + picked_u[...]
-        out_ref[plane] = value.astype(BF16)
-
-
-def join_kernel(pattern_ref, local_ref, before_hbm, after_hbm, vu_hbm, out_ref, before, after, vu_ref, total, sem, v_sem):
+        out_ref = low_ref if plane < planes // 2 else high_ref
+        out_ref[plane % (planes // 2)] = value.astype(BF16)
+
+
+def join_kernel(pattern_ref, local_ref, before_hbm, after_hbm, vu_hbm, *refs):
+    first_ref = refs[0] if len(refs) == 8 else None
+    out_ref, before, after, vu_ref = refs[-7:-3] if first_ref is not None else refs[:4]
+    sem, v_sem = refs[-2:]
     planes, rows, cols = local_ref.shape
-    parts = sem.shape[1]
-    group = planes // parts
     scale = pattern_ref[0].astype(F32)
     small = fetch([vu_hbm], [vu_ref], [v_sem.at[0]])
-    copies = []
-    for part in range(parts):
-        some = slice(part * group, (part + 1) * group)
-        copies.append(
-            fetch(
-                [before_hbm.at[some], after_hbm.at[some]],
-                [before.at[some], after.at[some]],
-                [sem.at[0, part], sem.at[1, part]],
-            )
-        )
-    size = total.shape[0] * total.shape[1]
-    out_ref[size:, :] = jnp.zeros((out_ref.shape[0] - size, LANES), BF16)
+    copies = fetch([before_hbm, after_hbm], [before, after], [sem.at[0], sem.at[1]])
+    if first_ref is not None:
+        total = refs[-3]
+        size = total.shape[0] * total.shape[1]
+        out_ref[size:, :] = jnp.zeros((out_ref.shape[0] - size, LANES), BF16)
+        for plane in range(planes):
+            spread(total, plane, 2 * planes, first_ref[plane].astype(F32))
     arrive(small)
     masked = (vu_ref[...].astype(F32) * scale).astype(BF16)
-    for part in range(parts):
-        some = slice(part * group, (part + 1) * group)
-        arrive(copies[part])
-        value = dot(before[some].reshape(group * rows, cols), masked)
-        for inner in range(group):
-            plane = part * group + inner
-            rest = after[plane].astype(F32) * scale + local_ref[plane].astype(F32)
-            spread(total, plane, planes, value[inner * rows : (inner + 1) * rows] + rest)
-    for tile in range(total.shape[0]):
-        at = slice(tile * total.shape[1], (tile + 1) * total.shape[1])
-        out_ref[at, :] = total[tile].astype(BF16)
+    arrive(copies)
+    value = dot(before[...].reshape(planes * rows, cols), masked)
+    for plane in range(planes):
+        rest = after[plane].astype(F32) * scale + local_ref[plane].astype(F32)
+        whole = value[plane * rows : (plane + 1) * rows] + rest
+        if first_ref is None:
+            out_ref[plane] = whole.astype(BF16)
+        else:
+            spread(total, planes + plane, 2 * planes, whole)
+    if first_ref is not None:
+        for tile in range(total.shape[0]):
+            at = slice(tile * total.shape[1], (tile + 1) * total.shape[1])
+            out_ref[at, :] = total[tile].astype(BF16)
 
 
 def unit_pairs(got_ref):
@@ -344,13 +349,14 @@
     turn = pltpu.VMEM((6, RG * planes, LANES), F32)
     big = planes * size * size * 2
 
-    def call(kernel, outs, ins, scratch, units, mib, place_out=vmem):
-        many = isinstance(outs, list)
+    def call(kernel, outs, ins, scratch, units, mib, places=None):
+        if places is None:
+            places = [vmem() for _ in outs] if isinstance(outs, list) else vmem()
         return pl.pallas_call(
             kernel,
             out_shape=outs,
             in_specs=ins,
-            out_specs=[place_out() for _ in outs] if many else place_out(),
+            out_specs=places,
             scratch_shapes=scratch,
             compiler_params=pltpu.CompilerParams(vmem_limit_bytes=mib * 2**20),
             cost_estimate=pl.CostEstimate(
@@ -374,20 +380,34 @@
     pair = pltpu.SemaphoreType.DMA((2,))
     block = pltpu.VMEM((size, size), BF16)
     inner, turned = call(
-        inner_kernel, [array(planes, size, size), array(size, size, dtype=F32)], [smem()] + [vmem()] * 4, [], 3.2, 12
+        inner_kernel,
+        [array(planes, size, size), array(size, size, dtype=F32)],
+        [smem()] + [vmem()] * 4,
+        [],
+        3.2,
+        12,
     )(v_pattern, v_d_near, v_u_near, p_d_near, p_u_near)
-    parcel = pltpu.VMEM((planes, live, size), BF16)
-    to_next, to_prev = call(
-        outward_kernel,
-        [array(planes, live, size)] * 2,
+    half = planes // 2
+    parcel = pltpu.VMEM((half, live, size), BF16)
+    moving = [pltpu.VMEM((2, half, live, size), BF16), pltpu.SemaphoreType.DMA((2, half // 2))]
+
+    def outward(part, ins, outs, specs, scratch):
+        kernel = functools.partial(outward_kernel, part)
+        places = [hbm(), hbm()] + [vmem()] * (len(outs) - 2)
+        return call(kernel, outs, specs, scratch + moving, 1, 8, places)(*ins)
+
+    leaving = [array(half, live, size)] * 2
+    to_next, to_prev, picked = outward(
+        0,
+        [present_next, turned, v_u_prev, p_u_near, inner],
+        leaving + [array(live, size)],
         [smem()] + [vmem()] * 4,
-        [idx, strip, pltpu.VMEM((2, planes, live, size), BF16), pltpu.SemaphoreType.DMA((2, 4))],
-        2,
-        10,
-        hbm,
-    )(present_next, turned, v_u_prev, p_u_near, inner)
-    after = shifted(to_prev, -1)
-    before = shifted(to_next, 1)
+        [idx, strip],
+    )
+    after, before = [shifted(to_prev, -1)], [shifted(to_next, 1)]
+    to_next, to_prev = outward(1, [picked, v_u_prev, p_u_near, inner], leaving, [vmem()] * 4, [])
+    after.append(shifted(to_prev, -1))
+    before.append(shifted(to_next, 1))
 
     send_green = call(
         pack_kernel,
@@ -396,14 +416,14 @@
         [idx, turn, pltpu.VMEM((routes, LANES), BF16), pltpu.SemaphoreType.DMA((tiles,))],
         0.3,
         8,
-        hbm,
+        hbm(),
     )(present, green)
     got_green = routed(send_green.reshape(peers, units, planes, LANES))
 
     stacked = pltpu.VMEM((flat, size), BF16)
     own = call(
         local_kernel,
-        array(planes, live, size),
+        [array(half, live, size)] * 2,
         [smem()] * 2 + [hbm()] * 2 + [vmem()] + [hbm()] * 2,
         [idx, square, strip, strip, stacked, stacked, whole, whole, block, block, sems, pair],
         5,
@@ -419,14 +439,23 @@
         8,
     )(forward, got_green)
 
+    scratch = [parcel, parcel, block]
+    partial = call(
+        join_kernel,
+        array(half, live, size),
+        [smem(), vmem()] + [hbm()] * 3,
+        scratch + [pair, pair],
+        0.5,
+        6,
+    )(v_pattern, own[0], stay(before[0]), stay(after[0]), v_u_here)
     send = call(
         join_kernel,
         array(routes, LANES),
-        [smem(), vmem()] + [hbm()] * 3,
-        [parcel, parcel, block, total, pltpu.SemaphoreType.DMA((2, 2)), pair],
-        1,
-        12,
-    )(v_pattern, own, stay(before), stay(after), v_u_here)
+        [smem(), vmem()] + [hbm()] * 3 + [vmem()],
+        scratch + [total, pair, pair],
+        0.5,
+        10,
+    )(v_pattern, own[1], stay(before[1]), stay(after[1]), v_u_here, partial)
     got = routed(send.reshape(peers, units, planes, LANES))
     result = call(
         convolve_kernel, array(peers, units, planes, LANES), [vmem()] * 4, [], 1, 10
@@ -440,7 +469,7 @@
         [turn, whole, pltpu.SemaphoreType.DMA((4,))],
         0.3,
         8,
-        hbm,
+        hbm(),
     )(present, returned)
     return sigma.reshape(halves, local, 1, size, size)
 

time: 137 us -> 149 us (1.088)
  waiting for transfers between devices: 46.2 us -> 53.9 us
  local copies, waits for them, and re-layouts: 3.47 us -> 7.04 us
    ppermute x5 -> x7, waiting for transfers between devices: 26.2 us -> 33.9 us  [shifted(): return lax.ppermute(value, 'space', pairs)]
    unnamed x20 -> x30, local copies, waits for them, and re-layouts: 3.47 us -> 7.04 us
    ppermute x5 -> x7, starting transfers between devices: 9.82 us -> 11.3 us  [shifted(): return lax.ppermute(value, 'space', pairs)]
    pallas_call x3 -> x5, Pallas kernels: 19.7 us -> 20.9 us  [the longest x1 9.95 us: per_device(): call(local_kernel, [array(half, live, size)] * 2, [smem()] * 2 + [hbm()]...]
  transfers between devices with their start and end apart: 7 -> 9, of which waited for: 3 -> 3; matrix products, arithmetic and copies ran while one was open for 0% -> 0% of each run, Pallas kernels for 15% -> 17%
where the time goes in v6:
time: 149 us
  waiting for transfers between devices  53.9 us (36%)
  Pallas kernels  32.2 us (22%)
  starting transfers between devices  28.8 us (19%)
  blocking collectives  25.8 us (17%)
  local copies, waits for them, and re-layouts  7.04 us (5%)
    ppermute x7, waiting for transfers between devices, shifted(): return lax.ppermute(value, 'space', pairs)  33.9 us
    all_to_all x1, blocking collectives, routed(): lax.all_to_all(value, 'energy', split_axis=0, concat_axis=0, tiled=True)  25.8 us
    all_to_all x2, waiting for transfers between devices, routed(): lax.all_to_all(value, 'energy', split_axis=0, concat_axis=0, tiled=True)  20 us
    all_to_all x2, starting transfers between devices, routed(): lax.all_to_all(value, 'energy', split_axis=0, concat_axis=0, tiled=True)  17.6 us
    ppermute x7, starting transfers between devices, shifted(): return lax.ppermute(value, 'space', pairs)  11.3 us
    pallas_call x1, Pallas kernels, per_device(): call(local_kernel, [array(half, live, size)] * 2, [smem()] * 2 + [hbm()]...  9.95 us
    unnamed x30, local copies, waits for them, and re-layouts  7.04 us
    pallas_call x2, Pallas kernels, outward(): return call(kernel, outs, specs, scratch + moving, 1, 8, places)(*ins)  5.25 us
  transfers between devices with their start and end apart: 9, of which 3 were waited for; matrix products, arithmetic and copies ran while one was open for 0% of the time, Pallas kernels for 17%

profile of v6, /device:TPU:1, one launch (start us, length us, event | category | flops | bytes accessed | tf_op | source)
XLA Modules:
  0.0 148.8 jit_solution(11253194964256171542)
XLA Ops:
  0.0 0.0 copy-start.3
  0.0 1.7 %copy-done.3 = bf16[2,4,1,384,384]{4,3,2,1,0:T(8,128)(2,1)S(1)} copy-done((bf16[2,4,1,384,384]{4,3,2,1,0:T(8,128)(2,1)S(1)}, bf16[2,4,1,384,384]{4,3,2,1,0:T(8,128)(2,1)}, u32[]{:S(2)}) %copy-start.3) | copy-done | bytes 2359320
  1.7 0.0 copy-start.7
  1.7 0.7 copy-done.7
  2.3 2.3 %shard_map.91 = bf16[5888,128]{1,0:T(8,128)(2,1)} custom-call(s32[48]{0:T(128)S(1)} %bitcast.23, bf16[8,384,384]{2,1,0:T(8,128)(2,1)S(1)} %bitcast.17), custom_call_target="tpu_custom_call" | custom-call | flops 169869312 | bytes 2359296 | tf_op jit(solution)/shard_map/pallas_call | solution.py:412
  4.6 0.0 copy-start.4
  4.6 0.0 copy-start.8
  4.7 8.7 %all-to-all-start = ((bf16[32,23,8,128]{3,2,1,0:T(8,128)(2,1)}), bf16[32,23,8,128]{3,2,1,0:T(8,128)(2,1)S(1)}, u32[]{:S(2)}, u32[]{:S(2)}) async-start(bf16[32,23,8,128]{3,2,1,0:T(8,128)(2,1)} %bitcast.2), calls=%async_computation | async-start | bytes 3014656 | tf_op jit(solution)/shard_map/all_to_all | solution.py:40
  14.0 0.0 copy-done.4
  14.0 0.0 copy-done.8
  14.1 0.0 copy-start
  14.1 0.0 copy-start.9
  14.1 0.0 copy-start.10
  14.1 0.7 shard_map.95
  14.8 1.7 %collective-permute-start.2 = (bf16[240,384]{1,0:T(8,128)(2,1)S(1)}, bf16[240,384]{1,0:T(8,128)(2,1)S(1)}, u32[]{:S(2)}, u32[]{:S(2)}) collective-permute-start(bf16[240,384]{1,0:T(8,128)(2,1)S(1)} %shard_map.95), channel_id=1, source_target_pairs={{0,1},{1,2},{2,3},{3,4},{4,5},{5,6},{6,7},{7,0},{8,9},{9,10},{10,1... | collective-permute-start | bytes 552968 | tf_op jit(solution)/shard_map/ppermute | solution.py:36
  16.5 4.0 %collective-permute-start.1 = (s32[48]{0:T(128)S(1)}, s32[48]{0:T(128)S(1)}, u32[]{:S(2)}, u32[]{:S(2)}) collective-permute-start(s32[48]{0:T(128)S(1)} %bitcast.25), channel_id=1, source_target_pairs={{0,7},{1,0},{2,1},{3,2},{4,3},{5,4},{6,5},{7,6},{8,15},{9,8},{10,9... | collective-permute-start | bytes 584 | tf_op jit(solution)/shard_map/ppermute | solution.py:36
  20.6 0.0 copy-done
  20.6 0.0 copy-done.9
  20.6 0.0 copy-done.10
  20.6 2.6 %shard_map.94 = (bf16[8,384,384]{2,1,0:T(8,128)(2,1)S(1)}, f32[384,384]{1,0:T(8,128)S(1)}) custom-call(s32[1]{0:T(128)S(6)} %copy.11.pattern_ref, bf16[384,384]{1,0:T(8,128)(2,1)S(1)} %bitcast.31, bf16[384,384]{1,0:T(8,128)(2,1)S(1)} %bitcast.22, bf16[8,384,384]{2,1,0:T(8,128)(2,1)S(1)} %bitcast.29, bf16[8,384,384]{2,1,0:T(8,128)(2,1)S(1)} %bitcast.13), custom_call_target="tpu_custom_call" | custom-call | flops 1811939328 | bytes 2359296 | tf_op jit(solution)/shard_map/pallas_call | solution.py:382
  23.2 0.0 collective-permute-done.1.refs_0_
  23.2 2.1 %collective-permute-done.2.refs_2_.refs_1_ = bf16[240,384]{1,0:T(8,128)(2,1)S(1)} collective-permute-done((bf16[240,384]{1,0:T(8,128)(2,1)S(1)}, bf16[240,384]{1,0:T(8,128)(2,1)S(1)}, u32[]{:S(2)}, u32[]{:S(2)}) %collective-permute-start.2) | collective-permute-done | bytes 184352 | tf_op jit(solution)/shard_map/ppermute | solution.py:36
  25.2 2.9 %shard_map.96 = (bf16[4,240,384]{2,1,0:T(8,128)(2,1)S(1)}, bf16[4,240,384]{2,1,0:T(8,128)(2,1)S(1)}, bf16[240,384]{1,0:T(8,128)(2,1)S(1)}) custom-call(s32[48]{0:T(128)S(1)} %collective-permute-done.1.refs_0_, f32[384,384]{1,0:T(8,128)S(1)} %get-tuple-element.15.refs_1_, bf16[240,384]{1,0:T(8,128)(2,1)S(1)} %collective-permute-done.2.refs_2_.refs_1_, ...), custom_call_target="tpu_custom_call" | custom-call | flops 566231040 | bytes 2359296 | tf_op jit(solution)/shard_map/pallas_call | solution.py:397
  28.2 0.1 collective-permute-start.5
  28.3 2.7 %collective-permute-start.6 = (bf16[4,240,384]{2,1,0:T(8,128)(2,1)S(1)}, bf16[4,240,384]{2,1,0:T(8,128)(2,1)S(1)}, u32[]{:S(2)}, u32[]{:S(2)}) collective-permute-start(bf16[4,240,384]{2,1,0:T(8,128)(2,1)S(1)} %get-tuple-element.22), channel_id=1, source_target_pairs={{0,7},{1,0},{2,1},{3,2},{4,3},{5,4},{6,5},{7,6},{8,15},{9,8},{10,9... | collective-permute-start | bytes 2211848 | tf_op jit(solution)/shard_map/ppermute | solution.py:36
  31.0 2.3 %shard_map.97 = (bf16[4,240,384]{2,1,0:T(8,128)(2,1)S(1)}, bf16[4,240,384]{2,1,0:T(8,128)(2,1)S(1)}) custom-call(bf16[240,384]{1,0:T(8,128)(2,1)S(1)} %get-tuple-element.17.refs_0_, bf16[240,384]{1,0:T(8,128)(2,1)S(1)} %collective-permute-done.2.refs_2_.refs_1_, bf16[8,384,384]{2,1,0:T(8,128)(2,1)S(1)} %bitcast.15, ...), custom_call_target="tpu_custom_call" | custom-call | flops 566231040 | bytes 2359296 | tf_op jit(solution)/shard_map/pallas_call | solution.py:397
  33.3 0.1 collective-permute-start.3
  33.4 2.7 %collective-permute-start.4 = (bf16[4,240,384]{2,1,0:T(8,128)(2,1)S(1)}, bf16[4,240,384]{2,1,0:T(8,128)(2,1)S(1)}, u32[]{:S(2)}, u32[]{:S(2)}) collective-permute-start(bf16[4,240,384]{2,1,0:T(8,128)(2,1)S(1)} %get-tuple-element.19), channel_id=1, source_target_pairs={{0,7},{1,0},{2,1},{3,2},{4,3},{5,4},{6,5},{7,6},{8,15},{9,8},{10,9... | collective-permute-start | bytes 2211848 | tf_op jit(solution)/shard_map/ppermute | solution.py:36
  36.0 0.0 collective-permute-start
  36.0 31.8 %collective-permute-done.vd_next_ref = bf16[384,384]{1,0:T(8,128)(2,1)S(1)} collective-permute-done((bf16[384,384]{1,0:T(8,128)(2,1)S(1)}, bf16[384,384]{1,0:T(8,128)(2,1)S(1)}, u32[]{:S(2)}, u32[]{:S(2)}) %collective-permute-start) | collective-permute-done | bytes 294944 | tf_op jit(solution)/shard_map/ppermute | solution.py:36
  67.8 9.9 %shard_map.93 = (bf16[4,240,384]{2,1,0:T(8,128)(2,1)S(1)}, bf16[4,240,384]{2,1,0:T(8,128)(2,1)S(1)}) custom-call(s32[48]{0:T(128)S(1)} %bitcast.26, s32[1]{0:T(128)S(6)} %copy.11.pattern_ref, bf16[384,384]{1,0:T(8,128)(2,1)} %bitcast.18, bf16[384,384]{1,0:T(8,128)(2,1)} %bitcast.30, bf16[384,384]{1,0:T(8,128)(2,1)S(1)} %collective-permute-done.vd_next_ref, ...), custom_call_target="tpu_custom_call" | custom-call | flops 2831155200 | bytes 2359296 | tf_op jit(solution)/shard_map/pallas_call | solution.py:424
  77.8 0.0 collective-permute-done.5.before_hbm
  77.8 0.0 copy-start.13
  77.8 0.0 collective-permute-done.6.after_hbm
  77.8 0.0 copy-start.14
  77.8 0.8 copy-done.13
  78.7 0.3 copy-done.14
  78.9 2.1 %shard_map.98.refs_0_ = bf16[4,240,384]{2,1,0:T(8,128)(2,1)S(1)} custom-call(s32[1]{0:T(128)S(6)} %copy.11.pattern_ref, bf16[4,240,384]{2,1,0:T(8,128)(2,1)S(1)} %get-tuple-element.20.local_ref, bf16[4,240,384]{2,1,0:T(8,128)(2,1)} %copy-done.13, bf16[4,240,384]{2,1,0:T(8,128)(2,1)} %copy-done.14, bf16[384,384]{1,0:T(8,128)(2,1)} %bitcast.19), custom_call_target="tpu_custom_call" | custom-call | flops 283115520 | bytes 2359296 | tf_op jit(solution)/shard_map/pallas_call | solution.py:443
  81.0 0.0 collective-permute-done.3.before_hbm
  81.0 0.0 copy-start.11
  81.1 0.0 collective-permute-done.4.after_hbm
  81.1 0.0 copy-start.12
  81.1 0.8 copy-done.11
  81.9 0.2 copy-done.12
  82.2 3.6 %shard_map.99 = bf16[5888,128]{1,0:T(8,128)(2,1)} custom-call(s32[1]{0:T(128)S(6)} %copy.11.pattern_ref, bf16[4,240,384]{2,1,0:T(8,128)(2,1)S(1)} %get-tuple-element.14.local_ref, bf16[4,240,384]{2,1,0:T(8,128)(2,1)} %copy-done.11, bf16[4,240,384]{2,1,0:T(8,128)(2,1)} %copy-done.12, bf16[384,384]{1,0:T(8,128)(2,1)} %bitcast.20, ...), custom_call_target="tpu_custom_call" | custom-call | flops 283115520 | bytes 2359296 | tf_op jit(solution)/shard_map/pallas_call | solution.py:451
  85.7 0.0 copy-start.5
  85.7 0.0 all-to-all-done.got_ref
  85.7 0.0 copy-start.1
  85.8 1.1 copy-done.1
  86.9 8.8 %all-to-all-start.1 = ((bf16[32,23,8,128]{3,2,1,0:T(8,128)(2,1)}), bf16[32,23,8,128]{3,2,1,0:T(8,128)(2,1)}, u32[]{:S(2)}, u32[]{:S(2)}) async-start(bf16[32,23,8,128]{3,2,1,0:T(8,128)(2,1)} %bitcast.7), calls=%async_computation.1 | async-start | bytes 3014656 | tf_op jit(solution)/shard_map/all_to_all | solution.py:40
  95.7 0.0 copy-done.5
  95.7 0.0 copy-start.2
  95.7 1.4 copy-done.2
  97.1 0.0 copy-start.6
  97.1 0.6 shard_map.92.green_ref
  97.7 20.0 %all-to-all-done.1.got_ref = bf16[32,23,8,128]{3,2,1,0:T(8,128)(2,1)} async-done(((bf16[32,23,8,128]{3,2,1,0:T(8,128)(2,1)}), bf16[32,23,8,128]{3,2,1,0:T(8,128)(2,1)}, u32[]{:S(2)}, u32[]{:S(2)}) %all-to-all-start.1) | async-done | bytes 1507360 | tf_op jit(solution)/shard_map/all_to_all | solution.py:40
  117.7 0.0 copy-done.6
  117.7 2.6 %shard_map.100 = bf16[32,23,8,128]{3,2,1,0:T(8,128)(2,1)S(1)} custom-call(bf16[256,256]{1,0:T(8,128)(2,1)S(1)} %copy-done.5, bf16[256,256]{1,0:T(8,128)(2,1)S(1)} %copy-done.6, f32[12,256,256]{2,1,0:T(8,128)S(1)} %shard_map.92.green_ref, bf16[32,23,8,128]{3,2,1,0:T(8,128)(2,1)} %all-to-all-done.1.got_ref), custom_call_target="tpu_custom_call" | custom-call | flops 566231040 | bytes 2359296 | tf_op jit(solution)/shard_map/pallas_call | solution.py:460
  120.3 25.8 %all_to_all.15 = bf16[32,23,8,128]{3,2,1,0:T(8,128)(2,1)S(1)} all-to-all(bf16[32,23,8,128]{3,2,1,0:T(8,128)(2,1)S(1)} %shard_map.100), channel_id=1, replica_groups=mesh['energy'=32,'space'=8] {'energy'}, dimensions={0} | all-to-all | bytes 3014656 | tf_op jit(solution)/shard_map/all_to_all | solution.py:40
  146.1 2.6 %shard_map.101 = bf16[8,384,384]{2,1,0:T(8,128)(2,1)} custom-call(s32[48]{0:T(128)S(1)} %bitcast.27, bf16[5888,128]{1,0:T(8,128)(2,1)S(1)} %bitcast.16), custom_call_target="tpu_custom_call" | custom-call | flops 169869312 | bytes 2359296 | tf_op jit(solution)/shard_map/pallas_call | solution.py:465
Async XLA Ops:
  0.0 1.7 %copy-start.3 = (bf16[2,4,1,384,384]{4,3,2,1,0:T(8,128)(2,1)S(1)}, bf16[2,4,1,384,384]{4,3,2,1,0:T(8,128)(2,1)}, u32[]{:S(2)}) copy-start(bf16[2,4,1,384,384]{4,3,2,1,0:T(8,128)(2,1)} %param.9) | copy-start | bytes 7077892
  1.7 0.7 copy-start.7
  4.6 9.4 %copy-start.4 = (bf16[1,384,384]{2,1,0:T(8,128)(2,1)S(1)}, bf16[1,384,384]{2,1,0:T(8,128)(2,1)}, u32[]{:S(2)}) copy-start(bf16[1,384,384]{2,1,0:T(8,128)(2,1)} %param.13) | copy-start | bytes 884740
  4.6 9.4 %copy-start.8 = (s32[1,48]{1,0:T(1,128)S(1)}, s32[1,48]{1,0:T(1,128)}, u32[]{:S(2)}) copy-start(s32[1,48]{1,0:T(1,128)} %param.15) | copy-start | bytes 580
  4.7 81.1 %all-to-all-start = ((bf16[32,23,8,128]{3,2,1,0:T(8,128)(2,1)}), bf16[32,23,8,128]{3,2,1,0:T(8,128)(2,1)S(1)}, u32[]{:S(2)}, u32[]{:S(2)}) async-start(bf16[32,23,8,128]{3,2,1,0:T(8,128)(2,1)} %bitcast.2), calls=%async_computation | async-start | bytes 3014656 | tf_op jit(solution)/shard_map/all_to_all | solution.py:40
  14.1 6.5 %copy-start = (bf16[2,4,1,384,384]{4,3,2,1,0:T(8,128)(2,1)S(1)}, bf16[2,4,1,384,384]{4,3,2,1,0:T(8,128)(2,1)}, u32[]{:S(2)}) copy-start(bf16[2,4,1,384,384]{4,3,2,1,0:T(8,128)(2,1)} %param.11) | copy-start | bytes 7077892
  14.1 6.5 %copy-start.9 = (bf16[2,4,1,384,384]{4,3,2,1,0:T(8,128)(2,1)S(1)}, bf16[2,4,1,384,384]{4,3,2,1,0:T(8,128)(2,1)}, u32[]{:S(2)}) copy-start(bf16[2,4,1,384,384]{4,3,2,1,0:T(8,128)(2,1)} %param.10) | copy-start | bytes 7077892
  14.1 6.5 %copy-start.10 = (bf16[1,384,384]{2,1,0:T(8,128)(2,1)S(1)}, bf16[1,384,384]{2,1,0:T(8,128)(2,1)}, u32[]{:S(2)}) copy-start(bf16[1,384,384]{2,1,0:T(8,128)(2,1)} %param.12) | copy-start | bytes 884740
  14.8 10.4 %collective-permute-start.2 = (bf16[240,384]{1,0:T(8,128)(2,1)S(1)}, bf16[240,384]{1,0:T(8,128)(2,1)S(1)}, u32[]{:S(2)}, u32[]{:S(2)}) collective-permute-start(bf16[240,384]{1,0:T(8,128)(2,1)S(1)} %shard_map.95), channel_id=1, source_target_pairs={{0,1},{1,2},{2,3},{3,4},{4,5},{5,6},{6,7},{7,0},{8,9},{9,10},{10,1... | collective-permute-start | bytes 552968 | tf_op jit(solution)/shard_map/ppermute | solution.py:36
  16.5 6.7 %collective-permute-start.1 = (s32[48]{0:T(128)S(1)}, s32[48]{0:T(128)S(1)}, u32[]{:S(2)}, u32[]{:S(2)}) collective-permute-start(s32[48]{0:T(128)S(1)} %bitcast.25), channel_id=1, source_target_pairs={{0,7},{1,0},{2,1},{3,2},{4,3},{5,4},{6,5},{7,6},{8,15},{9,8},{10,9... | collective-permute-start | bytes 584 | tf_op jit(solution)/shard_map/ppermute | solution.py:36
  28.2 49.6 %collective-permute-start.5 = (bf16[4,240,384]{2,1,0:T(8,128)(2,1)S(1)}, bf16[4,240,384]{2,1,0:T(8,128)(2,1)S(1)}, u32[]{:S(2)}, u32[]{:S(2)}) collective-permute-start(bf16[4,240,384]{2,1,0:T(8,128)(2,1)S(1)} %get-tuple-element.21), channel_id=1, source_target_pairs={{0,1},{1,2},{2,3},{3,4},{4,5},{5,6},{6,7},{7,0},{8,9},{9,10},{10,1... | collective-permute-start | bytes 2211848 | tf_op jit(solution)/shard_map/ppermute | solution.py:36
  28.3 49.5 %collective-permute-start.6 = (bf16[4,240,384]{2,1,0:T(8,128)(2,1)S(1)}, bf16[4,240,384]{2,1,0:T(8,128)(2,1)S(1)}, u32[]{:S(2)}, u32[]{:S(2)}) collective-permute-start(bf16[4,240,384]{2,1,0:T(8,128)(2,1)S(1)} %get-tuple-element.22), channel_id=1, source_target_pairs={{0,7},{1,0},{2,1},{3,2},{4,3},{5,4},{6,5},{7,6},{8,15},{9,8},{10,9... | collective-permute-start | bytes 2211848 | tf_op jit(solution)/shard_map/ppermute | solution.py:36
  33.3 47.8 %collective-permute-start.3 = (bf16[4,240,384]{2,1,0:T(8,128)(2,1)S(1)}, bf16[4,240,384]{2,1,0:T(8,128)(2,1)S(1)}, u32[]{:S(2)}, u32[]{:S(2)}) collective-permute-start(bf16[4,240,384]{2,1,0:T(8,128)(2,1)S(1)} %get-tuple-element.18), channel_id=1, source_target_pairs={{0,1},{1,2},{2,3},{3,4},{4,5},{5,6},{6,7},{7,0},{8,9},{9,10},{10,1... | collective-permute-start | bytes 2211848 | tf_op jit(solution)/shard_map/ppermute | solution.py:36
  33.4 47.7 %collective-permute-start.4 = (bf16[4,240,384]{2,1,0:T(8,128)(2,1)S(1)}, bf16[4,240,384]{2,1,0:T(8,128)(2,1)S(1)}, u32[]{:S(2)}, u32[]{:S(2)}) collective-permute-start(bf16[4,240,384]{2,1,0:T(8,128)(2,1)S(1)} %get-tuple-element.19), channel_id=1, source_target_pairs={{0,7},{1,0},{2,1},{3,2},{4,3},{5,4},{6,5},{7,6},{8,15},{9,8},{10,9... | collective-permute-start | bytes 2211848 | tf_op jit(solution)/shard_map/ppermute | solution.py:36
  36.0 31.8 %collective-permute-start = (bf16[384,384]{1,0:T(8,128)(2,1)S(1)}, bf16[384,384]{1,0:T(8,128)(2,1)S(1)}, u32[]{:S(2)}, u32[]{:S(2)}) collective-permute-start(bf16[384,384]{1,0:T(8,128)(2,1)S(1)} %bitcast.32), channel_id=1, source_target_pairs={{0,7},{1,0},{2,1},{3,2},{4,3},{5,4},{6,5},{7,6},{8,15},{9,8},{10,9... | collective-permute-start | bytes 884744 | tf_op jit(solution)/shard_map/ppermute | solution.py:36
  77.8 0.9 copy-start.13
  77.8 1.1 copy-start.14
  81.0 0.9 copy-start.11
  81.1 1.1 copy-start.12
  85.7 10.0 %copy-start.5 = (bf16[256,256]{1,0:T(8,128)(2,1)S(1)}, bf16[256,256]{1,0:T(8,128)(2,1)}, u32[]{:S(2)}) copy-start(bf16[256,256]{1,0:T(8,128)(2,1)} %constant.4.clone.forward_ref) | copy-start | bytes 393220
  85.7 1.1 copy-start.1
  86.9 30.8 %all-to-all-start.1 = ((bf16[32,23,8,128]{3,2,1,0:T(8,128)(2,1)}), bf16[32,23,8,128]{3,2,1,0:T(8,128)(2,1)}, u32[]{:S(2)}, u32[]{:S(2)}) async-start(bf16[32,23,8,128]{3,2,1,0:T(8,128)(2,1)} %bitcast.7), calls=%async_computation.1 | async-start | bytes 3014656 | tf_op jit(solution)/shard_map/all_to_all | solution.py:40
  95.7 1.4 copy-start.2
  97.1 20.6 %copy-start.6 = (bf16[256,256]{1,0:T(8,128)(2,1)S(1)}, bf16[256,256]{1,0:T(8,128)(2,1)}, u32[]{:S(2)}) copy-start(bf16[256,256]{1,0:T(8,128)(2,1)} %constant.5.clone.inverse_ref) | copy-start | bytes 393220

commit v7 on v6

--- a/solution.py
+++ b/solution.py
@@ -101,19 +101,18 @@
 
 def pack_kernel(present_ref, g_ref, out_hbm, idx_ref, turn_ref, ready, sem):
     planes = g_ref.shape[0]
-    tiles = g_ref.shape[2] // LANES
-    span = LIVE * RG * planes
+    tiles, span, _ = turn_ref.shape
     live_list(present_ref, idx_ref)
     copies = []
     for tile in range(tiles):
         cols = slice(tile * LANES, (tile + 1) * LANES)
         for slot in range(LIVE):
-            turn = turn_ref.at[slot % turn_ref.shape[0]]
             row = pl.multiple_of(idx_ref[slot] * RG, RG)
             for plane in range(planes):
-                turn[pl.ds(plane, RG, stride=planes), :] = g_ref[plane, pl.ds(row, RG), cols].astype(F32)
-            at = tile * span + slot * RG * planes
-            ready[at : at + RG * planes, :] = turn[...].astype(BF16)
+                at = slot * RG * planes + plane
+                value = g_ref[plane, pl.ds(row, RG), cols].astype(F32)
+                turn_ref[tile, pl.ds(at, RG, stride=planes), :] = value
+        ready[tile * span : (tile + 1) * span, :] = turn_ref[tile].astype(BF16)
         end = (tile + 1) * span
         if tile == tiles - 1:
             ready[end:, :] = jnp.zeros((ready.shape[0] - end, LANES), BF16)
@@ -288,26 +287,20 @@
     tiles = cols // LANES
     span = LIVE * RG * planes
     batch = groups // sem.shape[0]
+    for tile in range(tiles):
+        turn_ref[tile, :span] = got_ref[tile * span : (tile + 1) * span, :].astype(F32)
     copies = []
     slot = jnp.int32(0)
     for group in range(groups):
         rows = slice(group * RG, (group + 1) * RG)
-
-        @pl.when(present_ref[group] > 0)
-        def _(slot=slot, rows=rows):
-            for tile in range(tiles):
-                turn = turn_ref.at[tile]
-                at = pl.multiple_of(tile * span + slot * RG * planes, RG * planes)
-                turn[...] = got_ref[pl.ds(at, RG * planes), :].astype(F32)
-                for plane in range(planes):
-                    value = turn[pl.ds(plane, RG, stride=planes), :]
-                    ready[plane, rows, tile * LANES : (tile + 1) * LANES] = value.astype(BF16)
-
-        @pl.when(present_ref[group] <= 0)
-        def _(rows=rows):
-            ready[:, rows, :] = jnp.zeros((planes, RG, cols), BF16)
-
-        slot = slot + jnp.where(present_ref[group] > 0, 1, 0)
+        live = present_ref[group] > 0
+        at = pl.multiple_of(slot * RG * planes, RG * planes)
+        for tile in range(tiles):
+            for plane in range(planes):
+                value = turn_ref[tile, pl.ds(at + plane, RG, stride=planes), :]
+                value = jnp.where(live, value, 0.0).astype(BF16)
+                ready[plane, rows, tile * LANES : (tile + 1) * LANES] = value
+        slot = slot + jnp.where(live, 1, 0)
         if group % batch == batch - 1:
             some = slice((group + 1 - batch) * RG, (group + 1) * RG)
             copies += fetch([ready.at[:, some]], [out_hbm.at[:, some]], [sem.at[group // batch]])
@@ -346,7 +339,6 @@
     square = pltpu.VMEM((size, size), F32)
     strip = pltpu.VMEM((live, size), F32)
     total = pltpu.VMEM((size // LANES, flat, LANES), F32)
-    turn = pltpu.VMEM((6, RG * planes, LANES), F32)
     big = planes * size * size * 2
 
     def call(kernel, outs, ins, scratch, units, mib, places=None):
@@ -413,7 +405,7 @@
         pack_kernel,
         array(routes, LANES),
         [smem(), vmem()],
-        [idx, turn, pltpu.VMEM((routes, LANES), BF16), pltpu.SemaphoreType.DMA((tiles,))],
+        [idx, total, pltpu.VMEM((routes, LANES), BF16), pltpu.SemaphoreType.DMA((tiles,))],
         0.3,
         8,
         hbm(),
@@ -466,7 +458,7 @@
         unpack_kernel,
         array(planes, size, size),
         [smem(), vmem()],
-        [turn, whole, pltpu.SemaphoreType.DMA((4,))],
+        [pltpu.VMEM((tiles, flat + RG * planes, LANES), F32), whole, pltpu.SemaphoreType.DMA((4,))],
         0.3,
         8,
         hbm(),

time: 149 us -> 149 us (level)
  no operation moved by 1% of the time
where the time goes in v7:
time: 149 us
  waiting for transfers between devices  53.9 us (36%)
  Pallas kernels  32.1 us (22%)
  starting transfers between devices  28.8 us (19%)
  blocking collectives  25.8 us (17%)
  local copies, waits for them, and re-layouts  7.04 us (5%)
    ppermute x7, waiting for transfers between devices, shifted(): return lax.ppermute(value, 'space', pairs)  33.9 us
    all_to_all x1, blocking collectives, routed(): lax.all_to_all(value, 'energy', split_axis=0, concat_axis=0, tiled=True)  25.8 us
    all_to_all x2, waiting for transfers between devices, routed(): lax.all_to_all(value, 'energy', split_axis=0, concat_axis=0, tiled=True)  20 us
    all_to_all x2, starting transfers between devices, routed(): lax.all_to_all(value, 'energy', split_axis=0, concat_axis=0, tiled=True)  17.6 us
    ppermute x7, starting transfers between devices, shifted(): return lax.ppermute(value, 'space', pairs)  11.3 us
    pallas_call x1, Pallas kernels, per_device(): call(local_kernel, [array(half, live, size)] * 2, [smem()] * 2 + [hbm()]...  9.95 us
    unnamed x30, local copies, waits for them, and re-layouts  7.04 us
    pallas_call x2, Pallas kernels, outward(): return call(kernel, outs, specs, scratch + moving, 1, 8, places)(*ins)  5.25 us
  transfers between devices with their start and end apart: 9, of which 3 were waited for; matrix products, arithmetic and copies ran while one was open for 0% of the time, Pallas kernels for 17%

profile of v7, /device:TPU:1, one launch (start us, length us, event | category | flops | bytes accessed | tf_op | source)
XLA Modules:
  0.0 148.7 jit_solution(863285856401880596)
XLA Ops:
  0.0 0.0 copy-start.3
  0.0 1.7 %copy-done.3 = bf16[2,4,1,384,384]{4,3,2,1,0:T(8,128)(2,1)S(1)} copy-done((bf16[2,4,1,384,384]{4,3,2,1,0:T(8,128)(2,1)S(1)}, bf16[2,4,1,384,384]{4,3,2,1,0:T(8,128)(2,1)}, u32[]{:S(2)}) %copy-start.3) | copy-done | bytes 2359320
  1.7 0.0 copy-start.7
  1.7 0.7 copy-done.7
  2.3 2.2 %shard_map.91 = bf16[5888,128]{1,0:T(8,128)(2,1)} custom-call(s32[48]{0:T(128)S(1)} %bitcast.23, bf16[8,384,384]{2,1,0:T(8,128)(2,1)S(1)} %bitcast.17), custom_call_target="tpu_custom_call" | custom-call | flops 169869312 | bytes 2359296 | tf_op jit(solution)/shard_map/pallas_call | solution.py:404
  4.5 0.0 copy-start.4
  4.5 0.0 copy-start.8
  4.5 8.7 %all-to-all-start = ((bf16[32,23,8,128]{3,2,1,0:T(8,128)(2,1)}), bf16[32,23,8,128]{3,2,1,0:T(8,128)(2,1)S(1)}, u32[]{:S(2)}, u32[]{:S(2)}) async-start(bf16[32,23,8,128]{3,2,1,0:T(8,128)(2,1)} %bitcast.2), calls=%async_computation | async-start | bytes 3014656 | tf_op jit(solution)/shard_map/all_to_all | solution.py:40
  13.9 0.0 copy-done.4
  13.9 0.0 copy-done.8
  13.9 0.0 copy-start
  14.0 0.0 copy-start.9
  14.0 0.0 copy-start.10
  14.0 0.7 shard_map.95
  14.7 1.7 %collective-permute-start.2 = (bf16[240,384]{1,0:T(8,128)(2,1)S(1)}, bf16[240,384]{1,0:T(8,128)(2,1)S(1)}, u32[]{:S(2)}, u32[]{:S(2)}) collective-permute-start(bf16[240,384]{1,0:T(8,128)(2,1)S(1)} %shard_map.95), channel_id=1, source_target_pairs={{0,1},{1,2},{2,3},{3,4},{4,5},{5,6},{6,7},{7,0},{8,9},{9,10},{10,1... | collective-permute-start | bytes 552968 | tf_op jit(solution)/shard_map/ppermute | solution.py:36
  16.4 4.0 %collective-permute-start.1 = (s32[48]{0:T(128)S(1)}, s32[48]{0:T(128)S(1)}, u32[]{:S(2)}, u32[]{:S(2)}) collective-permute-start(s32[48]{0:T(128)S(1)} %bitcast.25), channel_id=1, source_target_pairs={{0,7},{1,0},{2,1},{3,2},{4,3},{5,4},{6,5},{7,6},{8,15},{9,8},{10,9... | collective-permute-start | bytes 584 | tf_op jit(solution)/shard_map/ppermute | solution.py:36
  20.4 0.0 copy-done
  20.4 0.0 copy-done.9
  20.5 0.0 copy-done.10
  20.5 2.6 %shard_map.94 = (bf16[8,384,384]{2,1,0:T(8,128)(2,1)S(1)}, f32[384,384]{1,0:T(8,128)S(1)}) custom-call(s32[1]{0:T(128)S(6)} %copy.11.pattern_ref, bf16[384,384]{1,0:T(8,128)(2,1)S(1)} %bitcast.31, bf16[384,384]{1,0:T(8,128)(2,1)S(1)} %bitcast.22, bf16[8,384,384]{2,1,0:T(8,128)(2,1)S(1)} %bitcast.29, bf16[8,384,384]{2,1,0:T(8,128)(2,1)S(1)} %bitcast.13), custom_call_target="tpu_custom_call" | custom-call | flops 1811939328 | bytes 2359296 | tf_op jit(solution)/shard_map/pallas_call | solution.py:374
  23.1 0.0 collective-permute-done.1.refs_0_
  23.1 2.1 %collective-permute-done.2.refs_2_.refs_1_ = bf16[240,384]{1,0:T(8,128)(2,1)S(1)} collective-permute-done((bf16[240,384]{1,0:T(8,128)(2,1)S(1)}, bf16[240,384]{1,0:T(8,128)(2,1)S(1)}, u32[]{:S(2)}, u32[]{:S(2)}) %collective-permute-start.2) | collective-permute-done | bytes 184352 | tf_op jit(solution)/shard_map/ppermute | solution.py:36
  25.1 2.9 %shard_map.96 = (bf16[4,240,384]{2,1,0:T(8,128)(2,1)S(1)}, bf16[4,240,384]{2,1,0:T(8,128)(2,1)S(1)}, bf16[240,384]{1,0:T(8,128)(2,1)S(1)}) custom-call(s32[48]{0:T(128)S(1)} %collective-permute-done.1.refs_0_, f32[384,384]{1,0:T(8,128)S(1)} %get-tuple-element.15.refs_1_, bf16[240,384]{1,0:T(8,128)(2,1)S(1)} %collective-permute-done.2.refs_2_.refs_1_, ...), custom_call_target="tpu_custom_call" | custom-call | flops 566231040 | bytes 2359296 | tf_op jit(solution)/shard_map/pallas_call | solution.py:389
  28.1 0.1 collective-permute-start.5
  28.2 2.7 %collective-permute-start.6 = (bf16[4,240,384]{2,1,0:T(8,128)(2,1)S(1)}, bf16[4,240,384]{2,1,0:T(8,128)(2,1)S(1)}, u32[]{:S(2)}, u32[]{:S(2)}) collective-permute-start(bf16[4,240,384]{2,1,0:T(8,128)(2,1)S(1)} %get-tuple-element.22), channel_id=1, source_target_pairs={{0,7},{1,0},{2,1},{3,2},{4,3},{5,4},{6,5},{7,6},{8,15},{9,8},{10,9... | collective-permute-start | bytes 2211848 | tf_op jit(solution)/shard_map/ppermute | solution.py:36
  30.8 2.3 %shard_map.97 = (bf16[4,240,384]{2,1,0:T(8,128)(2,1)S(1)}, bf16[4,240,384]{2,1,0:T(8,128)(2,1)S(1)}) custom-call(bf16[240,384]{1,0:T(8,128)(2,1)S(1)} %get-tuple-element.17.refs_0_, bf16[240,384]{1,0:T(8,128)(2,1)S(1)} %collective-permute-done.2.refs_2_.refs_1_, bf16[8,384,384]{2,1,0:T(8,128)(2,1)S(1)} %bitcast.15, ...), custom_call_target="tpu_custom_call" | custom-call | flops 566231040 | bytes 2359296 | tf_op jit(solution)/shard_map/pallas_call | solution.py:389
  33.2 0.1 collective-permute-start.3
  33.3 2.7 %collective-permute-start.4 = (bf16[4,240,384]{2,1,0:T(8,128)(2,1)S(1)}, bf16[4,240,384]{2,1,0:T(8,128)(2,1)S(1)}, u32[]{:S(2)}, u32[]{:S(2)}) collective-permute-start(bf16[4,240,384]{2,1,0:T(8,128)(2,1)S(1)} %get-tuple-element.19), channel_id=1, source_target_pairs={{0,7},{1,0},{2,1},{3,2},{4,3},{5,4},{6,5},{7,6},{8,15},{9,8},{10,9... | collective-permute-start | bytes 2211848 | tf_op jit(solution)/shard_map/ppermute | solution.py:36
  35.9 0.0 collective-permute-start
  35.9 31.8 %collective-permute-done.vd_next_ref = bf16[384,384]{1,0:T(8,128)(2,1)S(1)} collective-permute-done((bf16[384,384]{1,0:T(8,128)(2,1)S(1)}, bf16[384,384]{1,0:T(8,128)(2,1)S(1)}, u32[]{:S(2)}, u32[]{:S(2)}) %collective-permute-start) | collective-permute-done | bytes 294944 | tf_op jit(solution)/shard_map/ppermute | solution.py:36
  67.7 9.9 %shard_map.93 = (bf16[4,240,384]{2,1,0:T(8,128)(2,1)S(1)}, bf16[4,240,384]{2,1,0:T(8,128)(2,1)S(1)}) custom-call(s32[48]{0:T(128)S(1)} %bitcast.26, s32[1]{0:T(128)S(6)} %copy.11.pattern_ref, bf16[384,384]{1,0:T(8,128)(2,1)} %bitcast.18, bf16[384,384]{1,0:T(8,128)(2,1)} %bitcast.30, bf16[384,384]{1,0:T(8,128)(2,1)S(1)} %collective-permute-done.vd_next_ref, ...), custom_call_target="tpu_custom_call" | custom-call | flops 2831155200 | bytes 2359296 | tf_op jit(solution)/shard_map/pallas_call | solution.py:416
  77.7 0.0 collective-permute-done.5.before_hbm
  77.7 0.0 copy-start.13
  77.7 0.0 collective-permute-done.6.after_hbm
  77.7 0.0 copy-start.14
  77.7 0.8 copy-done.13
  78.6 0.3 copy-done.14
  78.8 2.1 %shard_map.98.refs_0_ = bf16[4,240,384]{2,1,0:T(8,128)(2,1)S(1)} custom-call(s32[1]{0:T(128)S(6)} %copy.11.pattern_ref, bf16[4,240,384]{2,1,0:T(8,128)(2,1)S(1)} %get-tuple-element.20.local_ref, bf16[4,240,384]{2,1,0:T(8,128)(2,1)} %copy-done.13, bf16[4,240,384]{2,1,0:T(8,128)(2,1)} %copy-done.14, bf16[384,384]{1,0:T(8,128)(2,1)} %bitcast.19), custom_call_target="tpu_custom_call" | custom-call | flops 283115520 | bytes 2359296 | tf_op jit(solution)/shard_map/pallas_call | solution.py:435
  80.9 0.0 collective-permute-done.3.before_hbm
  80.9 0.0 copy-start.11
  80.9 0.0 collective-permute-done.4.after_hbm
  81.0 0.0 copy-start.12
  81.0 0.8 copy-done.11
  81.8 0.2 copy-done.12
  82.0 3.6 %shard_map.99 = bf16[5888,128]{1,0:T(8,128)(2,1)} custom-call(s32[1]{0:T(128)S(6)} %copy.11.pattern_ref, bf16[4,240,384]{2,1,0:T(8,128)(2,1)S(1)} %get-tuple-element.14.local_ref, bf16[4,240,384]{2,1,0:T(8,128)(2,1)} %copy-done.11, bf16[4,240,384]{2,1,0:T(8,128)(2,1)} %copy-done.12, bf16[384,384]{1,0:T(8,128)(2,1)} %bitcast.20, ...), custom_call_target="tpu_custom_call" | custom-call | flops 283115520 | bytes 2359296 | tf_op jit(solution)/shard_map/pallas_call | solution.py:443
  85.6 0.0 copy-start.5
  85.6 0.0 all-to-all-done.got_ref
  85.6 0.0 copy-start.1
  85.6 1.1 copy-done.1
  86.8 8.8 %all-to-all-start.1 = ((bf16[32,23,8,128]{3,2,1,0:T(8,128)(2,1)}), bf16[32,23,8,128]{3,2,1,0:T(8,128)(2,1)}, u32[]{:S(2)}, u32[]{:S(2)}) async-start(bf16[32,23,8,128]{3,2,1,0:T(8,128)(2,1)} %bitcast.7), calls=%async_computation.1 | async-start | bytes 3014656 | tf_op jit(solution)/shard_map/all_to_all | solution.py:40
  95.6 0.0 copy-done.5
  95.6 0.0 copy-start.2
  95.6 1.4 copy-done.2
  97.0 0.0 copy-start.6
  97.0 0.6 shard_map.92.green_ref
  97.6 20.0 %all-to-all-done.1.got_ref = bf16[32,23,8,128]{3,2,1,0:T(8,128)(2,1)} async-done(((bf16[32,23,8,128]{3,2,1,0:T(8,128)(2,1)}), bf16[32,23,8,128]{3,2,1,0:T(8,128)(2,1)}, u32[]{:S(2)}, u32[]{:S(2)}) %all-to-all-start.1) | async-done | bytes 1507360 | tf_op jit(solution)/shard_map/all_to_all | solution.py:40
  117.6 0.0 copy-done.6
  117.6 2.6 %shard_map.100 = bf16[32,23,8,128]{3,2,1,0:T(8,128)(2,1)S(1)} custom-call(bf16[256,256]{1,0:T(8,128)(2,1)S(1)} %copy-done.5, bf16[256,256]{1,0:T(8,128)(2,1)S(1)} %copy-done.6, f32[12,256,256]{2,1,0:T(8,128)S(1)} %shard_map.92.green_ref, bf16[32,23,8,128]{3,2,1,0:T(8,128)(2,1)} %all-to-all-done.1.got_ref), custom_call_target="tpu_custom_call" | custom-call | flops 566231040 | bytes 2359296 | tf_op jit(solution)/shard_map/pallas_call | solution.py:452
  120.2 25.8 %all_to_all.15 = bf16[32,23,8,128]{3,2,1,0:T(8,128)(2,1)S(1)} all-to-all(bf16[32,23,8,128]{3,2,1,0:T(8,128)(2,1)S(1)} %shard_map.100), channel_id=1, replica_groups=mesh['energy'=32,'space'=8] {'energy'}, dimensions={0} | all-to-all | bytes 3014656 | tf_op jit(solution)/shard_map/all_to_all | solution.py:40
  146.0 2.6 %shard_map.101 = bf16[8,384,384]{2,1,0:T(8,128)(2,1)} custom-call(s32[48]{0:T(128)S(1)} %bitcast.27, bf16[5888,128]{1,0:T(8,128)(2,1)S(1)} %bitcast.16), custom_call_target="tpu_custom_call" | custom-call | flops 169869312 | bytes 2359296 | tf_op jit(solution)/shard_map/pallas_call | solution.py:457
Async XLA Ops:
  0.0 1.7 %copy-start.3 = (bf16[2,4,1,384,384]{4,3,2,1,0:T(8,128)(2,1)S(1)}, bf16[2,4,1,384,384]{4,3,2,1,0:T(8,128)(2,1)}, u32[]{:S(2)}) copy-start(bf16[2,4,1,384,384]{4,3,2,1,0:T(8,128)(2,1)} %param.9) | copy-start | bytes 7077892
  1.7 0.7 copy-start.7
  4.5 9.4 %copy-start.4 = (bf16[1,384,384]{2,1,0:T(8,128)(2,1)S(1)}, bf16[1,384,384]{2,1,0:T(8,128)(2,1)}, u32[]{:S(2)}) copy-start(bf16[1,384,384]{2,1,0:T(8,128)(2,1)} %param.13) | copy-start | bytes 884740
  4.5 9.4 %copy-start.8 = (s32[1,48]{1,0:T(1,128)S(1)}, s32[1,48]{1,0:T(1,128)}, u32[]{:S(2)}) copy-start(s32[1,48]{1,0:T(1,128)} %param.15) | copy-start | bytes 580
  4.5 81.1 %all-to-all-start = ((bf16[32,23,8,128]{3,2,1,0:T(8,128)(2,1)}), bf16[32,23,8,128]{3,2,1,0:T(8,128)(2,1)S(1)}, u32[]{:S(2)}, u32[]{:S(2)}) async-start(bf16[32,23,8,128]{3,2,1,0:T(8,128)(2,1)} %bitcast.2), calls=%async_computation | async-start | bytes 3014656 | tf_op jit(solution)/shard_map/all_to_all | solution.py:40
  13.9 6.5 %copy-start = (bf16[2,4,1,384,384]{4,3,2,1,0:T(8,128)(2,1)S(1)}, bf16[2,4,1,384,384]{4,3,2,1,0:T(8,128)(2,1)}, u32[]{:S(2)}) copy-start(bf16[2,4,1,384,384]{4,3,2,1,0:T(8,128)(2,1)} %param.11) | copy-start | bytes 7077892
  14.0 6.5 %copy-start.9 = (bf16[2,4,1,384,384]{4,3,2,1,0:T(8,128)(2,1)S(1)}, bf16[2,4,1,384,384]{4,3,2,1,0:T(8,128)(2,1)}, u32[]{:S(2)}) copy-start(bf16[2,4,1,384,384]{4,3,2,1,0:T(8,128)(2,1)} %param.10) | copy-start | bytes 7077892
  14.0 6.5 %copy-start.10 = (bf16[1,384,384]{2,1,0:T(8,128)(2,1)S(1)}, bf16[1,384,384]{2,1,0:T(8,128)(2,1)}, u32[]{:S(2)}) copy-start(bf16[1,384,384]{2,1,0:T(8,128)(2,1)} %param.12) | copy-start | bytes 884740
  14.7 10.4 %collective-permute-start.2 = (bf16[240,384]{1,0:T(8,128)(2,1)S(1)}, bf16[240,384]{1,0:T(8,128)(2,1)S(1)}, u32[]{:S(2)}, u32[]{:S(2)}) collective-permute-start(bf16[240,384]{1,0:T(8,128)(2,1)S(1)} %shard_map.95), channel_id=1, source_target_pairs={{0,1},{1,2},{2,3},{3,4},{4,5},{5,6},{6,7},{7,0},{8,9},{9,10},{10,1... | collective-permute-start | bytes 552968 | tf_op jit(solution)/shard_map/ppermute | solution.py:36
  16.4 6.7 %collective-permute-start.1 = (s32[48]{0:T(128)S(1)}, s32[48]{0:T(128)S(1)}, u32[]{:S(2)}, u32[]{:S(2)}) collective-permute-start(s32[48]{0:T(128)S(1)} %bitcast.25), channel_id=1, source_target_pairs={{0,7},{1,0},{2,1},{3,2},{4,3},{5,4},{6,5},{7,6},{8,15},{9,8},{10,9... | collective-permute-start | bytes 584 | tf_op jit(solution)/shard_map/ppermute | solution.py:36
  28.1 49.6 %collective-permute-start.5 = (bf16[4,240,384]{2,1,0:T(8,128)(2,1)S(1)}, bf16[4,240,384]{2,1,0:T(8,128)(2,1)S(1)}, u32[]{:S(2)}, u32[]{:S(2)}) collective-permute-start(bf16[4,240,384]{2,1,0:T(8,128)(2,1)S(1)} %get-tuple-element.21), channel_id=1, source_target_pairs={{0,1},{1,2},{2,3},{3,4},{4,5},{5,6},{6,7},{7,0},{8,9},{9,10},{10,1... | collective-permute-start | bytes 2211848 | tf_op jit(solution)/shard_map/ppermute | solution.py:36
  28.2 49.5 %collective-permute-start.6 = (bf16[4,240,384]{2,1,0:T(8,128)(2,1)S(1)}, bf16[4,240,384]{2,1,0:T(8,128)(2,1)S(1)}, u32[]{:S(2)}, u32[]{:S(2)}) collective-permute-start(bf16[4,240,384]{2,1,0:T(8,128)(2,1)S(1)} %get-tuple-element.22), channel_id=1, source_target_pairs={{0,7},{1,0},{2,1},{3,2},{4,3},{5,4},{6,5},{7,6},{8,15},{9,8},{10,9... | collective-permute-start | bytes 2211848 | tf_op jit(solution)/shard_map/ppermute | solution.py:36
  33.2 47.8 %collective-permute-start.3 = (bf16[4,240,384]{2,1,0:T(8,128)(2,1)S(1)}, bf16[4,240,384]{2,1,0:T(8,128)(2,1)S(1)}, u32[]{:S(2)}, u32[]{:S(2)}) collective-permute-start(bf16[4,240,384]{2,1,0:T(8,128)(2,1)S(1)} %get-tuple-element.18), channel_id=1, source_target_pairs={{0,1},{1,2},{2,3},{3,4},{4,5},{5,6},{6,7},{7,0},{8,9},{9,10},{10,1... | collective-permute-start | bytes 2211848 | tf_op jit(solution)/shard_map/ppermute | solution.py:36
  33.3 47.7 %collective-permute-start.4 = (bf16[4,240,384]{2,1,0:T(8,128)(2,1)S(1)}, bf16[4,240,384]{2,1,0:T(8,128)(2,1)S(1)}, u32[]{:S(2)}, u32[]{:S(2)}) collective-permute-start(bf16[4,240,384]{2,1,0:T(8,128)(2,1)S(1)} %get-tuple-element.19), channel_id=1, source_target_pairs={{0,7},{1,0},{2,1},{3,2},{4,3},{5,4},{6,5},{7,6},{8,15},{9,8},{10,9... | collective-permute-start | bytes 2211848 | tf_op jit(solution)/shard_map/ppermute | solution.py:36
  35.9 31.8 %collective-permute-start = (bf16[384,384]{1,0:T(8,128)(2,1)S(1)}, bf16[384,384]{1,0:T(8,128)(2,1)S(1)}, u32[]{:S(2)}, u32[]{:S(2)}) collective-permute-start(bf16[384,384]{1,0:T(8,128)(2,1)S(1)} %bitcast.32), channel_id=1, source_target_pairs={{0,7},{1,0},{2,1},{3,2},{4,3},{5,4},{6,5},{7,6},{8,15},{9,8},{10,9... | collective-permute-start | bytes 884744 | tf_op jit(solution)/shard_map/ppermute | solution.py:36
  77.7 0.9 copy-start.13
  77.7 1.1 copy-start.14
  80.9 0.9 copy-start.11
  81.0 1.1 copy-start.12
  85.6 10.0 %copy-start.5 = (bf16[256,256]{1,0:T(8,128)(2,1)S(1)}, bf16[256,256]{1,0:T(8,128)(2,1)}, u32[]{:S(2)}) copy-start(bf16[256,256]{1,0:T(8,128)(2,1)} %constant.4.clone.forward_ref) | copy-start | bytes 393220
  85.6 1.1 copy-start.1
  86.8 30.8 %all-to-all-start.1 = ((bf16[32,23,8,128]{3,2,1,0:T(8,128)(2,1)}), bf16[32,23,8,128]{3,2,1,0:T(8,128)(2,1)}, u32[]{:S(2)}, u32[]{:S(2)}) async-start(bf16[32,23,8,128]{3,2,1,0:T(8,128)(2,1)} %bitcast.7), calls=%async_computation.1 | async-start | bytes 3014656 | tf_op jit(solution)/shard_map/all_to_all | solution.py:40
  95.6 1.4 copy-start.2
  97.0 20.6 %copy-start.6 = (bf16[256,256]{1,0:T(8,128)(2,1)S(1)}, bf16[256,256]{1,0:T(8,128)(2,1)}, u32[]{:S(2)}) copy-start(bf16[256,256]{1,0:T(8,128)(2,1)} %constant.5.clone.inverse_ref) | copy-start | bytes 393220

commit v8 on v7

--- a/solution.py
+++ b/solution.py
@@ -132,11 +132,15 @@
         out_ref[plane] = dot(left, right).astype(BF16)
 
 
-def prepare_kernel(present_ref, pattern_ref, vu_ref, out_ref, idx_ref, wide, picked):
+def prepare_kernel(present_ref, pattern_ref, vu_hbm, out_ref, idx_ref, held, sem):
     live_list(present_ref, idx_ref)
-    wide[...] = vu_ref[...].astype(F32) * pattern_ref[0].astype(F32)
-    pick_rows(idx_ref, wide, picked)
-    out_ref[...] = picked[...].astype(BF16)
+    copies = []
+    for slot in range(LIVE):
+        row = pl.multiple_of(idx_ref[slot] * RG, RG)
+        target = held.at[pl.ds(slot * RG, RG), :]
+        copies += fetch([vu_hbm.at[pl.ds(row, RG), :]], [target], [sem.at[slot]])
+    arrive(copies)
+    out_ref[...] = (held[...].astype(F32) * pattern_ref[0].astype(F32)).astype(BF16)
 
 
 def outward_kernel(half, *refs):
@@ -221,35 +225,39 @@
         out_ref[plane % (planes // 2)] = value.astype(BF16)
 
 
-def join_kernel(pattern_ref, local_ref, before_hbm, after_hbm, vu_hbm, *refs):
-    first_ref = refs[0] if len(refs) == 8 else None
-    out_ref, before, after, vu_ref = refs[-7:-3] if first_ref is not None else refs[:4]
-    sem, v_sem = refs[-2:]
+def join_low_kernel(
+    pattern_ref, local_ref, before_hbm, after_hbm, vu_hbm, out_ref, masked_ref, before, after, vu_ref, sem
+):
     planes, rows, cols = local_ref.shape
     scale = pattern_ref[0].astype(F32)
-    small = fetch([vu_hbm], [vu_ref], [v_sem.at[0]])
-    copies = fetch([before_hbm, after_hbm], [before, after], [sem.at[0], sem.at[1]])
-    if first_ref is not None:
-        total = refs[-3]
-        size = total.shape[0] * total.shape[1]
-        out_ref[size:, :] = jnp.zeros((out_ref.shape[0] - size, LANES), BF16)
-        for plane in range(planes):
-            spread(total, plane, 2 * planes, first_ref[plane].astype(F32))
-    arrive(small)
-    masked = (vu_ref[...].astype(F32) * scale).astype(BF16)
-    arrive(copies)
-    value = dot(before[...].reshape(planes * rows, cols), masked)
+    copies = fetch([vu_hbm, before_hbm, after_hbm], [vu_ref, before, after], [sem.at[0], sem.at[1], sem.at[2]])
+    arrive(copies)
+    masked_ref[...] = (vu_ref[...].astype(F32) * scale).astype(BF16)
+    value = dot(before[...].reshape(planes * rows, cols), masked_ref[...])
     for plane in range(planes):
         rest = after[plane].astype(F32) * scale + local_ref[plane].astype(F32)
-        whole = value[plane * rows : (plane + 1) * rows] + rest
-        if first_ref is None:
-            out_ref[plane] = whole.astype(BF16)
-        else:
-            spread(total, planes + plane, 2 * planes, whole)
-    if first_ref is not None:
-        for tile in range(total.shape[0]):
-            at = slice(tile * total.shape[1], (tile + 1) * total.shape[1])
-            out_ref[at, :] = total[tile].astype(BF16)
+        out_ref[plane] = (value[plane * rows : (plane + 1) * rows] + rest).astype(BF16)
+
+
+def join_high_kernel(
+    pattern_ref, local_ref, before_hbm, after_hbm, masked_ref, low_ref, out_ref, before, after, total, sem
+):
+    planes, rows, cols = local_ref.shape
+    lows = low_ref.shape[0]
+    copies = fetch([before_hbm, after_hbm], [before, after], [sem.at[0], sem.at[1]])
+    scale = pattern_ref[0].astype(F32)
+    size = total.shape[0] * total.shape[1]
+    out_ref[size:, :] = jnp.zeros((out_ref.shape[0] - size, LANES), BF16)
+    for plane in range(lows):
+        spread(total, plane, lows + planes, low_ref[plane].astype(F32))
+    arrive(copies)
+    value = dot(before[...].reshape(planes * rows, cols), masked_ref[...])
+    for plane in range(planes):
+        rest = after[plane].astype(F32) * scale + local_ref[plane].astype(F32)
+        spread(total, lows + plane, lows + planes, value[plane * rows : (plane + 1) * rows] + rest)
+    for tile in range(total.shape[0]):
+        at = slice(tile * total.shape[1], (tile + 1) * total.shape[1])
+        out_ref[at, :] = total[tile].astype(BF16)
 
 
 def unit_pairs(got_ref):
@@ -360,8 +368,13 @@
         return jax.ShapeDtypeStruct(shape, dtype)
 
     chosen = call(
-        prepare_kernel, array(live, size), [smem()] * 2 + [vmem()], [idx, square, strip], 8, 6
-    )(present, v_pattern, v_u)
+        prepare_kernel,
+        array(live, size),
+        [smem()] * 2 + [hbm()],
+        [idx, pltpu.VMEM((live, size), BF16), pltpu.SemaphoreType.DMA((LIVE,))],
+        8,
+        6,
+    )(present, v_pattern, v_u_here)
     v_u_prev = shifted(chosen, 1)
     present_next = shifted(present, -1)
     v_d_next = shifted(v_d, -1)
@@ -431,23 +444,22 @@
         8,
     )(forward, got_green)
 
-    scratch = [parcel, parcel, block]
-    partial = call(
-        join_kernel,
-        array(half, live, size),
+    partial, masked = call(
+        join_low_kernel,
+        [array(half, live, size), array(size, size)],
         [smem(), vmem()] + [hbm()] * 3,
-        scratch + [pair, pair],
+        [parcel, parcel, block, pltpu.SemaphoreType.DMA((3,))],
         0.5,
         6,
     )(v_pattern, own[0], stay(before[0]), stay(after[0]), v_u_here)
     send = call(
-        join_kernel,
+        join_high_kernel,
         array(routes, LANES),
-        [smem(), vmem()] + [hbm()] * 3 + [vmem()],
-        scratch + [total, pair, pair],
+        [smem(), vmem()] + [hbm()] * 2 + [vmem()] * 2,
+        [parcel, parcel, total, pair],
         0.5,
         10,
-    )(v_pattern, own[1], stay(before[1]), stay(after[1]), v_u_here, partial)
+    )(v_pattern, own[1], stay(before[1]), stay(after[1]), masked, partial)
     got = routed(send.reshape(peers, units, planes, LANES))
     result = call(
         convolve_kernel, array(peers, units, planes, LANES), [vmem()] * 4, [], 1, 10

time: 149 us -> 150 us (level)
  no operation moved by 1% of the time
where the time goes in v8:
time: 150 us
  waiting for transfers between devices  53.9 us (36%)
  Pallas kernels  33.5 us (22%)
  starting transfers between devices  28.7 us (19%)
  blocking collectives  25.8 us (17%)
  local copies, waits for them, and re-layouts  7.04 us (5%)
    ppermute x7, waiting for transfers between devices, shifted(): return lax.ppermute(value, 'space', pairs)  33.9 us
    all_to_all x1, blocking collectives, routed(): lax.all_to_all(value, 'energy', split_axis=0, concat_axis=0, tiled=True)  25.8 us
    all_to_all x2, waiting for transfers between devices, routed(): lax.all_to_all(value, 'energy', split_axis=0, concat_axis=0, tiled=True)  20 us
    all_to_all x2, starting transfers between devices, routed(): lax.all_to_all(value, 'energy', split_axis=0, concat_axis=0, tiled=True)  17.4 us
    ppermute x7, starting transfers between devices, shifted(): return lax.ppermute(value, 'space', pairs)  11.3 us
    pallas_call x1, Pallas kernels, per_device(): call(local_kernel, [array(half, live, size)] * 2, [smem()] * 2 + [hbm()]...  9.93 us
    unnamed x30, local copies, waits for them, and re-layouts  7.04 us
    pallas_call x2, Pallas kernels, outward(): return call(kernel, outs, specs, scratch + moving, 1, 8, places)(*ins)  5.25 us
  transfers between devices with their start and end apart: 9, of which 3 were waited for; matrix products, arithmetic and copies ran while one was open for 0% of the time, Pallas kernels for 17%

profile of v8, /device:TPU:1, one launch (start us, length us, event | category | flops | bytes accessed | tf_op | source)
XLA Modules:
  0.0 149.9 jit_solution(6050246991024451414)
XLA Ops:
  0.0 0.0 copy-start.3
  0.0 1.7 %copy-done.3 = bf16[2,4,1,384,384]{4,3,2,1,0:T(8,128)(2,1)S(1)} copy-done((bf16[2,4,1,384,384]{4,3,2,1,0:T(8,128)(2,1)S(1)}, bf16[2,4,1,384,384]{4,3,2,1,0:T(8,128)(2,1)}, u32[]{:S(2)}) %copy-start.3) | copy-done | bytes 2359320
  1.7 0.0 copy-start.7
  1.7 0.7 copy-done.7
  2.3 2.2 %shard_map.91 = bf16[5888,128]{1,0:T(8,128)(2,1)} custom-call(s32[48]{0:T(128)S(1)} %bitcast.22, bf16[8,384,384]{2,1,0:T(8,128)(2,1)S(1)} %bitcast.17), custom_call_target="tpu_custom_call" | custom-call | flops 169869312 | bytes 2359296 | tf_op jit(solution)/shard_map/pallas_call | solution.py:417
  4.5 0.0 copy-start.8
  4.5 8.6 %all-to-all-start = ((bf16[32,23,8,128]{3,2,1,0:T(8,128)(2,1)}), bf16[32,23,8,128]{3,2,1,0:T(8,128)(2,1)S(1)}, u32[]{:S(2)}, u32[]{:S(2)}) async-start(bf16[32,23,8,128]{3,2,1,0:T(8,128)(2,1)} %bitcast.2), calls=%async_computation | async-start | bytes 3014656 | tf_op jit(solution)/shard_map/all_to_all | solution.py:40
  13.8 0.0 copy-done.8
  13.8 0.0 copy-start
  13.8 0.0 copy-start.5
  13.8 0.0 copy-start.9
  13.8 0.0 copy-start.10
  13.8 2.2 %shard_map.95 = bf16[240,384]{1,0:T(8,128)(2,1)S(1)} custom-call(s32[48]{0:T(128)S(1)} %bitcast.23, s32[1]{0:T(128)S(6)} %copy.11.pattern_ref, bf16[384,384]{1,0:T(8,128)(2,1)} %bitcast.18), custom_call_target="tpu_custom_call" | custom-call | flops 4529848320 | bytes 2359296 | tf_op jit(solution)/shard_map/pallas_call | solution.py:370
  16.0 1.7 %collective-permute-start.2 = (bf16[240,384]{1,0:T(8,128)(2,1)S(1)}, bf16[240,384]{1,0:T(8,128)(2,1)S(1)}, u32[]{:S(2)}, u32[]{:S(2)}) collective-permute-start(bf16[240,384]{1,0:T(8,128)(2,1)S(1)} %shard_map.95), channel_id=1, source_target_pairs={{0,1},{1,2},{2,3},{3,4},{4,5},{5,6},{6,7},{7,0},{8,9},{9,10},{10,1... | collective-permute-start | bytes 552968 | tf_op jit(solution)/shard_map/ppermute | solution.py:36
  17.8 4.0 %collective-permute-start.1 = (s32[48]{0:T(128)S(1)}, s32[48]{0:T(128)S(1)}, u32[]{:S(2)}, u32[]{:S(2)}) collective-permute-start(s32[48]{0:T(128)S(1)} %bitcast.24), channel_id=1, source_target_pairs={{0,7},{1,0},{2,1},{3,2},{4,3},{5,4},{6,5},{7,6},{8,15},{9,8},{10,9... | collective-permute-start | bytes 584 | tf_op jit(solution)/shard_map/ppermute | solution.py:36
  21.8 0.0 copy-done
  21.8 0.0 copy-done.5
  21.8 0.0 copy-done.9
  21.8 0.0 copy-done.10
  21.8 2.6 %shard_map.94 = (bf16[8,384,384]{2,1,0:T(8,128)(2,1)S(1)}, f32[384,384]{1,0:T(8,128)S(1)}) custom-call(s32[1]{0:T(128)S(6)} %copy.11.pattern_ref, bf16[384,384]{1,0:T(8,128)(2,1)S(1)} %bitcast.30, bf16[384,384]{1,0:T(8,128)(2,1)S(1)} %bitcast.21, bf16[8,384,384]{2,1,0:T(8,128)(2,1)S(1)} %bitcast.28, bf16[8,384,384]{2,1,0:T(8,128)(2,1)S(1)} %bitcast.13), custom_call_target="tpu_custom_call" | custom-call | flops 1811939328 | bytes 2359296 | tf_op jit(solution)/shard_map/pallas_call | solution.py:387
  24.4 0.0 collective-permute-done.1.refs_0_
  24.4 2.1 %collective-permute-done.2.refs_2_.refs_1_ = bf16[240,384]{1,0:T(8,128)(2,1)S(1)} collective-permute-done((bf16[240,384]{1,0:T(8,128)(2,1)S(1)}, bf16[240,384]{1,0:T(8,128)(2,1)S(1)}, u32[]{:S(2)}, u32[]{:S(2)}) %collective-permute-start.2) | collective-permute-done | bytes 184352 | tf_op jit(solution)/shard_map/ppermute | solution.py:36
  26.5 2.9 %shard_map.96 = (bf16[4,240,384]{2,1,0:T(8,128)(2,1)S(1)}, bf16[4,240,384]{2,1,0:T(8,128)(2,1)S(1)}, bf16[240,384]{1,0:T(8,128)(2,1)S(1)}) custom-call(s32[48]{0:T(128)S(1)} %collective-permute-done.1.refs_0_, f32[384,384]{1,0:T(8,128)S(1)} %get-tuple-element.17.refs_1_, bf16[240,384]{1,0:T(8,128)(2,1)S(1)} %collective-permute-done.2.refs_2_.refs_1_, ...), custom_call_target="tpu_custom_call" | custom-call | flops 566231040 | bytes 2359296 | tf_op jit(solution)/shard_map/pallas_call | solution.py:402
  29.4 0.1 collective-permute-start.5
  29.5 2.7 %collective-permute-start.6 = (bf16[4,240,384]{2,1,0:T(8,128)(2,1)S(1)}, bf16[4,240,384]{2,1,0:T(8,128)(2,1)S(1)}, u32[]{:S(2)}, u32[]{:S(2)}) collective-permute-start(bf16[4,240,384]{2,1,0:T(8,128)(2,1)S(1)} %get-tuple-element.24), channel_id=1, source_target_pairs={{0,7},{1,0},{2,1},{3,2},{4,3},{5,4},{6,5},{7,6},{8,15},{9,8},{10,9... | collective-permute-start | bytes 2211848 | tf_op jit(solution)/shard_map/ppermute | solution.py:36
  32.2 2.3 %shard_map.97 = (bf16[4,240,384]{2,1,0:T(8,128)(2,1)S(1)}, bf16[4,240,384]{2,1,0:T(8,128)(2,1)S(1)}) custom-call(bf16[240,384]{1,0:T(8,128)(2,1)S(1)} %get-tuple-element.19.refs_0_, bf16[240,384]{1,0:T(8,128)(2,1)S(1)} %collective-permute-done.2.refs_2_.refs_1_, bf16[8,384,384]{2,1,0:T(8,128)(2,1)S(1)} %bitcast.15, ...), custom_call_target="tpu_custom_call" | custom-call | flops 566231040 | bytes 2359296 | tf_op jit(solution)/shard_map/pallas_call | solution.py:402
  34.5 0.1 collective-permute-start.3
  34.6 2.7 %collective-permute-start.4 = (bf16[4,240,384]{2,1,0:T(8,128)(2,1)S(1)}, bf16[4,240,384]{2,1,0:T(8,128)(2,1)S(1)}, u32[]{:S(2)}, u32[]{:S(2)}) collective-permute-start(bf16[4,240,384]{2,1,0:T(8,128)(2,1)S(1)} %get-tuple-element.21), channel_id=1, source_target_pairs={{0,7},{1,0},{2,1},{3,2},{4,3},{5,4},{6,5},{7,6},{8,15},{9,8},{10,9... | collective-permute-start | bytes 2211848 | tf_op jit(solution)/shard_map/ppermute | solution.py:36
  37.2 0.0 collective-permute-start
  37.3 31.8 %collective-permute-done.vd_next_ref = bf16[384,384]{1,0:T(8,128)(2,1)S(1)} collective-permute-done((bf16[384,384]{1,0:T(8,128)(2,1)S(1)}, bf16[384,384]{1,0:T(8,128)(2,1)S(1)}, u32[]{:S(2)}, u32[]{:S(2)}) %collective-permute-start) | collective-permute-done | bytes 294944 | tf_op jit(solution)/shard_map/ppermute | solution.py:36
  69.1 9.9 %shard_map.93 = (bf16[4,240,384]{2,1,0:T(8,128)(2,1)S(1)}, bf16[4,240,384]{2,1,0:T(8,128)(2,1)S(1)}) custom-call(s32[48]{0:T(128)S(1)} %bitcast.25, s32[1]{0:T(128)S(6)} %copy.11.pattern_ref, bf16[384,384]{1,0:T(8,128)(2,1)} %bitcast.19, bf16[384,384]{1,0:T(8,128)(2,1)} %bitcast.29, bf16[384,384]{1,0:T(8,128)(2,1)S(1)} %collective-permute-done.vd_next_ref, ...), custom_call_target="tpu_custom_call" | custom-call | flops 2831155200 | bytes 2359296 | tf_op jit(solution)/shard_map/pallas_call | solution.py:429
  79.0 0.0 collective-permute-done.5.before_hbm
  79.0 0.0 copy-start.13
  79.0 0.0 collective-permute-done.6.after_hbm
  79.0 0.0 copy-start.14
  79.0 0.8 copy-done.13
  79.9 0.3 copy-done.14
  80.1 2.1 %shard_map.98 = (bf16[4,240,384]{2,1,0:T(8,128)(2,1)S(1)}, bf16[384,384]{1,0:T(8,128)(2,1)S(1)}) custom-call(s32[1]{0:T(128)S(6)} %copy.11.pattern_ref, bf16[4,240,384]{2,1,0:T(8,128)(2,1)S(1)} %get-tuple-element.22.local_ref, bf16[4,240,384]{2,1,0:T(8,128)(2,1)} %copy-done.13, bf16[4,240,384]{2,1,0:T(8,128)(2,1)} %copy-done.14, bf16[384,384]{1,0:T(8,128)(2,1)} %bitcast.20), custom_call_target="tpu_custom_call" | custom-call | flops 283115520 | bytes 2359296 | tf_op jit(solution)/shard_map/pallas_call | solution.py:447
  82.3 0.0 collective-permute-done.3.before_hbm
  82.3 0.0 copy-start.11
  82.3 0.0 collective-permute-done.4.after_hbm
  82.3 0.0 copy-start.12
  82.3 0.8 copy-done.11
  83.1 0.2 copy-done.12
  83.4 3.5 %shard_map.99 = bf16[5888,128]{1,0:T(8,128)(2,1)} custom-call(s32[1]{0:T(128)S(6)} %copy.11.pattern_ref, bf16[4,240,384]{2,1,0:T(8,128)(2,1)S(1)} %get-tuple-element.16.local_ref, bf16[4,240,384]{2,1,0:T(8,128)(2,1)} %copy-done.11, bf16[4,240,384]{2,1,0:T(8,128)(2,1)} %copy-done.12, bf16[384,384]{1,0:T(8,128)(2,1)S(1)} %get-tuple-element.25.masked_ref, ...), custom_call_target="tpu_custom_call" | custom-call | flops 283115520 | bytes 2359296 | tf_op jit(solution)/shard_map/pallas_call | solution.py:455
  86.9 0.0 copy-start.4
  86.9 0.0 all-to-all-done.got_ref
  86.9 0.0 copy-start.1
  86.9 1.1 copy-done.1
  88.0 8.8 %all-to-all-start.1 = ((bf16[32,23,8,128]{3,2,1,0:T(8,128)(2,1)}), bf16[32,23,8,128]{3,2,1,0:T(8,128)(2,1)}, u32[]{:S(2)}, u32[]{:S(2)}) async-start(bf16[32,23,8,128]{3,2,1,0:T(8,128)(2,1)} %bitcast.7), calls=%async_computation.1 | async-start | bytes 3014656 | tf_op jit(solution)/shard_map/all_to_all | solution.py:40
  96.8 0.0 copy-done.4
  96.8 0.0 copy-start.2
  96.9 1.4 copy-done.2
  98.2 0.0 copy-start.6
  98.2 0.6 shard_map.92.green_ref
  98.8 20.0 %all-to-all-done.1.got_ref = bf16[32,23,8,128]{3,2,1,0:T(8,128)(2,1)} async-done(((bf16[32,23,8,128]{3,2,1,0:T(8,128)(2,1)}), bf16[32,23,8,128]{3,2,1,0:T(8,128)(2,1)}, u32[]{:S(2)}, u32[]{:S(2)}) %all-to-all-start.1) | async-done | bytes 1507360 | tf_op jit(solution)/shard_map/all_to_all | solution.py:40
  118.8 0.0 copy-done.6
  118.8 2.6 %shard_map.100 = bf16[32,23,8,128]{3,2,1,0:T(8,128)(2,1)S(1)} custom-call(bf16[256,256]{1,0:T(8,128)(2,1)S(1)} %copy-done.4, bf16[256,256]{1,0:T(8,128)(2,1)S(1)} %copy-done.6, f32[12,256,256]{2,1,0:T(8,128)S(1)} %shard_map.92.green_ref, bf16[32,23,8,128]{3,2,1,0:T(8,128)(2,1)} %all-to-all-done.1.got_ref), custom_call_target="tpu_custom_call" | custom-call | flops 566231040 | bytes 2359296 | tf_op jit(solution)/shard_map/pallas_call | solution.py:464
  121.4 25.8 %all_to_all.15 = bf16[32,23,8,128]{3,2,1,0:T(8,128)(2,1)S(1)} all-to-all(bf16[32,23,8,128]{3,2,1,0:T(8,128)(2,1)S(1)} %shard_map.100), channel_id=1, replica_groups=mesh['energy'=32,'space'=8] {'energy'}, dimensions={0} | all-to-all | bytes 3014656 | tf_op jit(solution)/shard_map/all_to_all | solution.py:40
  147.2 2.6 %shard_map.101 = bf16[8,384,384]{2,1,0:T(8,128)(2,1)} custom-call(s32[48]{0:T(128)S(1)} %bitcast.26, bf16[5888,128]{1,0:T(8,128)(2,1)S(1)} %bitcast.16), custom_call_target="tpu_custom_call" | custom-call | flops 169869312 | bytes 2359296 | tf_op jit(solution)/shard_map/pallas_call | solution.py:469
Async XLA Ops:
  0.0 1.7 %copy-start.3 = (bf16[2,4,1,384,384]{4,3,2,1,0:T(8,128)(2,1)S(1)}, bf16[2,4,1,384,384]{4,3,2,1,0:T(8,128)(2,1)}, u32[]{:S(2)}) copy-start(bf16[2,4,1,384,384]{4,3,2,1,0:T(8,128)(2,1)} %param.9) | copy-start | bytes 7077892
  1.7 0.7 copy-start.7
  4.5 9.3 %copy-start.8 = (s32[1,48]{1,0:T(1,128)S(1)}, s32[1,48]{1,0:T(1,128)}, u32[]{:S(2)}) copy-start(s32[1,48]{1,0:T(1,128)} %param.15) | copy-start | bytes 580
  4.5 82.3 %all-to-all-start = ((bf16[32,23,8,128]{3,2,1,0:T(8,128)(2,1)}), bf16[32,23,8,128]{3,2,1,0:T(8,128)(2,1)S(1)}, u32[]{:S(2)}, u32[]{:S(2)}) async-start(bf16[32,23,8,128]{3,2,1,0:T(8,128)(2,1)} %bitcast.2), calls=%async_computation | async-start | bytes 3014656 | tf_op jit(solution)/shard_map/all_to_all | solution.py:40
  13.8 8.0 %copy-start = (bf16[2,4,1,384,384]{4,3,2,1,0:T(8,128)(2,1)S(1)}, bf16[2,4,1,384,384]{4,3,2,1,0:T(8,128)(2,1)}, u32[]{:S(2)}) copy-start(bf16[2,4,1,384,384]{4,3,2,1,0:T(8,128)(2,1)} %param.11) | copy-start | bytes 7077892
  13.8 8.0 %copy-start.5 = (bf16[1,384,384]{2,1,0:T(8,128)(2,1)S(1)}, bf16[1,384,384]{2,1,0:T(8,128)(2,1)}, u32[]{:S(2)}) copy-start(bf16[1,384,384]{2,1,0:T(8,128)(2,1)} %param.13) | copy-start | bytes 884740
  13.8 8.0 %copy-start.9 = (bf16[2,4,1,384,384]{4,3,2,1,0:T(8,128)(2,1)S(1)}, bf16[2,4,1,384,384]{4,3,2,1,0:T(8,128)(2,1)}, u32[]{:S(2)}) copy-start(bf16[2,4,1,384,384]{4,3,2,1,0:T(8,128)(2,1)} %param.10) | copy-start | bytes 7077892
  13.8 8.0 %copy-start.10 = (bf16[1,384,384]{2,1,0:T(8,128)(2,1)S(1)}, bf16[1,384,384]{2,1,0:T(8,128)(2,1)}, u32[]{:S(2)}) copy-start(bf16[1,384,384]{2,1,0:T(8,128)(2,1)} %param.12) | copy-start | bytes 884740
  16.0 10.4 %collective-permute-start.2 = (bf16[240,384]{1,0:T(8,128)(2,1)S(1)}, bf16[240,384]{1,0:T(8,128)(2,1)S(1)}, u32[]{:S(2)}, u32[]{:S(2)}) collective-permute-start(bf16[240,384]{1,0:T(8,128)(2,1)S(1)} %shard_map.95), channel_id=1, source_target_pairs={{0,1},{1,2},{2,3},{3,4},{4,5},{5,6},{6,7},{7,0},{8,9},{9,10},{10,1... | collective-permute-start | bytes 552968 | tf_op jit(solution)/shard_map/ppermute | solution.py:36
  17.8 6.7 %collective-permute-start.1 = (s32[48]{0:T(128)S(1)}, s32[48]{0:T(128)S(1)}, u32[]{:S(2)}, u32[]{:S(2)}) collective-permute-start(s32[48]{0:T(128)S(1)} %bitcast.24), channel_id=1, source_target_pairs={{0,7},{1,0},{2,1},{3,2},{4,3},{5,4},{6,5},{7,6},{8,15},{9,8},{10,9... | collective-permute-start | bytes 584 | tf_op jit(solution)/shard_map/ppermute | solution.py:36
  29.4 49.6 %collective-permute-start.5 = (bf16[4,240,384]{2,1,0:T(8,128)(2,1)S(1)}, bf16[4,240,384]{2,1,0:T(8,128)(2,1)S(1)}, u32[]{:S(2)}, u32[]{:S(2)}) collective-permute-start(bf16[4,240,384]{2,1,0:T(8,128)(2,1)S(1)} %get-tuple-element.23), channel_id=1, source_target_pairs={{0,1},{1,2},{2,3},{3,4},{4,5},{5,6},{6,7},{7,0},{8,9},{9,10},{10,1... | collective-permute-start | bytes 2211848 | tf_op jit(solution)/shard_map/ppermute | solution.py:36
  29.5 49.5 %collective-permute-start.6 = (bf16[4,240,384]{2,1,0:T(8,128)(2,1)S(1)}, bf16[4,240,384]{2,1,0:T(8,128)(2,1)S(1)}, u32[]{:S(2)}, u32[]{:S(2)}) collective-permute-start(bf16[4,240,384]{2,1,0:T(8,128)(2,1)S(1)} %get-tuple-element.24), channel_id=1, source_target_pairs={{0,7},{1,0},{2,1},{3,2},{4,3},{5,4},{6,5},{7,6},{8,15},{9,8},{10,9... | collective-permute-start | bytes 2211848 | tf_op jit(solution)/shard_map/ppermute | solution.py:36
  34.5 47.8 %collective-permute-start.3 = (bf16[4,240,384]{2,1,0:T(8,128)(2,1)S(1)}, bf16[4,240,384]{2,1,0:T(8,128)(2,1)S(1)}, u32[]{:S(2)}, u32[]{:S(2)}) collective-permute-start(bf16[4,240,384]{2,1,0:T(8,128)(2,1)S(1)} %get-tuple-element.20), channel_id=1, source_target_pairs={{0,1},{1,2},{2,3},{3,4},{4,5},{5,6},{6,7},{7,0},{8,9},{9,10},{10,1... | collective-permute-start | bytes 2211848 | tf_op jit(solution)/shard_map/ppermute | solution.py:36
  34.6 47.7 %collective-permute-start.4 = (bf16[4,240,384]{2,1,0:T(8,128)(2,1)S(1)}, bf16[4,240,384]{2,1,0:T(8,128)(2,1)S(1)}, u32[]{:S(2)}, u32[]{:S(2)}) collective-permute-start(bf16[4,240,384]{2,1,0:T(8,128)(2,1)S(1)} %get-tuple-element.21), channel_id=1, source_target_pairs={{0,7},{1,0},{2,1},{3,2},{4,3},{5,4},{6,5},{7,6},{8,15},{9,8},{10,9... | collective-permute-start | bytes 2211848 | tf_op jit(solution)/shard_map/ppermute | solution.py:36
  37.2 31.8 %collective-permute-start = (bf16[384,384]{1,0:T(8,128)(2,1)S(1)}, bf16[384,384]{1,0:T(8,128)(2,1)S(1)}, u32[]{:S(2)}, u32[]{:S(2)}) collective-permute-start(bf16[384,384]{1,0:T(8,128)(2,1)S(1)} %bitcast.31), channel_id=1, source_target_pairs={{0,7},{1,0},{2,1},{3,2},{4,3},{5,4},{6,5},{7,6},{8,15},{9,8},{10,9... | collective-permute-start | bytes 884744 | tf_op jit(solution)/shard_map/ppermute | solution.py:36
  79.0 0.9 copy-start.13
  79.0 1.1 copy-start.14
  82.3 0.9 copy-start.11
  82.3 1.1 copy-start.12
  86.9 10.0 %copy-start.4 = (bf16[256,256]{1,0:T(8,128)(2,1)S(1)}, bf16[256,256]{1,0:T(8,128)(2,1)}, u32[]{:S(2)}) copy-start(bf16[256,256]{1,0:T(8,128)(2,1)} %constant.4.clone.forward_ref) | copy-start | bytes 393220
  86.9 1.1 copy-start.1
  88.0 30.8 %all-to-all-start.1 = ((bf16[32,23,8,128]{3,2,1,0:T(8,128)(2,1)}), bf16[32,23,8,128]{3,2,1,0:T(8,128)(2,1)}, u32[]{:S(2)}, u32[]{:S(2)}) async-start(bf16[32,23,8,128]{3,2,1,0:T(8,128)(2,1)} %bitcast.7), calls=%async_computation.1 | async-start | bytes 3014656 | tf_op jit(solution)/shard_map/all_to_all | solution.py:40
  96.8 1.4 copy-start.2
  98.2 20.6 %copy-start.6 = (bf16[256,256]{1,0:T(8,128)(2,1)S(1)}, bf16[256,256]{1,0:T(8,128)(2,1)}, u32[]{:S(2)}) copy-start(bf16[256,256]{1,0:T(8,128)(2,1)} %constant.5.clone.inverse_ref) | copy-start | bytes 393220

commit v9 on v8

--- a/solution.py
+++ b/solution.py
@@ -127,27 +127,27 @@
     turned = (vu_ref[...].astype(F32) * scale).T
     turned_ref[...] = turned
     right = jnp.concatenate([vd_ref[...], turned.astype(BF16)], axis=0)
-    for plane in range(pu_ref.shape[0]):
+    for plane in range(out_ref.shape[0]):
         left = jnp.concatenate([pd_ref[plane], pu_ref[plane]], axis=1)
         out_ref[plane] = dot(left, right).astype(BF16)
 
 
-def prepare_kernel(present_ref, pattern_ref, vu_hbm, out_ref, idx_ref, held, sem):
+def prepare_kernel(present_ref, pattern_ref, vu_ref, out_ref, idx_ref, wide, picked):
     live_list(present_ref, idx_ref)
-    copies = []
-    for slot in range(LIVE):
-        row = pl.multiple_of(idx_ref[slot] * RG, RG)
-        target = held.at[pl.ds(slot * RG, RG), :]
-        copies += fetch([vu_hbm.at[pl.ds(row, RG), :]], [target], [sem.at[slot]])
-    arrive(copies)
-    out_ref[...] = (held[...].astype(F32) * pattern_ref[0].astype(F32)).astype(BF16)
+    wide[...] = vu_ref[...].astype(F32) * pattern_ref[0].astype(F32)
+    pick_rows(idx_ref, wide, picked)
+    out_ref[...] = picked[...].astype(BF16)
 
 
 def outward_kernel(half, *refs):
     if half == 0:
         next_ref, turned_ref, left_ref, pu_ref, inner_ref, to_next, to_prev, picked_ref, idx, picked, ready, sem = refs
     else:
-        picked_ref, left_ref, pu_ref, inner_ref, to_next, to_prev, ready, sem = refs
+        picked_ref, left_ref, pu_ref, pd_ref, vd_ref, turned_ref, to_next, to_prev, inner_ref, ready, sem = refs
+        right = jnp.concatenate([vd_ref[...], turned_ref[...].astype(BF16)], axis=0)
+        for plane in range(inner_ref.shape[0]):
+            at = plane + inner_ref.shape[0]
+            inner_ref[plane] = dot(jnp.concatenate([pd_ref[at], pu_ref[at]], axis=1), right).astype(BF16)
     planes = ready.shape[1]
     left_prev = left_ref[...]
     copies = []
@@ -161,7 +161,8 @@
         elif way == 1:
             left = picked_ref[...]
         for plane in range(planes):
-            ready[way, plane] = dot(left, right_ref[half * planes + plane]).astype(BF16)
+            at = plane + (half * planes if way == 1 else 0)
+            ready[way, plane] = dot(left, right_ref[at]).astype(BF16)
             if plane % 2 == 1:
                 some = slice(plane - 1, plane + 1)
                 copies += fetch([ready.at[way, some]], [out_hbm.at[some]], [sem.at[way, plane // 2]])
@@ -368,13 +369,8 @@
         return jax.ShapeDtypeStruct(shape, dtype)
 
     chosen = call(
-        prepare_kernel,
-        array(live, size),
-        [smem()] * 2 + [hbm()],
-        [idx, pltpu.VMEM((live, size), BF16), pltpu.SemaphoreType.DMA((LIVE,))],
-        8,
-        6,
-    )(present, v_pattern, v_u_here)
+        prepare_kernel, array(live, size), [smem()] * 2 + [vmem()], [idx, square, strip], 8, 6
+    )(present, v_pattern, v_u)
     v_u_prev = shifted(chosen, 1)
     present_next = shifted(present, -1)
     v_d_next = shifted(v_d, -1)
@@ -386,7 +382,7 @@
     block = pltpu.VMEM((size, size), BF16)
     inner, turned = call(
         inner_kernel,
-        [array(planes, size, size), array(size, size, dtype=F32)],
+        [array(planes // 2, size, size), array(size, size, dtype=F32)],
         [smem()] + [vmem()] * 4,
         [],
         3.2,
@@ -410,7 +406,13 @@
         [idx, strip],
     )
     after, before = [shifted(to_prev, -1)], [shifted(to_next, 1)]
-    to_next, to_prev = outward(1, [picked, v_u_prev, p_u_near, inner], leaving, [vmem()] * 4, [])
+    to_next, to_prev = outward(
+        1,
+        [picked, v_u_prev, p_u_near, p_d_near, v_d_near, turned],
+        leaving,
+        [vmem()] * 6,
+        [pltpu.VMEM((half, size, size), BF16)],
+    )
     after.append(shifted(to_prev, -1))
     before.append(shifted(to_next, 1))
 

time: 150 us -> 149 us (level)
  Pallas kernels: 33.5 us -> 32 us
    pallas_call x2, Pallas kernels: 4.8 us -> 2.12 us  [the longest x1 1.41 us: per_device(): call(inner_kernel, [array(planes // 2, size, size), array(size, size, dty...]
where the time goes in v9:
time: 149 us
  waiting for transfers between devices  53.9 us (36%)
  Pallas kernels  32 us (21%)
  starting transfers between devices  28.8 us (19%)
  blocking collectives  25.8 us (17%)
  local copies, waits for them, and re-layouts  7.03 us (5%)
    ppermute x7, waiting for transfers between devices, shifted(): return lax.ppermute(value, 'space', pairs)  33.8 us
    all_to_all x1, blocking collectives, routed(): lax.all_to_all(value, 'energy', split_axis=0, concat_axis=0, tiled=True)  25.8 us
    all_to_all x2, waiting for transfers between devices, routed(): lax.all_to_all(value, 'energy', split_axis=0, concat_axis=0, tiled=True)  20 us
    all_to_all x2, starting transfers between devices, routed(): lax.all_to_all(value, 'energy', split_axis=0, concat_axis=0, tiled=True)  17.6 us
    ppermute x7, starting transfers between devices, shifted(): return lax.ppermute(value, 'space', pairs)  11.3 us
    pallas_call x1, Pallas kernels, per_device(): call(local_kernel, [array(half, live, size)] * 2, [smem()] * 2 + [hbm()]...  9.93 us
    unnamed x30, local copies, waits for them, and re-layouts  7.03 us
    pallas_call x2, Pallas kernels, outward(): return call(kernel, outs, specs, scratch + moving, 1, 8, places)(*ins)  6.48 us
  transfers between devices with their start and end apart: 9, of which 3 were waited for; matrix products, arithmetic and copies ran while one was open for 0% of the time, Pallas kernels for 17%

profile of v9, /device:TPU:1, one launch (start us, length us, event | category | flops | bytes accessed | tf_op | source)
XLA Modules:
  0.0 148.6 jit_solution(17424492370896757800)
XLA Ops:
  0.0 0.0 copy-start.3
  0.0 1.7 %copy-done.3 = bf16[2,4,1,384,384]{4,3,2,1,0:T(8,128)(2,1)S(1)} copy-done((bf16[2,4,1,384,384]{4,3,2,1,0:T(8,128)(2,1)S(1)}, bf16[2,4,1,384,384]{4,3,2,1,0:T(8,128)(2,1)}, u32[]{:S(2)}) %copy-start.3) | copy-done | bytes 2359320
  1.7 0.0 copy-start.9
  1.7 0.7 copy-done.9
  2.3 2.2 %shard_map.91 = bf16[5888,128]{1,0:T(8,128)(2,1)} custom-call(s32[48]{0:T(128)S(1)} %bitcast.29, bf16[8,384,384]{2,1,0:T(8,128)(2,1)S(1)} %bitcast.17), custom_call_target="tpu_custom_call" | custom-call | flops 169869312 | bytes 2359296 | tf_op jit(solution)/shard_map/pallas_call | solution.py:419
  4.5 0.0 copy-start.7
  4.5 0.0 copy-start.10
  4.5 8.7 %all-to-all-start = ((bf16[32,23,8,128]{3,2,1,0:T(8,128)(2,1)}), bf16[32,23,8,128]{3,2,1,0:T(8,128)(2,1)S(1)}, u32[]{:S(2)}, u32[]{:S(2)}) async-start(bf16[32,23,8,128]{3,2,1,0:T(8,128)(2,1)} %bitcast.2), calls=%async_computation | async-start | bytes 3014656 | tf_op jit(solution)/shard_map/all_to_all | solution.py:40
  13.9 0.0 copy-done.7
  13.9 0.0 copy-done.10
  13.9 0.0 copy-start
  14.0 0.0 copy-start.4
  14.0 0.0 copy-start.6
  14.0 0.7 shard_map.95
  14.7 1.7 %collective-permute-start.2 = (bf16[240,384]{1,0:T(8,128)(2,1)S(1)}, bf16[240,384]{1,0:T(8,128)(2,1)S(1)}, u32[]{:S(2)}, u32[]{:S(2)}) collective-permute-start(bf16[240,384]{1,0:T(8,128)(2,1)S(1)} %shard_map.95), channel_id=1, source_target_pairs={{0,1},{1,2},{2,3},{3,4},{4,5},{5,6},{6,7},{7,0},{8,9},{9,10},{10,1... | collective-permute-start | bytes 552968 | tf_op jit(solution)/shard_map/ppermute | solution.py:36
  16.4 4.0 %collective-permute-start.1 = (s32[48]{0:T(128)S(1)}, s32[48]{0:T(128)S(1)}, u32[]{:S(2)}, u32[]{:S(2)}) collective-permute-start(s32[48]{0:T(128)S(1)} %bitcast.31), channel_id=1, source_target_pairs={{0,7},{1,0},{2,1},{3,2},{4,3},{5,4},{6,5},{7,6},{8,15},{9,8},{10,9... | collective-permute-start | bytes 584 | tf_op jit(solution)/shard_map/ppermute | solution.py:36
  20.4 0.0 copy-done
  20.4 0.0 copy-done.4
  20.5 0.0 copy-done.6
  20.5 1.4 shard_map.94
  21.9 0.0 collective-permute-done.1.refs_0_
  21.9 3.3 %collective-permute-done.2.refs_2_.refs_1_ = bf16[240,384]{1,0:T(8,128)(2,1)S(1)} collective-permute-done((bf16[240,384]{1,0:T(8,128)(2,1)S(1)}, bf16[240,384]{1,0:T(8,128)(2,1)S(1)}, u32[]{:S(2)}, u32[]{:S(2)}) %collective-permute-start.2) | collective-permute-done | bytes 184352 | tf_op jit(solution)/shard_map/ppermute | solution.py:36
  25.1 2.9 %shard_map.96 = (bf16[4,240,384]{2,1,0:T(8,128)(2,1)S(1)}, bf16[4,240,384]{2,1,0:T(8,128)(2,1)S(1)}, bf16[240,384]{1,0:T(8,128)(2,1)S(1)}) custom-call(s32[48]{0:T(128)S(1)} %collective-permute-done.1.refs_0_, f32[384,384]{1,0:T(8,128)S(1)} %get-tuple-element.17.refs_1_.refs_5_, bf16[240,384]{1,0:T(8,128)(2,1)S(1)} %collective-permute-done.2.refs_2_.refs_1_, ...), custom_call_target="tpu_custom_call" | custom-call | flops 566231040 | bytes 2359296 | tf_op jit(solution)/shard_map/pallas_call | solution.py:398
  28.1 0.1 collective-permute-start.5
  28.2 2.7 %collective-permute-start.6 = (bf16[4,240,384]{2,1,0:T(8,128)(2,1)S(1)}, bf16[4,240,384]{2,1,0:T(8,128)(2,1)S(1)}, u32[]{:S(2)}, u32[]{:S(2)}) collective-permute-start(bf16[4,240,384]{2,1,0:T(8,128)(2,1)S(1)} %get-tuple-element.24), channel_id=1, source_target_pairs={{0,7},{1,0},{2,1},{3,2},{4,3},{5,4},{6,5},{7,6},{8,15},{9,8},{10,9... | collective-permute-start | bytes 2211848 | tf_op jit(solution)/shard_map/ppermute | solution.py:36
  30.8 3.5 %shard_map.97 = (bf16[4,240,384]{2,1,0:T(8,128)(2,1)S(1)}, bf16[4,240,384]{2,1,0:T(8,128)(2,1)S(1)}) custom-call(bf16[240,384]{1,0:T(8,128)(2,1)S(1)} %get-tuple-element.19.refs_0_, bf16[240,384]{1,0:T(8,128)(2,1)S(1)} %collective-permute-done.2.refs_2_.refs_1_, bf16[8,384,384]{2,1,0:T(8,128)(2,1)S(1)} %bitcast.15, bf16[8,384,384]{2,1,0:T(8,128)(2,1)S(1)} %bitcast.20, ...), custom_call_target="tpu_custom_call" | custom-call | flops 566231040 | bytes 2359296 | tf_op jit(solution)/shard_map/pallas_call | solution.py:398
  34.4 0.1 collective-permute-start.3
  34.5 2.7 %collective-permute-start.4 = (bf16[4,240,384]{2,1,0:T(8,128)(2,1)S(1)}, bf16[4,240,384]{2,1,0:T(8,128)(2,1)S(1)}, u32[]{:S(2)}, u32[]{:S(2)}) collective-permute-start(bf16[4,240,384]{2,1,0:T(8,128)(2,1)S(1)} %get-tuple-element.21), channel_id=1, source_target_pairs={{0,7},{1,0},{2,1},{3,2},{4,3},{5,4},{6,5},{7,6},{8,15},{9,8},{10,9... | collective-permute-start | bytes 2211848 | tf_op jit(solution)/shard_map/ppermute | solution.py:36
  37.1 0.0 collective-permute-start
  37.2 30.6 %collective-permute-done.vd_next_ref = bf16[384,384]{1,0:T(8,128)(2,1)S(1)} collective-permute-done((bf16[384,384]{1,0:T(8,128)(2,1)S(1)}, bf16[384,384]{1,0:T(8,128)(2,1)S(1)}, u32[]{:S(2)}, u32[]{:S(2)}) %collective-permute-start) | collective-permute-done | bytes 294944 | tf_op jit(solution)/shard_map/ppermute | solution.py:36
  67.7 9.9 %shard_map.93 = (bf16[4,240,384]{2,1,0:T(8,128)(2,1)S(1)}, bf16[4,240,384]{2,1,0:T(8,128)(2,1)S(1)}) custom-call(s32[48]{0:T(128)S(1)} %bitcast.32, s32[1]{0:T(128)S(6)} %copy.11.pattern_ref, bf16[384,384]{1,0:T(8,128)(2,1)} %bitcast.25, bf16[384,384]{1,0:T(8,128)(2,1)} %bitcast.21, bf16[384,384]{1,0:T(8,128)(2,1)S(1)} %collective-permute-done.vd_next_ref, ...), custom_call_target="tpu_custom_call" | custom-call | flops 2831155200 | bytes 2359296 | tf_op jit(solution)/shard_map/pallas_call | solution.py:431
  77.7 0.0 collective-permute-done.5.before_hbm
  77.7 0.0 copy-start.13
  77.7 0.0 collective-permute-done.6.after_hbm
  77.7 0.0 copy-start.14
  77.7 0.8 copy-done.13
  78.5 0.3 copy-done.14
  78.8 2.1 %shard_map.98 = (bf16[4,240,384]{2,1,0:T(8,128)(2,1)S(1)}, bf16[384,384]{1,0:T(8,128)(2,1)S(1)}) custom-call(s32[1]{0:T(128)S(6)} %copy.11.pattern_ref, bf16[4,240,384]{2,1,0:T(8,128)(2,1)S(1)} %get-tuple-element.22.local_ref, bf16[4,240,384]{2,1,0:T(8,128)(2,1)} %copy-done.13, bf16[4,240,384]{2,1,0:T(8,128)(2,1)} %copy-done.14, bf16[384,384]{1,0:T(8,128)(2,1)} %bitcast.26), custom_call_target="tpu_custom_call" | custom-call | flops 283115520 | bytes 2359296 | tf_op jit(solution)/shard_map/pallas_call | solution.py:449
  80.9 0.0 collective-permute-done.3.before_hbm
  80.9 0.0 copy-start.11
  80.9 0.0 collective-permute-done.4.after_hbm
  81.0 0.0 copy-start.12
  81.0 0.8 copy-done.11
  81.8 0.2 copy-done.12
  82.0 3.5 %shard_map.99 = bf16[5888,128]{1,0:T(8,128)(2,1)} custom-call(s32[1]{0:T(128)S(6)} %copy.11.pattern_ref, bf16[4,240,384]{2,1,0:T(8,128)(2,1)S(1)} %get-tuple-element.16.local_ref, bf16[4,240,384]{2,1,0:T(8,128)(2,1)} %copy-done.11, bf16[4,240,384]{2,1,0:T(8,128)(2,1)} %copy-done.12, bf16[384,384]{1,0:T(8,128)(2,1)S(1)} %get-tuple-element.25.masked_ref, ...), custom_call_target="tpu_custom_call" | custom-call | flops 283115520 | bytes 2359296 | tf_op jit(solution)/shard_map/pallas_call | solution.py:457
  85.5 0.0 all-to-all-done.got_ref
  85.5 0.0 copy-start.1
  85.5 0.0 copy-start.5
  85.6 1.1 copy-done.1
  86.7 8.8 %all-to-all-start.1 = ((bf16[32,23,8,128]{3,2,1,0:T(8,128)(2,1)}), bf16[32,23,8,128]{3,2,1,0:T(8,128)(2,1)}, u32[]{:S(2)}, u32[]{:S(2)}) async-start(bf16[32,23,8,128]{3,2,1,0:T(8,128)(2,1)} %bitcast.7), calls=%async_computation.1 | async-start | bytes 3014656 | tf_op jit(solution)/shard_map/all_to_all | solution.py:40
  95.5 0.0 copy-done.5
  95.5 0.0 copy-start.2
  95.5 1.4 copy-done.2
  96.9 0.0 copy-start.8
  96.9 0.6 shard_map.92.green_ref
  97.5 20.0 %all-to-all-done.1.got_ref = bf16[32,23,8,128]{3,2,1,0:T(8,128)(2,1)} async-done(((bf16[32,23,8,128]{3,2,1,0:T(8,128)(2,1)}), bf16[32,23,8,128]{3,2,1,0:T(8,128)(2,1)}, u32[]{:S(2)}, u32[]{:S(2)}) %all-to-all-start.1) | async-done | bytes 1507360 | tf_op jit(solution)/shard_map/all_to_all | solution.py:40
  117.5 0.0 copy-done.8
  117.5 2.6 %shard_map.100 = bf16[32,23,8,128]{3,2,1,0:T(8,128)(2,1)S(1)} custom-call(bf16[256,256]{1,0:T(8,128)(2,1)S(1)} %copy-done.5, bf16[256,256]{1,0:T(8,128)(2,1)S(1)} %copy-done.8, f32[12,256,256]{2,1,0:T(8,128)S(1)} %shard_map.92.green_ref, bf16[32,23,8,128]{3,2,1,0:T(8,128)(2,1)} %all-to-all-done.1.got_ref), custom_call_target="tpu_custom_call" | custom-call | flops 566231040 | bytes 2359296 | tf_op jit(solution)/shard_map/pallas_call | solution.py:466
  120.1 25.8 %all_to_all.15 = bf16[32,23,8,128]{3,2,1,0:T(8,128)(2,1)S(1)} all-to-all(bf16[32,23,8,128]{3,2,1,0:T(8,128)(2,1)S(1)} %shard_map.100), channel_id=1, replica_groups=mesh['energy'=32,'space'=8] {'energy'}, dimensions={0} | all-to-all | bytes 3014656 | tf_op jit(solution)/shard_map/all_to_all | solution.py:40
  145.8 2.6 %shard_map.101 = bf16[8,384,384]{2,1,0:T(8,128)(2,1)} custom-call(s32[48]{0:T(128)S(1)} %bitcast.33, bf16[5888,128]{1,0:T(8,128)(2,1)S(1)} %bitcast.16), custom_call_target="tpu_custom_call" | custom-call | flops 169869312 | bytes 2359296 | tf_op jit(solution)/shard_map/pallas_call | solution.py:471
Async XLA Ops:
  0.0 1.7 %copy-start.3 = (bf16[2,4,1,384,384]{4,3,2,1,0:T(8,128)(2,1)S(1)}, bf16[2,4,1,384,384]{4,3,2,1,0:T(8,128)(2,1)}, u32[]{:S(2)}) copy-start(bf16[2,4,1,384,384]{4,3,2,1,0:T(8,128)(2,1)} %param.9) | copy-start | bytes 7077892
  1.7 0.7 copy-start.9
  4.5 9.4 %copy-start.7 = (bf16[1,384,384]{2,1,0:T(8,128)(2,1)S(1)}, bf16[1,384,384]{2,1,0:T(8,128)(2,1)}, u32[]{:S(2)}) copy-start(bf16[1,384,384]{2,1,0:T(8,128)(2,1)} %param.13) | copy-start | bytes 884740
  4.5 9.4 %copy-start.10 = (s32[1,48]{1,0:T(1,128)S(1)}, s32[1,48]{1,0:T(1,128)}, u32[]{:S(2)}) copy-start(s32[1,48]{1,0:T(1,128)} %param.15) | copy-start | bytes 580
  4.5 81.0 %all-to-all-start = ((bf16[32,23,8,128]{3,2,1,0:T(8,128)(2,1)}), bf16[32,23,8,128]{3,2,1,0:T(8,128)(2,1)S(1)}, u32[]{:S(2)}, u32[]{:S(2)}) async-start(bf16[32,23,8,128]{3,2,1,0:T(8,128)(2,1)} %bitcast.2), calls=%async_computation | async-start | bytes 3014656 | tf_op jit(solution)/shard_map/all_to_all | solution.py:40
  13.9 6.5 %copy-start = (bf16[2,4,1,384,384]{4,3,2,1,0:T(8,128)(2,1)S(1)}, bf16[2,4,1,384,384]{4,3,2,1,0:T(8,128)(2,1)}, u32[]{:S(2)}) copy-start(bf16[2,4,1,384,384]{4,3,2,1,0:T(8,128)(2,1)} %param.11) | copy-start | bytes 7077892
  14.0 6.5 %copy-start.4 = (bf16[2,4,1,384,384]{4,3,2,1,0:T(8,128)(2,1)S(1)}, bf16[2,4,1,384,384]{4,3,2,1,0:T(8,128)(2,1)}, u32[]{:S(2)}) copy-start(bf16[2,4,1,384,384]{4,3,2,1,0:T(8,128)(2,1)} %param.10) | copy-start | bytes 7077892
  14.0 6.5 %copy-start.6 = (bf16[1,384,384]{2,1,0:T(8,128)(2,1)S(1)}, bf16[1,384,384]{2,1,0:T(8,128)(2,1)}, u32[]{:S(2)}) copy-start(bf16[1,384,384]{2,1,0:T(8,128)(2,1)} %param.12) | copy-start | bytes 884740
  14.7 10.4 %collective-permute-start.2 = (bf16[240,384]{1,0:T(8,128)(2,1)S(1)}, bf16[240,384]{1,0:T(8,128)(2,1)S(1)}, u32[]{:S(2)}, u32[]{:S(2)}) collective-permute-start(bf16[240,384]{1,0:T(8,128)(2,1)S(1)} %shard_map.95), channel_id=1, source_target_pairs={{0,1},{1,2},{2,3},{3,4},{4,5},{5,6},{6,7},{7,0},{8,9},{9,10},{10,1... | collective-permute-start | bytes 552968 | tf_op jit(solution)/shard_map/ppermute | solution.py:36
  16.4 5.5 %collective-permute-start.1 = (s32[48]{0:T(128)S(1)}, s32[48]{0:T(128)S(1)}, u32[]{:S(2)}, u32[]{:S(2)}) collective-permute-start(s32[48]{0:T(128)S(1)} %bitcast.31), channel_id=1, source_target_pairs={{0,7},{1,0},{2,1},{3,2},{4,3},{5,4},{6,5},{7,6},{8,15},{9,8},{10,9... | collective-permute-start | bytes 584 | tf_op jit(solution)/shard_map/ppermute | solution.py:36
  28.1 49.6 %collective-permute-start.5 = (bf16[4,240,384]{2,1,0:T(8,128)(2,1)S(1)}, bf16[4,240,384]{2,1,0:T(8,128)(2,1)S(1)}, u32[]{:S(2)}, u32[]{:S(2)}) collective-permute-start(bf16[4,240,384]{2,1,0:T(8,128)(2,1)S(1)} %get-tuple-element.23), channel_id=1, source_target_pairs={{0,1},{1,2},{2,3},{3,4},{4,5},{5,6},{6,7},{7,0},{8,9},{9,10},{10,1... | collective-permute-start | bytes 2211848 | tf_op jit(solution)/shard_map/ppermute | solution.py:36
  28.2 49.5 %collective-permute-start.6 = (bf16[4,240,384]{2,1,0:T(8,128)(2,1)S(1)}, bf16[4,240,384]{2,1,0:T(8,128)(2,1)S(1)}, u32[]{:S(2)}, u32[]{:S(2)}) collective-permute-start(bf16[4,240,384]{2,1,0:T(8,128)(2,1)S(1)} %get-tuple-element.24), channel_id=1, source_target_pairs={{0,7},{1,0},{2,1},{3,2},{4,3},{5,4},{6,5},{7,6},{8,15},{9,8},{10,9... | collective-permute-start | bytes 2211848 | tf_op jit(solution)/shard_map/ppermute | solution.py:36
  34.4 46.5 %collective-permute-start.3 = (bf16[4,240,384]{2,1,0:T(8,128)(2,1)S(1)}, bf16[4,240,384]{2,1,0:T(8,128)(2,1)S(1)}, u32[]{:S(2)}, u32[]{:S(2)}) collective-permute-start(bf16[4,240,384]{2,1,0:T(8,128)(2,1)S(1)} %get-tuple-element.20), channel_id=1, source_target_pairs={{0,1},{1,2},{2,3},{3,4},{4,5},{5,6},{6,7},{7,0},{8,9},{9,10},{10,1... | collective-permute-start | bytes 2211848 | tf_op jit(solution)/shard_map/ppermute | solution.py:36
  34.5 46.5 %collective-permute-start.4 = (bf16[4,240,384]{2,1,0:T(8,128)(2,1)S(1)}, bf16[4,240,384]{2,1,0:T(8,128)(2,1)S(1)}, u32[]{:S(2)}, u32[]{:S(2)}) collective-permute-start(bf16[4,240,384]{2,1,0:T(8,128)(2,1)S(1)} %get-tuple-element.21), channel_id=1, source_target_pairs={{0,7},{1,0},{2,1},{3,2},{4,3},{5,4},{6,5},{7,6},{8,15},{9,8},{10,9... | collective-permute-start | bytes 2211848 | tf_op jit(solution)/shard_map/ppermute | solution.py:36
  37.1 30.6 %collective-permute-start = (bf16[384,384]{1,0:T(8,128)(2,1)S(1)}, bf16[384,384]{1,0:T(8,128)(2,1)S(1)}, u32[]{:S(2)}, u32[]{:S(2)}) collective-permute-start(bf16[384,384]{1,0:T(8,128)(2,1)S(1)} %bitcast.24), channel_id=1, source_target_pairs={{0,7},{1,0},{2,1},{3,2},{4,3},{5,4},{6,5},{7,6},{8,15},{9,8},{10,9... | collective-permute-start | bytes 884744 | tf_op jit(solution)/shard_map/ppermute | solution.py:36
  77.7 0.9 copy-start.13
  77.7 1.1 copy-start.14
  80.9 0.9 copy-start.11
  81.0 1.1 copy-start.12
  85.5 1.1 copy-start.1
  85.5 10.0 %copy-start.5 = (bf16[256,256]{1,0:T(8,128)(2,1)S(1)}, bf16[256,256]{1,0:T(8,128)(2,1)}, u32[]{:S(2)}) copy-start(bf16[256,256]{1,0:T(8,128)(2,1)} %constant.4.clone.forward_ref) | copy-start | bytes 393220
  86.7 30.8 %all-to-all-start.1 = ((bf16[32,23,8,128]{3,2,1,0:T(8,128)(2,1)}), bf16[32,23,8,128]{3,2,1,0:T(8,128)(2,1)}, u32[]{:S(2)}, u32[]{:S(2)}) async-start(bf16[32,23,8,128]{3,2,1,0:T(8,128)(2,1)} %bitcast.7), calls=%async_computation.1 | async-start | bytes 3014656 | tf_op jit(solution)/shard_map/all_to_all | solution.py:40
  95.5 1.4 copy-start.2
  96.9 20.6 %copy-start.8 = (bf16[256,256]{1,0:T(8,128)(2,1)S(1)}, bf16[256,256]{1,0:T(8,128)(2,1)}, u32[]{:S(2)}) copy-start(bf16[256,256]{1,0:T(8,128)(2,1)} %constant.5.clone.inverse_ref) | copy-start | bytes 393220
